TPU v7x, 32 devices: a whole 2x2x4 slice. The times are simulated.
32 devices in a mesh: dp: 16 (over z, y, core), mp: 2 (over x).
Axes of the slice: x: 2, y: 2, z: 4, core: 2. Of those that a mesh axis runs over, the one named last changes fastest.
Arguments:
- tokens: bfloat16 [32, 1024, 768], P('dp'), may hold values from -6 to 6
- valid: int32 [32, 1024], P('dp'), may hold values from 0 to 1, as said below
- steps: int32 [32], replicated, may hold values from 0 to 999
- labels: int32 [32], replicated, may hold values from 0 to 999
- w_mod: bfloat16 [768, 4608], replicated, may hold values from -0.21875 to 0.21875
- step_table: bfloat16 [1000, 768], replicated, may hold values from -4 to 4
- class_table: bfloat16 [1000, 768], replicated, may hold values from -4 to 4
- conv_attn: bfloat16 [9, 768], replicated, may hold values from -2 to 2
- w_qkv: bfloat16 [768, 3, 768], P(None, None, 'mp'), may hold values from -0.21875 to 0.21875
- w_out: bfloat16 [768, 768], P(None, 'mp'), may hold values from -0.875 to 0.875
- conv_ffn: bfloat16 [9, 3072], P(None, 'mp'), may hold values from -2 to 2
- w_up: bfloat16 [768, 3072], P(None, 'mp'), may hold values from -0.21875 to 0.21875
- w_down: bfloat16 [768, 3072], P(None, 'mp'), may hold values from -0.109375 to 0.109375
- cotangent: bfloat16 [32, 1024, 768], P('dp'), may hold values from -6 to 6
Outputs:
- output: bfloat16 [32, 1024, 768], P('dp')
- grad_tokens: bfloat16 [32, 1024, 768], P('dp')
- grad_w_mod: float32 [768, 4608], P('dp')
- grad_step_table: float32 [1000, 768], replicated
- grad_class_table: float32 [1000, 768], replicated
- grad_conv_attn: float32 [9, 768], replicated
- grad_w_qkv: float32 [768, 3, 768], P('dp', None, 'mp')
- grad_w_out: float32 [768, 768], P('dp', 'mp')
- grad_conv_ffn: float32 [9, 3072], P(None, 'mp')
- grad_w_up: float32 [768, 3072], P('dp', 'mp')
- grad_w_down: float32 [768, 3072], P('dp', 'mp')
Inputs may be any that keep to these rules, and one draw needn't show every extreme that they name: tokens 0, 1, 32 and 33 of every latent are valid, so each group has a valid key.
All inputs are finite; a program needn't handle non-finite values.
Results may differ from a plain program's by a relative error of at most 0.017.
The roundings to bfloat16 on the way count: a program that leaves them out, or rounds other values in their place, can miss the bound.
Values may be sent and summed in bfloat16 or wider, within the bound.
No kernel may reach another device: no remote copies, remote signals or barrier semaphores. Data moves between devices by JAX's collectives and lax.ppermute only.
A program may use at most 384 MiB of HBM per device.

v0:
```python
from functools import partial

import jax
import jax.numpy as jnp
from jax import lax
from jax.sharding import PartitionSpec as P

SIDE = 32
HEAD_DIM = 64


eps_norm = 1e-06


def layer_norm(values_in):
    centre = values_in - jnp.mean(values_in, axis=-1, keepdims=True)
    return centre * lax.rsqrt(jnp.mean(centre * centre, axis=-1, keepdims=True) + eps_norm)


def depthwise(values_in, kernel):
    batches = values_in.shape[0]
    channels = values_in.shape[-1]
    blocked = values_in.reshape(batches, SIDE, SIDE, channels)
    padded = jnp.pad(blocked, ((0, 0), (1, 1), (1, 1), (0, 0)))
    summed = jnp.zeros_like(blocked)
    for row_off in range(3):
        for col_off in range(3):
            window = padded[:, row_off : row_off + SIDE, col_off : col_off + SIDE, :]
            summed = summed + kernel[row_off * 3 + col_off] * window
    return summed.reshape(values_in.shape)


def unshuffle(tokens_in):
    halfside = SIDE // 2
    batches = tokens_in.shape[0]
    channels = tokens_in.shape[-1]
    blocked = tokens_in.reshape(batches, halfside, 2, halfside, 2, channels)
    return blocked.transpose(0, 2, 4, 1, 3, 5).reshape(batches, 4, halfside * halfside, channels)


def reshuffle(groups_in):
    halfside = SIDE // 2
    batches = groups_in.shape[0]
    channels = groups_in.shape[-1]
    blocked = groups_in.reshape(batches, 2, 2, halfside, halfside, channels)
    return blocked.transpose(0, 3, 1, 4, 2, 5).reshape(batches, SIDE * SIDE, channels)


def silu_of(values_in):
    return values_in * jax.nn.sigmoid(values_in)


def table_grad(indices, gradients, row_count):
    onehot_rows = (jnp.arange(row_count, dtype=jnp.int32)[:, None] == indices[None, :]).astype(
        jnp.float32
    )
    return jnp.dot(onehot_rows, gradients, precision=lax.Precision.HIGHEST)


def soft_weights(queries, keyset, keep_mask, score_scale):
    raw_scores = jnp.einsum("gqhe,gkhe->ghqk", queries, keyset, preferred_element_type=jnp.float32)
    scores = jnp.where(keep_mask[:, None, None, :] > 0, raw_scores * score_scale, -1e30)
    shifted = scores - jnp.max(scores, axis=-1, keepdims=True)
    exponent = jnp.exp(shifted)
    return exponent / jnp.sum(exponent, axis=-1, keepdims=True)


def attend_block(score_scale, inputs):
    head_view, keep_mask = inputs
    weights_soft = soft_weights(head_view[:, :, 0], head_view[:, :, 1], keep_mask, score_scale)
    mixed = jnp.einsum(
        "ghqk,gkhe->gqhe",
        weights_soft.astype(jnp.bfloat16),
        head_view[:, :, 2],
        preferred_element_type=jnp.float32,
    )
    return mixed.astype(jnp.bfloat16)


def attend_back(score_scale, inputs):
    head_view, keep_mask, grad_mixed = inputs
    queries = head_view[:, :, 0]
    keyset = head_view[:, :, 1]
    values = head_view[:, :, 2]
    weights_soft = soft_weights(queries, keyset, keep_mask, score_scale)
    grad_soft = jnp.einsum(
        "gqhe,gkhe->ghqk", grad_mixed, values, preferred_element_type=jnp.float32
    )
    grad_values = jnp.einsum(
        "ghqk,gqhe->gkhe",
        weights_soft.astype(jnp.bfloat16),
        grad_mixed,
        preferred_element_type=jnp.float32,
    )
    grad_scores = weights_soft * (
        grad_soft - jnp.sum(weights_soft * grad_soft, axis=-1, keepdims=True)
    )
    grad_raw = (grad_scores * score_scale).astype(jnp.bfloat16)
    grad_queries = jnp.einsum(
        "ghqk,gkhe->gqhe", grad_raw, keyset, preferred_element_type=jnp.float32
    )
    grad_keys = jnp.einsum("ghqk,gqhe->gkhe", grad_raw, queries, preferred_element_type=jnp.float32)
    return jnp.stack([grad_queries, grad_keys, grad_values], axis=2).astype(jnp.bfloat16)


def attn_input(tok_in, scale_in, shift_in, kernel_in):
    return depthwise(layer_norm(tok_in) * (1.0 + scale_in) + shift_in, kernel_in)


def ffn_input(res_in, scale_in, shift_in):
    return layer_norm(res_in) * (1.0 + scale_in) + shift_in


def ffn_middle(upper_in, kernel_in):
    return jax.nn.gelu(depthwise(upper_in, kernel_in))


def local(
    tokens,
    valid,
    steps,
    labels,
    w_mod,
    step_table,
    class_table,
    conv_attn,
    w_qkv,
    w_out,
    conv_ffn,
    w_up,
    w_down,
    cotangent,
):
    lat_dev = tokens.shape[0]
    first_row = lax.axis_index("dp") * lat_dev
    my_steps = lax.dynamic_slice_in_dim(steps, first_row, lat_dev)
    my_labels = lax.dynamic_slice_in_dim(labels, first_row, lat_dev)
    embedding = jnp.take(step_table, my_steps, axis=0).astype(jnp.float32) + jnp.take(
        class_table, my_labels, axis=0
    ).astype(jnp.float32)
    silu_value, silu_pull = jax.vjp(silu_of, embedding)
    silu_low = silu_value.astype(jnp.bfloat16)
    modulation = jnp.dot(silu_low, w_mod, preferred_element_type=jnp.float32).reshape(
        lat_dev, 6, 1, -1
    )
    shift_a = modulation[:, 0]
    scale_a = modulation[:, 1]
    gate_a = modulation[:, 2]
    shift_f = modulation[:, 3]
    scale_f = modulation[:, 4]
    gate_f = modulation[:, 5]
    tok_float = tokens.astype(jnp.float32)
    kernel_a = conv_attn.astype(jnp.float32)
    kernel_f = conv_ffn.astype(jnp.float32)
    conved, attn_pull = jax.vjp(attn_input, tok_float, scale_a, shift_a, kernel_a)
    grouped = unshuffle(conved.astype(jnp.bfloat16))
    qkv_low = jnp.einsum(
        "lgtd,dch->lgtch", grouped, w_qkv, preferred_element_type=jnp.float32
    ).astype(jnp.bfloat16)
    heads_local = w_qkv.shape[2] // HEAD_DIM
    group_len = grouped.shape[2]
    head_view = qkv_low.reshape(lat_dev, 4, group_len, 3, heads_local, HEAD_DIM)
    keep_mask = unshuffle(valid[:, :, None])[..., 0]
    score_scale = HEAD_DIM ** (-0.5)
    mixed_groups = lax.map(partial(attend_block, score_scale), (head_view, keep_mask))
    mixed_low = reshuffle(mixed_groups.reshape(lat_dev, 4, group_len, -1))
    attn_part = jnp.einsum("lpe,de->lpd", mixed_low, w_out, preferred_element_type=jnp.float32)
    attn_full = lax.psum(attn_part.astype(jnp.bfloat16), "mp").astype(jnp.float32)
    residual = tok_float + gate_a * attn_full
    normed_value = ffn_input(residual, scale_f, shift_f)
    normed_low = normed_value.astype(jnp.bfloat16)
    upper_proj = jnp.einsum("lpd,df->lpf", normed_low, w_up, preferred_element_type=jnp.float32)
    active_value, ffn_pull = jax.vjp(ffn_middle, upper_proj, kernel_f)
    active_low = active_value.astype(jnp.bfloat16)
    down_part = jnp.einsum("lpf,df->lpd", active_low, w_down, preferred_element_type=jnp.float32)
    grad_out = cotangent.astype(jnp.float32)
    down_full = lax.psum(down_part.astype(jnp.bfloat16), "mp").astype(jnp.float32)
    output_low = (residual + gate_f * down_full).astype(jnp.bfloat16)
    gate_f_part = jnp.sum(grad_out * down_full, axis=1, keepdims=True)
    grad_down_low = (gate_f * grad_out).astype(jnp.bfloat16)
    grad_w_down = jnp.einsum(
        "lpd,lpf->df", grad_down_low, active_low, preferred_element_type=jnp.float32
    )
    grad_active = jnp.einsum(
        "lpd,df->lpf", grad_down_low, w_down, preferred_element_type=jnp.float32
    )
    grad_upper, grad_kernel_f = ffn_pull(grad_active)
    grad_upper_low = grad_upper.astype(jnp.bfloat16)
    grad_w_up = jnp.einsum(
        "lpd,lpf->df", normed_low, grad_upper_low, preferred_element_type=jnp.float32
    )
    grad_normed_part = jnp.einsum(
        "lpf,df->lpd", grad_upper_low, w_up, preferred_element_type=jnp.float32
    )
    grad_normed = lax.psum(grad_normed_part.astype(jnp.bfloat16), "mp").astype(jnp.float32)
    _, full_pull = jax.vjp(ffn_input, residual, scale_f, shift_f)
    grad_res_norm, grad_scale_f, grad_shift_f = full_pull(grad_normed)
    grad_residual = grad_out + grad_res_norm
    grad_gate_a = jnp.sum(grad_residual * attn_full, axis=1, keepdims=True)
    grad_attn_low = (gate_a * grad_residual).astype(jnp.bfloat16)
    grad_w_out = jnp.einsum(
        "lpd,lpe->de", grad_attn_low, mixed_low, preferred_element_type=jnp.float32
    )
    grad_mixed_low = jnp.einsum(
        "lpd,de->lpe", grad_attn_low, w_out, preferred_element_type=jnp.float32
    ).astype(jnp.bfloat16)
    grad_groups = unshuffle(grad_mixed_low).reshape(lat_dev, 4, group_len, heads_local, HEAD_DIM)
    grad_qkv_low = lax.map(partial(attend_back, score_scale), (head_view, keep_mask, grad_groups))
    grad_qkv_low = grad_qkv_low.reshape(lat_dev, 4, group_len, 3, -1)
    grad_w_qkv = jnp.einsum(
        "lgtd,lgtch->dch", grouped, grad_qkv_low, preferred_element_type=jnp.float32
    )
    grad_grouped_part = jnp.einsum(
        "lgtch,dch->lgtd", grad_qkv_low, w_qkv, preferred_element_type=jnp.float32
    )
    grad_conved = lax.psum(reshuffle(grad_grouped_part).astype(jnp.bfloat16), "mp").astype(
        jnp.float32
    )
    grad_tok_norm, grad_scale_a, grad_shift_a, grad_kernel_a = attn_pull(grad_conved)
    grad_tokens = (grad_residual + grad_tok_norm).astype(jnp.bfloat16)
    grad_modulation = jnp.concatenate(
        [grad_shift_a, grad_scale_a, grad_gate_a, grad_shift_f, grad_scale_f, gate_f_part], axis=1
    )
    grad_mod_low = grad_modulation.reshape(lat_dev, -1).astype(jnp.bfloat16)
    grad_w_qkv, grad_w_out, grad_w_up, grad_w_down = (
        lax.psum_scatter(grad_w_qkv, "dp", scatter_dimension=0, tiled=True),
        lax.psum_scatter(grad_w_out, "dp", scatter_dimension=0, tiled=True),
        lax.psum_scatter(grad_w_up, "dp", scatter_dimension=0, tiled=True),
        lax.psum_scatter(grad_w_down, "dp", scatter_dimension=0, tiled=True),
    )
    grad_silu = jnp.einsum("lc,kc->lk", grad_mod_low, w_mod, preferred_element_type=jnp.float32)
    (grad_embedding,) = silu_pull(grad_silu)
    part_mod = jnp.einsum("lk,lc->kc", silu_low, grad_mod_low, preferred_element_type=jnp.float32)
    grad_w_mod = lax.psum_scatter(part_mod, "dp", scatter_dimension=0, tiled=True)
    part_steps = table_grad(my_steps, grad_embedding, step_table.shape[0])
    part_labels = table_grad(my_labels, grad_embedding, class_table.shape[0])
    grad_step_table, grad_class_table, grad_conv_attn, grad_conv_ffn = lax.psum(
        (part_steps, part_labels, grad_kernel_a, grad_kernel_f), "dp"
    )
    return (
        output_low,
        grad_tokens,
        grad_w_mod,
        grad_step_table,
        grad_class_table,
        grad_conv_attn,
        grad_w_qkv,
        grad_w_out,
        grad_conv_ffn,
        grad_w_up,
        grad_w_down,
    )


def solution(mesh):
    in_specs = (
        P("dp", None, None),
        P("dp", None),
        P(),
        P(),
        P(),
        P(),
        P(),
        P(),
        P(None, None, "mp"),
        P(None, "mp"),
        P(None, "mp"),
        P(None, "mp"),
        P(None, "mp"),
        P("dp", None, None),
    )
    out_specs = (
        P("dp", None, None),
        P("dp", None, None),
        P("dp", None),
        P(),
        P(),
        P(),
        P("dp", None, "mp"),
        P("dp", "mp"),
        P(None, "mp"),
        P("dp", "mp"),
        P("dp", "mp"),
    )
    return jax.shard_map(local, mesh=mesh, in_specs=in_specs, out_specs=out_specs, check_vma=False)
```

profile of v0, /device:TPU:0, one launch (start us, length us, event | category | flops | bytes accessed | tf_op | source)
XLA Modules:
  0.0 1469.2 jit_solution(7925308656870331402)
XLA Ops:
  13.7 4.1 fusion.129
  27.1 22.2 %add_convert_fusion.2 = bf16[2,32,32,768]{3,2,1,0:T(8,128)(2,1)S(1)} fusion(f32[2,32,32,768]{3,2,1,0:T(8,128)} %bitcast.267, f32[768]{0:T(1024)S(1)} %get-tuple-element.130, f32[768]{0:T(1024)S(1)} %get-tuple-element.131, f32[768]{0:T(1024)S(1)} %get-tuple-element.132, f32[768]{0:T(1024)S(1)} %get-tuple-element.133, f32[768]{0:T(1024)S(1)} %get-tuple-element.134, ...), kind=kLoop, calls=%fused_computation.177 | loop fusion | flops 28311552 | bytes 9464832 | tf_op jit(solution)/shard_map/convert_element_type | solution.py:156
  54.8 5.8 convolution_convert_fusion
  60.7 6.7 copy.141
  68.4 13.8 while.20
  82.8 5.0 copy.112
  87.8 6.3 reshape_reshape.6
  98.3 3.5 convolution_convert_fusion.1
  102.1 88.3 %all-reduce.47.cloned.1.call-done = bf16[2,1024,768]{2,1,0:T(8,128)(2,1)} async-done(((bf16[2,1024,768]{2,1,0:T(8,128)(2,1)}), bf16[2,1024,768]{2,1,0:T(8,128)(2,1)}) %all-reduce.47.cloned.1.call-update) | async-done | bytes 3145744 | tf_op jit(solution)/shard_map/psum | solution.py:168
  190.4 4.1 fusion.95
  197.5 8.5 fusion.106
  206.0 41.3 %multiply_add_fusion = f32[2,32,32,1536]{3,2,1,0:T(8,128)} fusion(f32[2,32,32,1536]{3,2,1,0:T(8,128)} %bitcast.264, f32[1536]{0:T(1024)S(1)} %get-tuple-element.121, f32[1536]{0:T(1024)S(1)} %get-tuple-element.122, f32[1536]{0:T(1024)S(1)} %get-tuple-element.123, f32[1536]{0:T(1024)S(1)} %get-tuple-element.124, f32[1536]{0:T(1024)S(1)} %get-tuple-element.125, ...), kind=kLoop, calls=%fused_computation.105 | loop fusion | flops 53477376 | bytes 25221120 | tf_op jit(solution)/shard_map/jvp()/add | solution.py:29
  247.3 12.8 fusion.68
  260.1 50.8 %broadcast_multiply_fusion = (f32[2,32,32,1536]{3,2,1,0:T(8,128)}, f32[2,32,32,1536]{3,2,1,0:T(8,128)}, f32[2,32,32,1536]{3,2,1,0:T(8,128)}, f32[2,32,32,1536]{3...) fusion(f32[1536]{0:T(1024)S(1)} %get-tuple-element.121, ...), kind=kOutput, calls=%fused_computation.166 | convolution fusion | flops 4912054272 | bytes 156561408 | tf_op jit(solution)/shard_map/lpd,df->lpf/dot_general | solution.py:184
  310.9 23.6 %pad_add_fusion = f32[2,34,34,1536]{3,2,1,0:T(8,128)} fusion(f32[2,32,32,1536]{3,2,1,0:T(8,128)} %get-tuple-element.177, f32[2,32,32,1536]{3,2,1,0:T(8,128)} %get-tuple-element.176, f32[2,32,32,1536]{3,2,1,0:T(8,128)} %get-tuple-element.175, f32[2,32,32,1536]{3,2,1,0:T(8,128)} %get-tuple-element.174), kind=kLoop, calls=%fused_computation.78 | loop fusion | flops 10653696 | bytes 64536576 | tf_op jit(solution)/shard_map/transpose(jvp())/add_any | solution.py:28
  334.5 31.8 %fusion.71 = bf16[2,32,32,1536]{3,2,1,0:T(8,128)(2,1)} fusion(f32[2,32,32,1536]{3,2,1,0:T(8,128)} %get-tuple-element.182, f32[2,32,32,1536]{3,2,1,0:T(8,128)} %get-tuple-element.181, f32[2,32,32,1536]{3,2,1,0:T(8,128)} %get-tuple-element.180, f32[2,32,32,1536]{3,2,1,0:T(8,128)} %get-tuple-element.179, f32[2,32,32,1536]{3,2,1,0:T(8,128)} %get-tuple-element.178, ...), kind=kLoop, calls=%fused_computation.86 | loop fusion | flops 18874368 | bytes 81788928 | tf_op jit(solution)/shard_map/convert.21
  366.4 9.0 fusion.108
  375.5 9.5 fusion.111
  385.0 76.4 %all-reduce.49.cloned.1.call-done = bf16[2,1024,768]{2,1,0:T(8,128)(2,1)} async-done(((bf16[2,1024,768]{2,1,0:T(8,128)(2,1)}), bf16[2,1024,768]{2,1,0:T(8,128)(2,1)}) %all-reduce.49.cloned.1.call-update) | async-done | bytes 3145744 | tf_op jit(solution)/shard_map/psum | solution.py:195
  461.4 5.8 fusion.85
  467.9 5.0 fusion.89
  473.0 4.4 fusion.86
  483.1 3.5 reshape.335
  488.0 5.9 reshape_reshape.7
  493.9 4.8 copy.117
  498.7 75.4 %while.21 = (s32[]{:T(128)}, bf16[2,4,256,3,6,64]{2,5,4,1,3,0:T(8,128)(2,1)}, bf16[2,4,256,3,6,64]{2,5,4,1,3,0:T(8,128)(2,1)}, s32[2,4,256]{2,1,0:T(4,128)S(1)}, bf16[2,4,256,6,64]{2,4,3,1,0:T(8,128)(2,1)}, /*index=5*/s32[]{:T(128)}) while((s32[]{:T(128)}, bf16[2,4,256,3,6,64]{2,5,4,1,3,0:T(8,128)(2,1)}, ...), condition=%wide.region_17.19_spmd, body=%wide.region_13.18_spmd.sunk | while | flops 1049507584 | bytes 108715136 | solution.py:208
  501.9 3.9 fusion.176
  505.8 3.7 fusion.178
  509.5 10.1 fusion.180
  519.7 11.0 fusion.179
  530.7 4.2 fusion.177
  539.5 3.9 fusion.176
  543.5 3.7 fusion.178
  547.1 10.1 fusion.180
  557.3 11.0 fusion.179
  568.3 4.2 fusion.177
  574.2 12.6 copy.118
  586.8 16.2 %dot_general.82 = bf16[2,2,2,16,16,3,384]{6,4,3,5,2,1,0:T(8,128)(2,1)} reshape(bf16[2,4,256,3,6,64]{5,4,2,3,1,0:T(8,128)(2,1)} %copy.118) | data formatting | bytes 9437184 | tf_op jit(solution)/shard_map/lgtch,dch->lgtd/dot_general | solution.py:213
  603.0 7.3 fusion.96
  610.3 4.9 copy.120
  615.2 7.7 convert_element_type.144
  623.0 5.7 convolution_bitcast_fusion.3
  629.3 12.6 convolution_bitcast_fusion.1
  642.0 9.7 convolution_bitcast_fusion
  652.0 38.9 %multiply_reduce_fusion.9 = (f32[1536]{0:T(1024)S(1)}, f32[1536]{0:T(1024)S(1)}, f32[1536]{0:T(1024)S(1)}, f32[1536]{0:T(1024)S(1)}, f32[1536]{0:T(1024)S(1)}, /...) fusion(f32[2,32,32,1536]{3,2,1,0:T(8,128)} %bitcast.266, f32[2,32,32,1536]{3,2,1,0:T(8,128)} %bitcast.265), kind=kLoop, calls=%fused_computation.104 | loop fusion | flops 50319360 | bytes 25214976 | tf_op jit(solution)/shard_map/transpose(jvp())/reduce_sum | solution.py:29
  691.1 9.3 multiply_reduce_fusion.5
  701.8 6.1 convolution_bitcast_fusion.2
  710.8 65.8 %all-reduce.55.cloned.1.call-done = (bf16[2,1024,768]{2,1,0:T(8,128)(2,1)}, bf16[2,1024,768]{2,1,0:T(8,128)(2,1)}) async-done(((bf16[2,1024,768]{2,1,0:T(8,128)(2,1)}, bf16[2,1024,768]{2,1,0:T(8,128)(2,1)}), (bf16[2,1024,768]{2,1,0:T(8,128)(2,1)}, bf16[2,1024,768]{2,1,0:T(8,128)(2,1)})) %all-reduce.55.cloned.1.call-update) | async-done | bytes 6291472 | tf_op jit(solution)/shard_map/psum | solution.py:177
  776.7 20.0 %broadcast_multiply_fusion.9 = (f32[2,32,32,768]{3,2,1,0:T(8,128)}, f32[2,32,32,768]{3,2,1,0:T(8,128)}, f32[2,32,32,768]{3,2,1,0:T(8,128)}, f32[2,32,32,768]{3,2...) fusion(f32[768]{0:T(1024)S(1)} %copy-done.55, ...), kind=kLoop, calls=%fused_computation.183 | loop fusion | flops 15728640 | bytes 59796480 | tf_op jit(solution)/shard_map/transpose(jvp())/mul | solution.py:29
  796.7 11.0 pad_add_fusion.6
  807.6 19.6 %fusion.132 = (bf16[2,768]{1,0:T(2,128)(2,1)S(1)}, f32[2,32,32,768]{3,2,1,0:T(8,128)}) fusion(f32[2,32,32,768]{3,2,1,0:T(8,128)} %get-tuple-element.189, f32[2,32,32,768]{3,2,1,0:T(8,128)} %get-tuple-element.190, f32[2,32,32,768]{3,2,1,0:T(8,128)} %get-tuple-element.191, f32[2,32,32,768]{3,2,1,0:T(8,128)} %get-tuple-element.192, ...), kind=kLoop, calls=%fused_computation.281 | loop fusion | flops 11008512 | bytes 50334720 | tf_op jit(solution)/shard_map/transpose(jvp())/reduce_sum | solution.py:107
  827.3 4.7 fusion.91
  833.8 6.2 fusion.84
  840.1 9.4 multiply_reduce_fusion.18
  850.3 14.4 fusion.93
  864.8 4.9 fusion.136
  876.1 7.2 fusion.128
  883.3 35.2 %reduce-scatter.12.cloned.1.call-done = f32[48,1536]{1,0:T(8,128)} async-done(((f32[768,1536]{1,0:T(8,128)}), f32[48,1536]{1,0:T(8,128)}) %reduce-scatter.12.cloned.1.call-update) | async-done | bytes 294928 | tf_op jit(solution)/shard_map/reduce_scatter | solution.py:228
  918.6 78.9 %reduce-scatter.14.cloned.1.call-done = f32[48,1536]{1,0:T(8,128)} async-done(((f32[768,1536]{1,0:T(8,128)}), f32[48,1536]{1,0:T(8,128)}) %reduce-scatter.14.cloned.1.call-update) | async-done | bytes 294928 | tf_op jit(solution)/shard_map/reduce_scatter | solution.py:229
  997.5 72.0 %reduce-scatter.8.cloned.1.call-done = f32[48,3,384]{2,0,1:T(8,128)} async-done(((f32[768,3,384]{2,0,1:T(8,128)}), f32[48,3,384]{2,0,1:T(8,128)}) %reduce-scatter.8.cloned.1.call-update) | async-done | bytes 221200 | tf_op jit(solution)/shard_map/reduce_scatter | solution.py:226
  1069.5 92.0 %all-reduce.51.cloned.1.call-done = (f32[9,768]{1,0:T(8,128)}, f32[9,1536]{1,0:T(8,128)}) async-done(((f32[9,768]{1,0:T(8,128)}, f32[9,1536]{1,0:T(8,128)}), (f32[9,768]{1,0:T(8,128)}, f32[9,1536]{1,0:T(8,128)})) %all-reduce.51.cloned.1.call-update) | async-done | bytes 82960 | tf_op jit(solution)/shard_map/psum | solution.py:237
  1161.4 143.8 %all-reduce.53.cloned.1.call-done = (f32[1000,768]{1,0:T(8,128)}, f32[1000,768]{1,0:T(8,128)}) async-done(((f32[1000,768]{1,0:T(8,128)}, f32[1000,768]{1,0:T(8,128)}), (f32[1000,768]{1,0:T(8,128)}, f32[1000,768]{1,0:T(8,128)})) %all-reduce.53.cloned.1.call-update) | async-done | bytes 6144016 | tf_op jit(solution)/shard_map/psum | solution.py:237
  1305.2 150.1 %reduce-scatter.6.cloned.1.call-done = f32[48,4608]{1,0:T(8,128)} async-done(((f32[768,4608]{1,0:T(8,128)}), f32[48,4608]{1,0:T(8,128)}) %reduce-scatter.6.cloned.1.call-update) | async-done | bytes 884752 | tf_op jit(solution)/shard_map/reduce_scatter | solution.py:234
  1455.3 3.9 copy.198
  (300 shorter events, 77.9 us)
Async XLA Ops:
  7.2 253.0 %copy-start = (bf16[768,1536]{1,0:T(8,128)(2,1)S(1)}, bf16[768,1536]{1,0:T(8,128)(2,1)}, u32[]{:S(2)}) copy-start(bf16[768,1536]{1,0:T(8,128)(2,1)} %param.32) | copy-start | bytes 7077892
  7.2 183.2 %all-reduce.47.cloned.1.call-start = ((), (), s32[]{:S(2)}) async-start(), calls=%async_computation.5 | async-start | bytes 6291456 | tf_op jit(solution)/shard_map/psum | solution.py:168
  13.7 9.8 copy-start.70
  17.9 9.2 copy-start.29
  17.9 9.2 copy-start.46
  20.5 6.6 copy-start.25
  23.6 25.8 %copy-start.52 = (f32[768]{0:T(1024)}, f32[768]{0:T(1024)S(1)}, u32[]{:S(2)}) copy-start(f32[768]{0:T(1024)S(1)} %get-tuple-element.129) | copy-start | bytes 9220
  23.6 25.8 %copy-start.54 = (f32[768]{0:T(1024)}, f32[768]{0:T(1024)S(1)}, u32[]{:S(2)}) copy-start(f32[768]{0:T(1024)S(1)} %get-tuple-element.130) | copy-start | bytes 9220
  23.6 25.8 %copy-start.56 = (f32[768]{0:T(1024)}, f32[768]{0:T(1024)S(1)}, u32[]{:S(2)}) copy-start(f32[768]{0:T(1024)S(1)} %get-tuple-element.131) | copy-start | bytes 9220
  23.6 25.8 %copy-start.58 = (f32[768]{0:T(1024)}, f32[768]{0:T(1024)S(1)}, u32[]{:S(2)}) copy-start(f32[768]{0:T(1024)S(1)} %get-tuple-element.132) | copy-start | bytes 9220
  23.6 25.8 %copy-start.60 = (f32[768]{0:T(1024)}, f32[768]{0:T(1024)S(1)}, u32[]{:S(2)}) copy-start(f32[768]{0:T(1024)S(1)} %get-tuple-element.133) | copy-start | bytes 9220
  23.6 25.8 %copy-start.62 = (f32[768]{0:T(1024)}, f32[768]{0:T(1024)S(1)}, u32[]{:S(2)}) copy-start(f32[768]{0:T(1024)S(1)} %get-tuple-element.134) | copy-start | bytes 9220
  23.6 25.8 %copy-start.64 = (f32[768]{0:T(1024)}, f32[768]{0:T(1024)S(1)}, u32[]{:S(2)}) copy-start(f32[768]{0:T(1024)S(1)} %get-tuple-element.135) | copy-start | bytes 9220
  23.6 25.8 %copy-start.66 = (f32[768]{0:T(1024)}, f32[768]{0:T(1024)S(1)}, u32[]{:S(2)}) copy-start(f32[768]{0:T(1024)S(1)} %get-tuple-element.136) | copy-start | bytes 9220
  23.6 25.8 %copy-start.68 = (f32[768]{0:T(1024)}, f32[768]{0:T(1024)S(1)}, u32[]{:S(2)}) copy-start(f32[768]{0:T(1024)S(1)} %get-tuple-element.137) | copy-start | bytes 9220
  60.7 6.7 copy-start.77
  82.8 15.5 %copy-start.19 = (bf16[768,384]{1,0:T(8,128)(2,1)S(1)}, bf16[768,384]{1,0:T(8,128)(2,1)}, u32[]{:S(2)}) copy-start(bf16[768,384]{1,0:T(8,128)(2,1)} %param.29) | copy-start | bytes 1769476
  94.1 7.8 copy-start.51
  101.8 359.6 %all-reduce.49.cloned.1.call-start = ((), (), s32[]{:S(2)}) async-start(), calls=%async_computation.6 | async-start | bytes 6291456 | tf_op jit(solution)/shard_map/psum | solution.py:195
  101.8 375.6 %copy-start.21 = (f32[2,1,1,768]{3,0,1,2:T(2,128)}, f32[2,1,1,768]{3,0,1,2:T(2,128)S(1)}, u32[]{:S(2)}) copy-start(f32[2,1,1,768]{3,0,1,2:T(2,128)S(1)} %copy.168) | copy-start | bytes 18436
  101.9 371.1 %copy-start.33 = (f32[2,1,1,768]{3,0,1,2:T(2,128)}, f32[2,1,1,768]{3,0,1,2:T(2,128)S(1)}, u32[]{:S(2)}) copy-start(f32[2,1,1,768]{3,0,1,2:T(2,128)S(1)} %copy.164) | copy-start | bytes 18436
  101.9 95.6 %copy-start.78 = (f32[2,1,1,768]{3,0,1,2:T(2,128)}, f32[2,1,1,768]{3,0,1,2:T(2,128)S(1)}, u32[]{:S(2)}) copy-start(f32[2,1,1,768]{3,0,1,2:T(2,128)S(1)} %copy.163) | copy-start | bytes 18436
  101.9 158.2 %copy-start.48 = (f32[2,1,1,768]{3,0,1,2:T(2,128)}, f32[2,1,1,768]{3,0,1,2:T(2,128)S(1)}, u32[]{:S(2)}) copy-start(f32[2,1,1,768]{3,0,1,2:T(2,128)S(1)} %copy.165) | copy-start | bytes 18436
  190.4 7.1 copy-start.84
  195.1 277.8 %copy-start.27 = (f32[2,1024]{1,0:T(2,128)}, f32[2,1024]{1,0:T(2,128)S(1)}, u32[]{:S(2)}) copy-start(f32[2,1024]{1,0:T(2,128)S(1)} %broadcast_multiply_fusion.18) | copy-start | bytes 24580
  197.5 275.4 %copy-start.44 = (f32[2,1024]{1,0:T(2,128)}, f32[2,1024]{1,0:T(2,128)S(1)}, u32[]{:S(2)}) copy-start(f32[2,1024]{1,0:T(2,128)S(1)} %fusion.127) | copy-start | bytes 24580
  375.4 401.2 %all-reduce.55.cloned.1.call-start = ((), (), s32[]{:S(2)}) async-start(), calls=%async_computation.14 | async-start | bytes 12582912 | tf_op jit(solution)/shard_map/psum | solution.py:177
  385.0 82.2 %copy-start.43 = (f32[2,1024]{1,0:T(2,128)S(1)}, f32[2,1024]{1,0:T(2,128)}, u32[]{:S(2)}) copy-start(f32[2,1024]{1,0:T(2,128)} %copy-done.42) | copy-start | bytes 24580
  473.0 7.1 copy-start.20
  488.0 10.7 copy-start.24
  586.8 16.2 %copy-start.86 = (bf16[768,3,384]{2,0,1:T(8,128)(2,1)S(1)}, bf16[768,3,384]{2,0,1:T(8,128)(2,1)}, u32[]{:S(2)}) copy-start(bf16[768,3,384]{2,0,1:T(8,128)(2,1)} %param.28) | copy-start | bytes 5308420
  615.2 7.8 copy-start.18
  615.2 7.8 copy-start.22
  623.0 260.4 %reduce-scatter.10.cloned.1.call-start = ((), (), s32[]{:S(2)}) async-start(), calls=%async_computation.9 | async-start | bytes 1253376 | tf_op jit(solution)/shard_map/reduce_scatter | solution.py:227
  628.7 13.3 copy-start.49
  628.7 289.8 %reduce-scatter.12.cloned.1.call-start = ((), (), s32[]{:S(2)}) async-start(), calls=%async_computation.10 | async-start | bytes 5013504 | tf_op jit(solution)/shard_map/reduce_scatter | solution.py:228
  641.9 355.5 %reduce-scatter.14.cloned.1.call-start = ((), (), s32[]{:S(2)}) async-start(), calls=%async_computation.11 | async-start | bytes 5013504 | tf_op jit(solution)/shard_map/reduce_scatter | solution.py:229
  651.8 417.7 %reduce-scatter.8.cloned.1.call-start = ((), (), s32[]{:S(2)}) async-start(), calls=%async_computation.8 | async-start | bytes 3760128 | tf_op jit(solution)/shard_map/reduce_scatter | solution.py:226
  652.0 49.1 %slice-start.2 = ((s8[4718592]{0:T(1024)(128)(4,1)}), s8[524288]{0:T(1024)(128)(4,1)S(1)}, s32[]{:S(2)}) async-start(s8[4718592]{0:T(1024)(128)(4,1)} %bitcast.277), calls=%async_computation.17 | async-start | bytes 1048576
  691.0 10.1 slice-start.3
  691.1 10.7 copy-start.15
  707.9 68.7 %copy-start.53 = (f32[768]{0:T(1024)S(1)}, f32[768]{0:T(1024)}, u32[]{:S(2)}) copy-start(f32[768]{0:T(1024)} %copy-done.52) | copy-start | bytes 9220
  707.9 68.7 %copy-start.55 = (f32[768]{0:T(1024)S(1)}, f32[768]{0:T(1024)}, u32[]{:S(2)}) copy-start(f32[768]{0:T(1024)} %copy-done.54) | copy-start | bytes 9220
  707.9 68.7 %copy-start.57 = (f32[768]{0:T(1024)S(1)}, f32[768]{0:T(1024)}, u32[]{:S(2)}) copy-start(f32[768]{0:T(1024)} %copy-done.56) | copy-start | bytes 9220
  707.9 68.8 %copy-start.59 = (f32[768]{0:T(1024)S(1)}, f32[768]{0:T(1024)}, u32[]{:S(2)}) copy-start(f32[768]{0:T(1024)} %copy-done.58) | copy-start | bytes 9220
  707.9 68.8 %copy-start.61 = (f32[768]{0:T(1024)S(1)}, f32[768]{0:T(1024)}, u32[]{:S(2)}) copy-start(f32[768]{0:T(1024)} %copy-done.60) | copy-start | bytes 9220
  707.9 68.8 %copy-start.63 = (f32[768]{0:T(1024)S(1)}, f32[768]{0:T(1024)}, u32[]{:S(2)}) copy-start(f32[768]{0:T(1024)} %copy-done.62) | copy-start | bytes 9220
  707.9 68.8 %copy-start.65 = (f32[768]{0:T(1024)S(1)}, f32[768]{0:T(1024)}, u32[]{:S(2)}) copy-start(f32[768]{0:T(1024)} %copy-done.64) | copy-start | bytes 9220
  707.9 68.8 %copy-start.67 = (f32[768]{0:T(1024)S(1)}, f32[768]{0:T(1024)}, u32[]{:S(2)}) copy-start(f32[768]{0:T(1024)} %copy-done.66) | copy-start | bytes 9220
  707.9 68.8 %copy-start.69 = (f32[768]{0:T(1024)S(1)}, f32[768]{0:T(1024)}, u32[]{:S(2)}) copy-start(f32[768]{0:T(1024)} %copy-done.68) | copy-start | bytes 9220
  707.9 453.5 %all-reduce.51.cloned.1.call-start = ((), (), s32[]{:S(2)}) async-start(), calls=%async_computation.12 | async-start | bytes 294912 | tf_op jit(solution)/shard_map/psum | solution.py:237
  807.6 19.7 %copy-start.26 = (f32[2,1024]{1,0:T(2,128)S(1)}, f32[2,1024]{1,0:T(2,128)}, u32[]{:S(2)}) copy-start(f32[2,1024]{1,0:T(2,128)} %copy-done.25) | copy-start | bytes 24580
  807.6 19.7 %copy-start.30 = (f32[2,1,1,768]{3,0,1,2:T(2,128)S(1)}, f32[2,1,1,768]{3,0,1,2:T(2,128)}, u32[]{:S(2)}) copy-start(f32[2,1,1,768]{3,0,1,2:T(2,128)} %copy-done.29) | copy-start | bytes 18436
  827.3 6.5 copy-start.8
  827.3 6.5 copy-start.32
  827.3 12.7 slice-start
  840.0 10.2 copy-start.76
  840.0 10.3 copy-start.75
  864.8 8.1 copy-start.81
  872.9 432.3 %all-reduce.53.cloned.1.call-start = ((), (), s32[]{:S(2)}) async-start(), calls=%async_computation.13 | async-start | bytes 12288000 | tf_op jit(solution)/shard_map/psum | solution.py:237
  876.0 579.3 %reduce-scatter.6.cloned.1.call-start = ((), (), s32[]{:S(2)}) async-start(), calls=%async_computation.7 | async-start | bytes 15040512 | tf_op jit(solution)/shard_map/reduce_scatter | solution.py:234
  1161.4 299.4 %copy-start.50 = (f32[9,768]{1,0:T(8,128)S(1)}, f32[9,768]{1,0:T(8,128)}, u32[]{:S(2)}) copy-start(f32[9,768]{1,0:T(8,128)} %get-tuple-element.308) | copy-start | bytes 82948
  1161.4 300.0 %copy-start.35 = (f32[9,1536]{1,0:T(8,128)S(1)}, f32[9,1536]{1,0:T(8,128)}, u32[]{:S(2)}) copy-start(f32[9,1536]{1,0:T(8,128)} %get-tuple-element.311) | copy-start | bytes 165892
  1455.3 6.8 copy-start.1
  (39 other events, 164.6 us)
Sparse Core Ops, SparseCore 0:
  101.9 88.4 all-reduce.46
  375.6 85.7 all-reduce.48
  623.0 153.5 all-reduce.54
  781.1 58.0 reduce-scatter.9
  844.0 74.5 reduce-scatter.11
  922.9 74.5 reduce-scatter.13
  1002.4 66.9 reduce-scatter.7
  1074.5 86.8 all-reduce.50
  1166.3 138.8 all-reduce.52
  1309.8 145.4 reduce-scatter.5
where the time goes:
time: 1470 us
  waiting for transfers between devices  803 us (55%)
  other arithmetic  316 us (21%)
  matrix products  219 us (15%)
  local copies, waits for them, and re-layouts  114 us (8%)
  between operations  15.8 us (1%)
    psum x2, waiting for transfers between devices, local(): lax.psum((part_steps, part_labels, grad_kernel_a, grad_kernel_f), 'dp')  236 us
    reduce_scatter x1, waiting for transfers between devices, local(): lax.psum_scatter(part_mod, 'dp', scatter_dimension=0, tiled=True)  150 us
    psum x1, waiting for transfers between devices, local(): lax.psum(attn_part.astype(jnp.bfloat16), 'mp').astype(jnp.float32)  88.3 us
    reduce_scatter x1, waiting for transfers between devices, local(): lax.psum_scatter(grad_w_down, 'dp', scatter_dimension=0, tiled=True)  78.9 us
    psum x1, waiting for transfers between devices, local(): lax.psum(grad_normed_part.astype(jnp.bfloat16), 'mp').astype(jnp.float32)  76.4 us
    reduce_scatter x1, waiting for transfers between devices, local(): lax.psum_scatter(grad_w_qkv, 'dp', scatter_dimension=0, tiled=True)  72 us
    psum x1, waiting for transfers between devices, local(): lax.psum(down_part.astype(jnp.bfloat16), 'mp').astype(jnp.float32)  65.8 us
    reduce_sum x3, other arithmetic, depthwise(): summed = summed + kernel[row_off * 3 + col_off] * window  57.6 us
  transfers between devices with their start and end apart: 10, of which 9 were waited for; matrix products, arithmetic and copies ran while one was open for 14% of the time, Pallas kernels for 0%

commit v1 on v0

v1 whole, which is shorter than its diff:
```python
from functools import partial

import jax
import jax.numpy as jnp
from jax import lax
from jax.experimental import pallas as pl
from jax.experimental.pallas import tpu as pltpu
from jax.sharding import PartitionSpec as P

SIDE = 32
HALF = SIDE // 2
HEAD_DIM = 64
GROUPS = 4
LANES = 128
TILE = 256
EPS = 1e-06
PITCH = HALF + 8
GROUP_ROWS = (HALF + 2) * PITCH + 8
PAD_ROWS = GROUPS * GROUP_ROWS
GELU_A = 0.7978845608028654
GELU_B = 0.044715
F32 = jnp.float32
BF16 = jnp.bfloat16
VMEM_BYTES = 60 * 1024 * 1024


def params(count=1):
    return pltpu.CompilerParams(
        dimension_semantics=("arbitrary",) * count, vmem_limit_bytes=VMEM_BYTES
    )


def whole(shape):
    zeros = (0,) * len(shape)
    return pl.BlockSpec(shape, lambda *_: zeros, pipeline_mode=pl.Buffered(1))


def dot(left, right):
    return jnp.dot(left, right, preferred_element_type=F32)


def dot_nt(left, right):
    return lax.dot_general(left, right, (((1,), (1,)), ((), ())), preferred_element_type=F32)


def pad_row(group, row, shift=0):
    return group * GROUP_ROWS + (row + 1) * PITCH + 8 + shift


AROUND = ((1, -1), (0, 0), (1, 0), (0, 1))


def neighbours(grid_ref, lane_block, row):
    found = []
    for row_par, row_off in AROUND:
        line = []
        for col_par, col_off in AROUND:
            const = pad_row(row_par * 2 + col_par, row_off, col_off)
            line.append(grid_ref[lane_block, pl.ds(row * PITCH + const, HALF), :])
        found.append(line)
    return found


def taps_of(kern_ref, lanes):
    return [
        jnp.broadcast_to(kern_ref[tap : tap + 1, lanes].astype(F32), (HALF, LANES))
        for tap in range(9)
    ]


def conv_at(found, taps, row_par, col_par):
    total = None
    for row_off in range(3):
        for col_off in range(3):
            term = taps[row_off * 3 + col_off] * found[row_par + row_off][col_par + col_off]
            total = term if total is None else total + term
    return total


def conv_back_at(found, taps, sums, source, row_par, col_par):
    total = None
    sums = list(sums)
    for row_off in range(3):
        for col_off in range(3):
            tap = row_off * 3 + col_off
            near = found[row_par + 2 - row_off][col_par + 2 - col_off]
            term = taps[tap] * near
            total = term if total is None else total + term
            part = source * near
            sums[tap] = sums[tap] + (part[:8] + part[8:])
    return total, tuple(sums)


def no_sums():
    return tuple(jnp.zeros((8, LANES), F32) for _ in range(9))


def split_lanes(values_in):
    count = values_in.shape[-1] // LANES
    return [values_in[:, j * LANES : (j + 1) * LANES] for j in range(count)]


def norm_parts(parts):
    width = len(parts) * LANES
    mean = jnp.sum(sum(parts[1:], parts[0]), axis=-1, keepdims=True) * (1.0 / width)
    centre = [part - mean for part in parts]
    squares = [part * part for part in centre]
    var = jnp.sum(sum(squares[1:], squares[0]), axis=-1, keepdims=True) * (1.0 / width)
    rstd = lax.rsqrt(var + EPS)
    return [part * rstd for part in centre], rstd


def norm_rows(values_in):
    mean = jnp.mean(values_in, axis=-1, keepdims=True)
    centre = values_in - mean
    rstd = lax.rsqrt(jnp.mean(centre * centre, axis=-1, keepdims=True) + EPS)
    return centre * rstd, rstd


def group_of(row_par, col_par):
    return row_par * 2 + col_par


def first_kernel(
    idx, tok_ref, cot_ref, mod_ref, kern_ref, conv_out, tok_out, cot_out, tok_tmp, cot_tmp, grid
):
    width = tok_ref.shape[-1]
    count = width // LANES
    grid[...] = jnp.zeros(grid.shape, F32)

    def one_row(row, carry):
        for row_par in range(2):
            start = pl.multiple_of((row * 2 + row_par) * SIDE, SIDE)
            values = tok_ref[0, pl.ds(start, SIDE), :].astype(F32)
            grads = cot_ref[0, pl.ds(start, SIDE), :].astype(F32)
            for j in range(count):
                tok_tmp[row_par, j] = values[:, j * LANES : (j + 1) * LANES]
                cot_tmp[row_par, j] = grads[:, j * LANES : (j + 1) * LANES]
            for col_par in range(2):
                group = group_of(row_par, col_par)
                out_row = pl.multiple_of(group * TILE + row * HALF, HALF)
                parts = [tok_tmp[row_par, j, pl.ds(col_par, HALF, stride=2), :] for j in range(count)]
                for j in range(count):
                    lanes = slice(j * LANES, (j + 1) * LANES)
                    tok_out[pl.ds(out_row, HALF), lanes] = parts[j].astype(BF16)
                    cot_out[pl.ds(out_row, HALF), lanes] = cot_tmp[
                        row_par, j, pl.ds(col_par, HALF, stride=2), :
                    ].astype(BF16)
                normed, _ = norm_parts(parts)
                for j in range(count):
                    lanes = slice(j * LANES, (j + 1) * LANES)
                    value = normed[j] * (1.0 + mod_ref[1:2, lanes]) + mod_ref[0:1, lanes]
                    grid[j, pl.ds(row * PITCH + pad_row(group, 0), HALF), :] = value
        return carry

    lax.fori_loop(0, HALF, one_row, 0)
    for j in range(count):
        lanes = slice(j * LANES, (j + 1) * LANES)
        taps = taps_of(kern_ref, lanes)

        def one_conv(row, carry, j=j, lanes=lanes, taps=taps):
            found = neighbours(grid, j, row)
            for row_par in range(2):
                for col_par in range(2):
                    out_row = pl.multiple_of(group_of(row_par, col_par) * TILE + row * HALF, HALF)
                    value = conv_at(found, taps, row_par, col_par)
                    conv_out[pl.ds(out_row, HALF), lanes] = value.astype(BF16)
            return carry

        lax.fori_loop(0, HALF, one_conv, 0)


def first_stage(idx, tokens, cotangent, mod, kern):
    _, length, width = tokens.shape
    shape = jax.ShapeDtypeStruct((length, width), BF16)
    mine = pl.BlockSpec((1, length, width), lambda i, idx: (idx[0], 0, 0))
    return pl.pallas_call(
        first_kernel,
        out_shape=(shape, shape, shape),
        grid_spec=pltpu.PrefetchScalarGridSpec(
            num_scalar_prefetch=1,
            grid=(1,),
            in_specs=[mine, mine, whole(mod.shape), whole(kern.shape)],
            out_specs=[whole((length, width))] * 3,
            scratch_shapes=[
                pltpu.VMEM((2, width // LANES, SIDE, LANES), F32),
                pltpu.VMEM((2, width // LANES, SIDE, LANES), F32),
                pltpu.VMEM((width // LANES, PAD_ROWS, LANES), F32),
            ],
        ),
        compiler_params=params(),
        name="norm_conv",
        cost_estimate=pl.CostEstimate(flops=40_000_000, bytes_accessed=8_000_000, transcendentals=0),
    )(idx, tokens, cotangent, mod, kern)


def head_mask(values_in, which):
    lane = lax.broadcasted_iota(jnp.int32, values_in.shape, 1)
    keep = lane < HEAD_DIM if which == 0 else lane >= HEAD_DIM
    return jnp.where(keep, values_in, jnp.zeros_like(values_in))


def soft_keys(keys, queries, keep):
    raw = dot_nt(keys, queries)
    scores = jnp.where(keep, raw * (HEAD_DIM**-0.5), -1e30)
    exponent = jnp.exp(scores - jnp.max(scores, axis=0, keepdims=True))
    return exponent * (1.0 / jnp.sum(exponent, axis=0, keepdims=True))


def attend_kernel(
    conv_ref, valid_ref, wa_ref, wb_ref, oa_ref, ob_ref, tok_ref, cot_ref, mod_ref,
    qkv_out, mixed_out, attn_out, res_out, norm_out, gdown_out,
):
    share = wa_ref.shape[-1]
    conved = conv_ref[...]
    keep = jnp.broadcast_to(valid_ref[0], (TILE, TILE)) > 0
    for side, weight_ref in enumerate((wa_ref, wb_ref)):
        for which in range(3):
            qkv_out[side, :, which * share : (which + 1) * share] = dot(
                conved, weight_ref[which]
            ).astype(BF16)
        for pair in range(share // LANES):
            lanes = [slice(t * share + pair * LANES, t * share + (pair + 1) * LANES) for t in range(3)]
            queries = qkv_out[side, :, lanes[0]]
            keys = qkv_out[side, :, lanes[1]]
            values_t = qkv_out[side, :, lanes[2]].astype(F32).T.astype(BF16)
            halves = []
            for which in range(2):
                probs = soft_keys(head_mask(keys, which), queries, keep).astype(BF16)
                halves.append(dot(values_t[which * HEAD_DIM : (which + 1) * HEAD_DIM], probs))
            mixed_t = jnp.concatenate(halves, axis=0)
            first = side * share + pair * LANES
            mixed_out[:, first : first + LANES] = mixed_t.T.astype(BF16)
    attn = dot_nt(mixed_out[:, :share], oa_ref[...]) + dot_nt(mixed_out[:, share:], ob_ref[...])
    attn_out[...] = attn
    residual = tok_ref[...].astype(F32) + mod_ref[2:3, :] * attn
    res_out[...] = residual
    normed, _ = norm_rows(residual)
    norm_out[...] = (normed * (1.0 + mod_ref[4:5, :]) + mod_ref[3:4, :]).astype(BF16)
    gdown_out[...] = (mod_ref[5:6, :] * cot_ref[...].astype(F32)).astype(BF16)


def attend_stage(conved, valid, w_own, w_other, o_own, o_other, tok, cot, mod):
    length, width = conved.shape
    share = w_own.shape[-1]
    rows = pl.BlockSpec((TILE, width), lambda g: (g, 0))
    qkv_rows = pl.BlockSpec((2, TILE, 3 * share), lambda g: (0, g, 0))
    low = jax.ShapeDtypeStruct((length, width), BF16)
    high = jax.ShapeDtypeStruct((length, width), F32)
    return pl.pallas_call(
        attend_kernel,
        out_shape=(jax.ShapeDtypeStruct((2, length, 3 * share), BF16), low, high, high, low, low),
        grid=(GROUPS,),
        in_specs=[
            rows,
            pl.BlockSpec((1, TILE, 1), lambda g: (g, 0, 0)),
            whole(w_own.shape),
            whole(w_other.shape),
            whole(o_own.shape),
            whole(o_other.shape),
            rows,
            rows,
            whole(mod.shape),
        ],
        out_specs=[qkv_rows, rows, rows, rows, rows, rows],
        compiler_params=params(),
        name="attend",
        cost_estimate=pl.CostEstimate(
            flops=8_000_000_000, bytes_accessed=30_000_000, transcendentals=3_200_000
        ),
    )(conved, valid, w_own, w_other, o_own, o_other, tok, cot, mod)


def gelu_pair(value):
    square = value * value
    inner = jnp.tanh(GELU_A * (value + GELU_B * (square * value)))
    cdf = 0.5 * (1.0 + inner)
    slope = cdf + (value * (0.5 * GELU_A)) * (1.0 - inner * inner) * (1.0 + (3.0 * GELU_B) * square)
    return value * cdf, slope


def ffn_kernel(
    idx, perm_ref, norm_ref, gdown_ref, up_ref, down_ref, kern_ref,
    up_keep, up_send, down_keep, down_send, kern_out, sum_out, gnorm_out,
    norm_t, gdown_t, grid_up, grid_gz, gact, active, gupper,
):
    width = norm_ref.shape[-1]
    chunk = up_ref.shape[-1]
    half_rows = up_keep.shape[0]
    first = pl.program_id(0) == 0

    @pl.when(first)
    def _():
        norm_t[...] = dot_nt(perm_ref[...], norm_ref[...]).astype(BF16)
        gdown_t[...] = dot_nt(perm_ref[...], gdown_ref[...]).astype(BF16)
        grid_up[...] = jnp.zeros(grid_up.shape, F32)
        grid_gz[...] = jnp.zeros(grid_gz.shape, F32)

    for block in range(chunk // TILE):
        cols = slice(block * TILE, (block + 1) * TILE)
        upper = dot(norm_ref[...], up_ref[:, cols])
        grads = dot(gdown_ref[...], down_ref[:, cols])
        for side in range(TILE // LANES):
            j = block * (TILE // LANES) + side
            lanes = slice(side * LANES, (side + 1) * LANES)
            gact[j] = grads[:, lanes]
            for group in range(GROUPS):
                for row in range(HALF):
                    at = group * TILE + row * HALF
                    grid_up[j, pl.ds(pad_row(group, row), HALF), :] = upper[at : at + HALF, lanes]

    def one_block(j, carry):
        lanes = pl.ds(pl.multiple_of(j * LANES, LANES), LANES)
        taps = taps_of(kern_ref, lanes)

        def forward(row, carry):
            found = neighbours(grid_up, j, row)
            for row_par in range(2):
                for col_par in range(2):
                    group = group_of(row_par, col_par)
                    out_row = pl.multiple_of(group * TILE + row * HALF, HALF)
                    act, slope = gelu_pair(conv_at(found, taps, row_par, col_par))
                    active[pl.ds(out_row, HALF), lanes] = act.astype(BF16)
                    grid_gz[j, pl.ds(row * PITCH + pad_row(group, 0), HALF), :] = (
                        gact[j, pl.ds(out_row, HALF), :] * slope
                    )
            return carry

        lax.fori_loop(0, HALF, forward, 0)

        def backward(row, sums):
            found = neighbours(grid_gz, j, row)
            for row_par in range(2):
                for col_par in range(2):
                    group = group_of(row_par, col_par)
                    out_row = pl.multiple_of(group * TILE + row * HALF, HALF)
                    source = grid_up[j, pl.ds(row * PITCH + pad_row(group, 0), HALF), :]
                    grad, sums = conv_back_at(found, taps, sums, source, row_par, col_par)
                    gupper[pl.ds(out_row, HALF), lanes] = grad.astype(BF16)
            return sums

        sums = lax.fori_loop(0, HALF, backward, no_sums())
        for tap in range(9):
            kern_out[tap : tap + 1, lanes] = jnp.sum(sums[tap], axis=0, keepdims=True)
        return carry

    lax.fori_loop(0, chunk // LANES, one_block, 0)

    mine = pl.multiple_of(idx[1] * half_rows, half_rows)
    theirs = pl.multiple_of((1 - idx[1]) * half_rows, half_rows)
    for block in range(chunk // TILE):
        cols = slice(block * TILE, (block + 1) * TILE)
        act = active[:, cols]
        gup = gupper[:, cols]
        down_send[:, cols] = dot(gdown_t[pl.ds(theirs, half_rows), :], act).astype(BF16)
        up_send[:, cols] = dot(norm_t[pl.ds(theirs, half_rows), :], gup).astype(BF16)
        down_keep[:, cols] = dot(gdown_t[pl.ds(mine, half_rows), :], act)
        up_keep[:, cols] = dot(norm_t[pl.ds(mine, half_rows), :], gup)
    for block in range(width // TILE):
        cols = slice(block * TILE, (block + 1) * TILE)
        part = dot_nt(active[...], down_ref[cols, :])
        gpart = dot_nt(gupper[...], up_ref[cols, :])

        @pl.when(first)
        def _(cols=cols, part=part, gpart=gpart):
            sum_out[:, cols] = part
            gnorm_out[:, cols] = gpart

        @pl.when(jnp.logical_not(first))
        def _(cols=cols, part=part, gpart=gpart):
            sum_out[:, cols] += part
            gnorm_out[:, cols] += gpart


def ffn_stage(idx, perm, normed, gdown, w_up, w_down, kern, chunk):
    length, width = normed.shape
    hidden = w_up.shape[-1]
    half_rows = width // 2
    cols = pl.BlockSpec((width, chunk), lambda i, idx: (0, i))
    half = pl.BlockSpec((half_rows, chunk), lambda i, idx: (0, i))
    small = pl.BlockSpec((9, chunk), lambda i, idx: (0, i))
    count = chunk // LANES
    keep = jax.ShapeDtypeStruct((half_rows, hidden), F32)
    send = jax.ShapeDtypeStruct((half_rows, hidden), BF16)
    full = jax.ShapeDtypeStruct((length, width), F32)
    return pl.pallas_call(
        ffn_kernel,
        out_shape=(keep, send, keep, send, jax.ShapeDtypeStruct((9, hidden), F32), full, full),
        grid_spec=pltpu.PrefetchScalarGridSpec(
            num_scalar_prefetch=1,
            grid=(hidden // chunk,),
            in_specs=[
                whole(perm.shape),
                whole(normed.shape),
                whole(gdown.shape),
                cols,
                cols,
                small,
            ],
            out_specs=[half, half, half, half, small, whole(full.shape), whole(full.shape)],
            scratch_shapes=[
                pltpu.VMEM((width, length), BF16),
                pltpu.VMEM((width, length), BF16),
                pltpu.VMEM((count, PAD_ROWS, LANES), F32),
                pltpu.VMEM((count, PAD_ROWS, LANES), F32),
                pltpu.VMEM((count, length, LANES), F32),
                pltpu.VMEM((length, chunk), BF16),
                pltpu.VMEM((length, chunk), BF16),
            ],
        ),
        compiler_params=params(),
        name="ffn",
        cost_estimate=pl.CostEstimate(
            flops=12 * length * width * hidden,
            bytes_accessed=4 * 1024 * 1024 * 6,
            transcendentals=length * hidden,
        ),
    )(idx, perm, normed, gdown, w_up, w_down, kern)


def middle_kernel(
    idx, perm_ref, res_ref, attn_ref, da_ref, db_ref, ga_ref, gb_ref, cot_ref, mixed_ref, oa_ref, ob_ref,
    mod_ref, out_ref, gres_out, gmix_out, sums_out, keep_out, send_out, ordered, total,
):
    share = oa_ref.shape[-1]
    width = res_ref.shape[-1]
    group = pl.program_id(0)
    residual = res_ref[...]
    cot = cot_ref[...].astype(F32)
    down = da_ref[...] + db_ref[...]
    result = residual + mod_ref[5:6, :] * down
    parity = (group // 2) * SIDE + lax.rem(group, 2)
    for row in range(HALF):
        for j in range(width // LANES):
            ordered[j, pl.ds(parity + row * 2 * SIDE, HALF, stride=2), :] = result[
                row * HALF : (row + 1) * HALF, j * LANES : (j + 1) * LANES
            ]
    grad_n = ga_ref[...] + gb_ref[...]
    normed, rstd = norm_rows(residual)
    scaled = grad_n * (1.0 + mod_ref[4:5, :])
    mean_a = jnp.mean(scaled, axis=-1, keepdims=True)
    mean_b = jnp.mean(scaled * normed, axis=-1, keepdims=True)
    gres = cot + rstd * (scaled - mean_a - normed * mean_b)
    gres_out[...] = gres
    sums = jnp.concatenate(
        [
            jnp.sum(gres * attn_ref[...], axis=0, keepdims=True),
            jnp.sum(grad_n, axis=0, keepdims=True),
            jnp.sum(grad_n * normed, axis=0, keepdims=True),
            jnp.sum(cot * down, axis=0, keepdims=True),
        ],
        axis=0,
    )
    gattn = (mod_ref[2:3, :] * gres).astype(BF16)
    gmix_out[:, :share] = dot(gattn, oa_ref[...]).astype(BF16)
    gmix_out[:, share:] = dot(gattn, ob_ref[...]).astype(BF16)
    part = dot(dot_nt(perm_ref[...], gattn).astype(BF16), mixed_ref[...])

    @pl.when(group == 0)
    def _():
        sums_out[...] = sums
        total[...] = part

    @pl.when(group > 0)
    def _():
        sums_out[...] += sums
        total[...] += part

    @pl.when(group == GROUPS - 1)
    def _():
        half_rows = width // 2
        keep_out[...] = total[pl.ds(pl.multiple_of(idx[1] * half_rows, half_rows), half_rows), :]
        send_out[...] = total[
            pl.ds(pl.multiple_of((1 - idx[1]) * half_rows, half_rows), half_rows), :
        ].astype(BF16)
        for j in range(width // LANES):
            out_ref[:, j * LANES : (j + 1) * LANES] = ordered[j].astype(BF16)


def middle_stage(idx, perm, res, attn, da, db, ga, gb, cot, mixed, o_own, o_other, mod):
    length, width = res.shape
    rows = pl.BlockSpec((TILE, width), lambda g, idx: (g, 0))
    half_rows = width // 2
    low = jax.ShapeDtypeStruct((length, width), BF16)
    return pl.pallas_call(
        middle_kernel,
        out_shape=(
            low,
            jax.ShapeDtypeStruct((length, width), F32),
            low,
            jax.ShapeDtypeStruct((4, width), F32),
            jax.ShapeDtypeStruct((half_rows, width), F32),
            jax.ShapeDtypeStruct((half_rows, width), BF16),
        ),
        grid_spec=pltpu.PrefetchScalarGridSpec(
            num_scalar_prefetch=1,
            grid=(GROUPS,),
            in_specs=[whole(perm.shape)]
            + [rows] * 8
            + [whole(o_own.shape), whole(o_other.shape), whole(mod.shape)],
            out_specs=[
                whole((length, width)),
                rows,
                rows,
                whole((4, width)),
                whole((half_rows, width)),
                whole((half_rows, width)),
            ],
            scratch_shapes=[
                pltpu.VMEM((width // LANES, length, LANES), F32),
                pltpu.VMEM((width, width), F32),
            ],
        ),
        compiler_params=params(),
        name="middle",
        cost_estimate=pl.CostEstimate(
            flops=4_000_000_000, bytes_accessed=32_000_000, transcendentals=0
        ),
    )(idx, perm, res, attn, da, db, ga, gb, cot, mixed, o_own, o_other, mod)


def attend_back_kernel(qkv_ref, gmix_ref, valid_ref, gqkv_out):
    share = qkv_ref.shape[-1] // 3
    keep = jnp.broadcast_to(valid_ref[0], (TILE, TILE)) > 0
    lane = lax.broadcasted_iota(jnp.int32, (TILE, LANES), 1)
    for side in range(2):
        for pair in range(share // LANES):
            lanes = [slice(t * share + pair * LANES, t * share + (pair + 1) * LANES) for t in range(3)]
            queries = qkv_ref[side, :, lanes[0]]
            keys = qkv_ref[side, :, lanes[1]]
            values = qkv_ref[side, :, lanes[2]]
            first = side * share + pair * LANES
            gmix = gmix_ref[:, first : first + LANES]
            keys_t = keys.astype(F32).T.astype(BF16)
            gq, gk, gv = [], [], []
            for which in range(2):
                probs = soft_keys(head_mask(keys, which), queries, keep)
                gprobs = dot_nt(head_mask(values, which), gmix)
                gv.append(dot(probs.astype(BF16), gmix))
                weighted = probs * gprobs
                gscores = weighted - probs * jnp.sum(weighted, axis=0, keepdims=True)
                graw = (gscores * (HEAD_DIM**-0.5)).astype(BF16)
                gk.append(dot(graw, queries))
                gq.append(dot(keys_t[which * HEAD_DIM : (which + 1) * HEAD_DIM], graw))
            gqkv_out[side, :, lanes[0]] = jnp.concatenate(gq, axis=0).T.astype(BF16)
            gqkv_out[side, :, lanes[1]] = jnp.where(lane < HEAD_DIM, gk[0], gk[1]).astype(BF16)
            gqkv_out[side, :, lanes[2]] = jnp.where(lane < HEAD_DIM, gv[0], gv[1]).astype(BF16)


def attend_back_stage(qkv, gmix, valid):
    length, width = gmix.shape
    rows = pl.BlockSpec((TILE, width), lambda g: (g, 0))
    qkv_rows = pl.BlockSpec((2, TILE, qkv.shape[-1]), lambda g: (0, g, 0))
    return pl.pallas_call(
        attend_back_kernel,
        out_shape=jax.ShapeDtypeStruct(qkv.shape, BF16),
        grid=(GROUPS,),
        in_specs=[qkv_rows, rows, pl.BlockSpec((1, TILE, 1), lambda g: (g, 0, 0))],
        out_specs=qkv_rows,
        compiler_params=params(),
        name="attend_back",
        cost_estimate=pl.CostEstimate(
            flops=12_000_000_000, bytes_accessed=12_000_000, transcendentals=3_200_000
        ),
    )(qkv, gmix, valid)


def qkv_grad_kernel(idx, perm_ref, conv_ref, gqkv_ref, keep_out, send_out, conv_t):
    @pl.when(pl.program_id(0) == 0)
    def _():
        conv_t[...] = dot_nt(perm_ref[...], conv_ref[...]).astype(BF16)

    half_rows = keep_out.shape[1]
    share = keep_out.shape[-1] // 3
    mine = pl.multiple_of(idx[1] * half_rows, half_rows)
    theirs = pl.multiple_of((1 - idx[1]) * half_rows, half_rows)
    for which in range(3):
        cols = slice(which * share, (which + 1) * share)
        grads = gqkv_ref[0, :, cols]
        send_out[0, :, cols] = dot(conv_t[pl.ds(theirs, half_rows), :], grads).astype(BF16)
        keep_out[0, :, cols] = dot(conv_t[pl.ds(mine, half_rows), :], grads)


def qkv_grad_stage(idx, perm, conved, gqkv):
    length, width = conved.shape
    cols = gqkv.shape[-1]
    half_rows = width // 2
    rows = pl.BlockSpec((1, half_rows, cols), lambda i, idx: (i, 0, 0))
    return pl.pallas_call(
        qkv_grad_kernel,
        out_shape=(
            jax.ShapeDtypeStruct((2, half_rows, cols), F32),
            jax.ShapeDtypeStruct((2, half_rows, cols), BF16),
        ),
        grid_spec=pltpu.PrefetchScalarGridSpec(
            num_scalar_prefetch=1,
            grid=(2,),
            in_specs=[
                whole(perm.shape),
                whole(conved.shape),
                pl.BlockSpec((1, length, cols), lambda i, idx: (i, 0, 0)),
            ],
            out_specs=[rows, rows],
            scratch_shapes=[pltpu.VMEM((width, length), BF16)],
        ),
        compiler_params=params(),
        name="qkv_grad",
        cost_estimate=pl.CostEstimate(
            flops=4_000_000_000, bytes_accessed=14_000_000, transcendentals=0
        ),
    )(idx, perm, conved, gqkv)


def last_kernel(
    gqkv_ref, wa_ref, wb_ref, tok_ref, gres_ref, mod_ref, kern_ref,
    gtok_out, sums_out, kern_out, grid_g, normed_s, grads_s, rstd_s,
):
    length, width = tok_ref.shape
    count = width // LANES
    share = wa_ref.shape[-1]
    grid_g[...] = jnp.zeros(grid_g.shape, F32)
    for block in range(width // TILE):
        rows = slice(block * TILE, (block + 1) * TILE)
        total = None
        for side, weight_ref in enumerate((wa_ref, wb_ref)):
            for which in range(3):
                part = dot_nt(
                    gqkv_ref[side, :, which * share : (which + 1) * share], weight_ref[which, rows, :]
                )
                total = part if total is None else total + part
        for side in range(TILE // LANES):
            j = block * (TILE // LANES) + side
            lanes = slice(side * LANES, (side + 1) * LANES)
            for group in range(GROUPS):
                for row in range(HALF):
                    at = group * TILE + row * HALF
                    grid_g[j, pl.ds(pad_row(group, row), HALF), :] = total[at : at + HALF, lanes]

    def one_norm(row, carry):
        at = pl.multiple_of(row * SIDE, SIDE)
        parts = split_lanes(tok_ref[pl.ds(at, SIDE), :].astype(F32))
        normed, rstd = norm_parts(parts)
        for j in range(count):
            normed_s[j, pl.ds(at, SIDE), :] = normed[j]
        rstd_s[pl.ds(at, SIDE), :] = jnp.broadcast_to(rstd, (SIDE, LANES))
        return carry

    lax.fori_loop(0, length // SIDE, one_norm, 0)

    for j in range(count):
        lanes = slice(j * LANES, (j + 1) * LANES)
        taps = taps_of(kern_ref, lanes)

        def backward(row, sums, j=j, lanes=lanes, taps=taps):
            found = neighbours(grid_g, j, row)
            for row_par in range(2):
                for col_par in range(2):
                    at = pl.multiple_of(group_of(row_par, col_par) * TILE + row * HALF, HALF)
                    source = normed_s[j, pl.ds(at, HALF), :] * (
                        1.0 + mod_ref[1:2, lanes]
                    ) + mod_ref[0:1, lanes]
                    grad, sums = conv_back_at(found, taps, sums, source, row_par, col_par)
                    grads_s[j, pl.ds(at, HALF), :] = grad
            return sums

        sums = lax.fori_loop(0, HALF, backward, no_sums())
        for tap in range(9):
            kern_out[tap : tap + 1, lanes] = jnp.sum(sums[tap], axis=0, keepdims=True)

    ordered = grid_g

    def one_back(row, carry):
        shifts, scales = carry
        shifts, scales = list(shifts), list(scales)
        for group in range(GROUPS):
            at = pl.multiple_of(group * TILE + row * HALF, HALF)
            normed = [normed_s[j, pl.ds(at, HALF), :] for j in range(count)]
            grads = [grads_s[j, pl.ds(at, HALF), :] for j in range(count)]
            rstd = rstd_s[pl.ds(at, HALF), :]
            scaled = []
            for j in range(count):
                lanes = slice(j * LANES, (j + 1) * LANES)
                prod = grads[j] * normed[j]
                shifts[j] = shifts[j] + (grads[j][:8] + grads[j][8:])
                scales[j] = scales[j] + (prod[:8] + prod[8:])
                scaled.append(grads[j] * (1.0 + mod_ref[1:2, lanes]))
            mixed = [scaled[j] * normed[j] for j in range(count)]
            mean_a = jnp.sum(sum(scaled[1:], scaled[0]), axis=-1, keepdims=True) * (1.0 / width)
            mean_b = jnp.sum(sum(mixed[1:], mixed[0]), axis=-1, keepdims=True) * (1.0 / width)
            start = (group // 2) * SIDE + group % 2
            for j in range(count):
                lanes = slice(j * LANES, (j + 1) * LANES)
                value = gres_ref[pl.ds(at, HALF), lanes] + rstd * (
                    scaled[j] - mean_a - normed[j] * mean_b
                )
                ordered[j, pl.ds(start + row * (2 * SIDE), HALF, stride=2), :] = value
        return tuple(shifts), tuple(scales)

    zero = tuple(jnp.zeros((8, LANES), F32) for _ in range(count))
    shifts, scales = lax.fori_loop(0, HALF, one_back, (zero, zero))
    for j in range(count):
        lanes = slice(j * LANES, (j + 1) * LANES)
        sums_out[0:1, lanes] = jnp.sum(shifts[j], axis=0, keepdims=True)
        sums_out[1:2, lanes] = jnp.sum(scales[j], axis=0, keepdims=True)
        gtok_out[:, lanes] = ordered[j, pl.ds(0, length), :].astype(BF16)


def last_stage(gqkv, w_own, w_other, tok, gres, mod, kern):
    length, width = tok.shape
    count = width // LANES
    operands = (gqkv, w_own, w_other, tok, gres, mod, kern)
    return pl.pallas_call(
        last_kernel,
        out_shape=(
            jax.ShapeDtypeStruct((length, width), BF16),
            jax.ShapeDtypeStruct((2, width), F32),
            jax.ShapeDtypeStruct((9, width), F32),
        ),
        grid=(1,),
        in_specs=[whole(each.shape) for each in operands],
        out_specs=[whole((length, width)), whole((2, width)), whole((9, width))],
        scratch_shapes=[
            pltpu.VMEM((count, PAD_ROWS, LANES), F32),
            pltpu.VMEM((count, length, LANES), F32),
            pltpu.VMEM((count, length, LANES), F32),
            pltpu.VMEM((length, LANES), F32),
        ],
        compiler_params=params(),
        name="conv_norm_back",
        cost_estimate=pl.CostEstimate(
            flops=4_000_000_000, bytes_accessed=16_000_000, transcendentals=0
        ),
    )(*operands)


def silu_of(values_in):
    return values_in * jax.nn.sigmoid(values_in)


def swap(values_in, axis, bit):
    size = lax.axis_size(axis)
    return lax.ppermute(values_in, axis, [(i, i ^ bit) for i in range(size)])


def spread(size, position):
    if size < 4:
        return position
    quarter = size // 4
    low, rest = position // (2 * quarter), position % (2 * quarter)
    return (rest % quarter) * 4 + (rest // quarter) * 2 + low


def row_permutation(size, width):
    block = width // size
    order = [spread(size, i // block) * block + i % block for i in range(width)]
    source = jnp.array(order, jnp.int32)
    return (source[:, None] == jnp.arange(width, dtype=jnp.int32)[None, :]).astype(BF16)


def halve(total, bit_set):
    rows = total.shape[0] // 2
    split = total.reshape((2, rows) + total.shape[1:])
    mine = lax.dynamic_index_in_dim(split, bit_set, 0, keepdims=False)
    theirs = lax.dynamic_index_in_dim(split, 1 - bit_set, 0, keepdims=False)
    return mine, theirs.astype(BF16)


def sum_rows(keep, send):
    size = lax.axis_size("dp")
    me = lax.axis_index("dp")
    total = keep + swap(send, "dp", 1).astype(F32)
    bits = [2]
    rest = size // 4
    while rest > 1:
        bits.append(rest * 2)
        rest //= 2
    for bit in bits:
        if bit >= size:
            continue
        mine, theirs = halve(total, (me // bit) % 2)
        total = mine + swap(theirs, "dp", bit).astype(F32)
    return total


def share_back(own, other):
    return own + swap(other.astype(BF16), "mp", 1).astype(F32)


def unshuffle(tokens_in):
    blocked = tokens_in.reshape(HALF, 2, HALF, 2)
    return blocked.transpose(1, 3, 0, 2).reshape(GROUPS, TILE)


def local(
    tokens,
    valid,
    steps,
    labels,
    w_mod,
    step_table,
    class_table,
    conv_attn,
    w_qkv,
    w_out,
    conv_ffn,
    w_up,
    w_down,
    cotangent,
):
    dp_size = lax.axis_size("dp")
    width = tokens.shape[-1]
    dp_at = lax.axis_index("dp")
    mp_at = lax.axis_index("mp")
    latent = dp_at * tokens.shape[0] + mp_at
    idx = jnp.stack([mp_at, dp_at % 2]).astype(jnp.int32)
    perm = row_permutation(dp_size, width)

    qkv_own = w_qkv.transpose(1, 0, 2)
    qkv_other = swap(qkv_own, "mp", 1)
    out_other = swap(w_out, "mp", 1)
    up_other = swap(w_up, "mp", 1)
    down_other = swap(w_down, "mp", 1)
    kern_other = swap(conv_ffn, "mp", 1)

    embedding = jnp.take(step_table, steps, axis=0).astype(F32) + jnp.take(
        class_table, labels, axis=0
    ).astype(F32)
    silu_value, silu_pull = jax.vjp(silu_of, embedding)
    silu_low = silu_value.astype(BF16)
    my_silu = lax.dynamic_slice_in_dim(silu_low, latent, 1)
    mod = jnp.dot(my_silu, w_mod, preferred_element_type=F32).reshape(6, width)

    my_valid = lax.dynamic_index_in_dim(valid, mp_at, 0, keepdims=False)
    keep = unshuffle(my_valid)[:, :, None]

    conved, tok, cot = first_stage(idx, tokens, cotangent, mod, conv_attn)
    qkv, mixed, attn, res, normed, gdown = attend_stage(
        conved, keep, qkv_own, qkv_other, w_out, out_other, tok, cot, mod
    )
    chunk = w_up.shape[-1] // 2
    first = ffn_stage(idx, perm, normed, gdown, w_up, w_down, conv_ffn, chunk)
    second = ffn_stage(idx, perm, normed, gdown, up_other, down_other, kern_other, chunk)
    output, gres, gmix, sums_mid, out_keep, out_send = middle_stage(
        idx, perm, res, attn, first[5], second[5], first[6], second[6], cot, mixed, w_out, out_other, mod
    )
    output_other = swap(output, "mp", 1)
    gqkv = attend_back_stage(qkv, gmix, keep)
    qkv_keep, qkv_send = qkv_grad_stage(idx, perm, conved, gqkv)
    gtok, sums_last, kern_a = last_stage(gqkv, qkv_own, qkv_other, tok, gres, mod, conv_attn)
    gtok_other = swap(gtok, "mp", 1)

    def both(mine, theirs):
        pair = jnp.stack([mine, theirs])
        return jnp.where(mp_at == 0, pair, pair[::-1])

    grad_up = share_back(sum_rows(first[0], first[1]), sum_rows(second[0], second[1]))
    grad_down = share_back(sum_rows(first[2], first[3]), sum_rows(second[2], second[3]))
    share = w_out.shape[-1]
    out_sum = sum_rows(out_keep, out_send)
    grad_out = share_back(out_sum[:, :share], out_sum[:, share:])
    qkv_own_sum = sum_rows(qkv_keep[0], qkv_send[0])
    qkv_other_sum = sum_rows(qkv_keep[1], qkv_send[1])
    grad_qkv = share_back(qkv_own_sum, qkv_other_sum)
    grad_qkv = grad_qkv.reshape(grad_qkv.shape[0], 3, share)

    kern_f = lax.psum(
        jnp.where(
            mp_at == 0,
            jnp.concatenate([first[4], second[4]], axis=1),
            jnp.concatenate([second[4], first[4]], axis=1),
        ),
        ("dp", "mp"),
    )
    kern_f = lax.dynamic_slice_in_dim(kern_f, mp_at * first[4].shape[1], first[4].shape[1], axis=1)
    kern_a = lax.psum(kern_a, ("dp", "mp"))

    grad_mod = jnp.concatenate(
        [sums_last[0:1], sums_last[1:2], sums_mid[0:1], sums_mid[1:2], sums_mid[2:3], sums_mid[3:4]],
        axis=0,
    )
    grad_mod_low = lax.all_gather(
        grad_mod.reshape(1, -1).astype(BF16), ("dp", "mp"), axis=0, tiled=True
    )
    rows = width // dp_size
    my_cols = lax.dynamic_slice_in_dim(silu_low, dp_at * rows, rows, axis=1)
    grad_w_mod = jnp.einsum("lk,lc->kc", my_cols, grad_mod_low, preferred_element_type=F32)
    grad_silu = jnp.einsum("lc,kc->lk", grad_mod_low, w_mod, preferred_element_type=F32)
    (grad_embedding,) = silu_pull(grad_silu)

    def table_grad(indices, count):
        onehot = (jnp.arange(count, dtype=jnp.int32)[:, None] == indices[None, :]).astype(F32)
        return jnp.dot(onehot, grad_embedding, precision=lax.Precision.HIGHEST)

    return (
        both(output, output_other),
        both(gtok, gtok_other),
        grad_w_mod,
        table_grad(steps, step_table.shape[0]),
        table_grad(labels, class_table.shape[0]),
        kern_a,
        grad_qkv,
        grad_out,
        kern_f,
        grad_up,
        grad_down,
    )


def solution(mesh):
    in_specs = (
        P("dp", None, None),
        P("dp", None),
        P(),
        P(),
        P(),
        P(),
        P(),
        P(),
        P(None, None, "mp"),
        P(None, "mp"),
        P(None, "mp"),
        P(None, "mp"),
        P(None, "mp"),
        P("dp", None, None),
    )
    out_specs = (
        P("dp", None, None),
        P("dp", None, None),
        P("dp", None),
        P(),
        P(),
        P(),
        P("dp", None, "mp"),
        P("dp", "mp"),
        P(None, "mp"),
        P("dp", "mp"),
        P("dp", "mp"),
    )
    return jax.shard_map(local, mesh=mesh, in_specs=in_specs, out_specs=out_specs, check_vma=False)
```

time: 1470 us -> 666 us (0.45)
  waiting for transfers between devices: 803 us -> 226 us
  other arithmetic: 316 us -> 17.7 us
  Pallas kernels: 0 us -> 213 us
  matrix products: 219 us -> 17.4 us
  blocking collectives: 0 us -> 111 us
  local copies, waits for them, and re-layouts: 114 us -> 22 us
  starting transfers between devices: 1.26 us -> 37.7 us
    psum x5 -> x1, waiting for transfers between devices: 466 us -> 0.01 us  [local(): lax.psum(jnp.where(mp_at == 0, jnp.concatenate([first[4], second[4]], axi...]
    reduce_scatter x5 -> x0, waiting for transfers between devices: 336 us -> none  [the longest x1 150 us: local(): lax.psum_scatter(part_mod, 'dp', scatter_dimension=0, tiled=True)]
    ppermute x0 -> x39, waiting for transfers between devices: none -> 226 us  [swap(): return lax.ppermute(values_in, axis, [(i, i ^ bit) for i in range(size)])]
    pallas_call x0 -> x8, Pallas kernels: none -> 213 us  [the longest x2 95.5 us: ffn_stage(): pl.pallas_call(ffn_kernel, out_shape=(keep, send, keep, send, jax.ShapeDt...]
    dot_general x31 -> x5, matrix products: 219 us -> 17.4 us  [the longest x2 5.95 us: table_grad(): return jnp.dot(onehot, grad_embedding, precision=lax.Precision.HIGHEST)]
    reduce_sum x15 -> x0, other arithmetic: 132 us -> none  [the longest x3 57.6 us: depthwise(): summed = summed + kernel[row_off * 3 + col_off] * window]
    all_gather x0 -> x1, blocking collectives: none -> 72.7 us  [local(): lax.all_gather(grad_mod.reshape(1, -1).astype(BF16), ('dp', 'mp'), axis=0...]
    psum x0 -> x1, blocking collectives: none -> 37.9 us  [local(): kern_a = lax.psum(kern_a, ('dp', 'mp'))]
  transfers between devices with their start and end apart: 10 -> 40, of which waited for: 9 -> 22; matrix products, arithmetic and copies ran while one was open for 14% -> 8% of each run, Pallas kernels for 0% -> 32%
where the time goes in v1:
time: 666 us; the launch traced here: 659 us
  waiting for transfers between devices  226 us (34%)
  Pallas kernels  213 us (32%)
  blocking collectives  111 us (17%)
  starting transfers between devices  37.7 us (6%)
  local copies, waits for them, and re-layouts  22 us (3%)
  other arithmetic  17.7 us (3%)
  matrix products  17.4 us (3%)
  between operations  15 us (2%)
    ppermute x39, waiting for transfers between devices, swap(): return lax.ppermute(values_in, axis, [(i, i ^ bit) for i in range(size)])  226 us
    pallas_call x2, Pallas kernels, ffn_stage(): pl.pallas_call(ffn_kernel, out_shape=(keep, send, keep, send, jax.ShapeDt...  95.5 us
    all_gather x1, blocking collectives, local(): lax.all_gather(grad_mod.reshape(1, -1).astype(BF16), ('dp', 'mp'), axis=0...  72.7 us
    psum x1, blocking collectives, local(): kern_a = lax.psum(kern_a, ('dp', 'mp'))  37.9 us
    ppermute x39, starting transfers between devices, swap(): return lax.ppermute(values_in, axis, [(i, i ^ bit) for i in range(size)])  37.7 us
    pallas_call x1, Pallas kernels, attend_stage(): pl.pallas_call(attend_kernel, out_shape=(jax.ShapeDtypeStruct((2, length,...  29.1 us
    pallas_call x1, Pallas kernels, last_stage(): pl.pallas_call(last_kernel, out_shape=(jax.ShapeDtypeStruct((length, widt...  24.3 us
    pallas_call x1, Pallas kernels, attend_back_stage(): pl.pallas_call(attend_back_kernel, out_shape=jax.ShapeDtypeStruct(qkv.sha...  22.4 us
  transfers between devices with their start and end apart: 40, of which 22 were waited for; matrix products, arithmetic and copies ran while one was open for 8% of the time, Pallas kernels for 32%

profile of v1, /device:TPU:0, one launch (start us, length us, event | category | flops | bytes accessed | tf_op | source)
XLA Modules:
  0.0 659.3 jit_solution(1954814304721510213)
XLA Ops:
  7.2 3.0 collective-permute-start
  10.3 1.9 collective-permute-start.1
  12.4 1.9 collective-permute-start.3
  14.3 10.3 %copy.32 = bf16[768,4608]{0,1:T(8,128)(2,1)} copy(bf16[768,4608]{1,0:T(8,128)(2,1)} %param.21) | data formatting | bytes 14155776 | tf_op args[4]
  25.3 2.2 gather_fusion.1
  27.7 4.9 fusion.44
  33.1 1.1 broadcast_in_dim_reshape.4.valid_ref
  35.4 11.6 %norm_conv.1 = (bf16[1024,768]{1,0:T(8,128)(2,1)}, bf16[1024,768]{1,0:T(8,128)(2,1)}, bf16[1024,768]{1,0:T(8,128)(2,1)}) custom-call(s32[2]{0:T(128)} %pad_add_fusion.idx, bf16[2,1024,768]{2,1,0:T(8,128)(2,1)} %tok_ref.1, bf16[2,1024,768]{2,1,0:T(8,128)(2,1)} %cot_ref.1, f32[6,768]{1,0:T(8,128)} %bitcast.208, bf16[9,768]{1,0:T(8,128)(2,1)} %kern_ref.5), custom_call_target="tpu_custom_call" | custom-call | flops 40000000 | bytes 8000000 | tf_op jit(solution)/shard_map/norm_conv/pallas_call | solution.py:177
  47.1 1.3 fusion.perm_ref
  48.4 15.2 %collective-permute-done.1.ob_ref = bf16[768,384]{1,0:T(8,128)(2,1)S(1)} collective-permute-done((bf16[768,384]{1,0:T(8,128)(2,1)}, bf16[768,384]{1,0:T(8,128)(2,1)S(1)}, u32[]{:S(2)}, u32[]{:S(2)}) %collective-permute-start.1) | collective-permute-done | bytes 589856 | tf_op jit(solution)/shard_map/ppermute | solution.py:742
  64.4 29.1 %attend.1 = (bf16[2,1024,1152]{2,1,0:T(8,128)(2,1)}, bf16[1024,768]{1,0:T(8,128)(2,1)}, f32[1024,768]{1,0:T(8,128)}, f32[1024,768]{1,0:T(8,128)}, bf16[1024,768]{1,0:T(8,128)(2,1)}, /*index=5*/bf16[1024,768]{1,0:T(8,128)(2,1)}) custom-call(bf16[1024,768]{1,0:T(8,128)(2,1)} %get-tuple-element.46.conv_ref, s32[4,256,1]{2,1,0:T(8,128)} %broadcast_in_dim_reshape.4.valid_ref, ...), custom_call_target="tpu_custom_call" | custom-call | flops 8000000000 | bytes 30000000 | tf_op jit(solution)/shard_map/attend/pallas_call | solution.py:250
  93.5 47.9 %ffn.2 = (f32[384,1536]{1,0:T(8,128)}, bf16[384,1536]{1,0:T(8,128)(2,1)}, f32[384,1536]{1,0:T(8,128)}, bf16[384,1536]{1,0:T(8,128)(2,1)}, f32[9,1536]{1,0:T(8,12...) custom-call(s32[2]{0:T(128)} %pad_add_fusion.idx, bf16[768,768]{1,0:T(8,128)(2,1)} %fusion.perm_ref, ...), custom_call_target="tpu_custom_call" | custom-call | flops 14495514624 | bytes 25165824 | tf_op jit(solution)/shard_map/ffn/pallas_call | solution.py:386
  142.0 21.9 %collective-permute-done.3.down_ref = bf16[768,1536]{1,0:T(8,128)(2,1)} collective-permute-done((bf16[768,1536]{1,0:T(8,128)(2,1)}, bf16[768,1536]{1,0:T(8,128)(2,1)}, u32[]{:S(2)}, u32[]{:S(2)}) %collective-permute-start.3) | collective-permute-done | bytes 2359328 | tf_op jit(solution)/shard_map/ppermute | solution.py:742
  164.0 47.6 %ffn.3 = (f32[384,1536]{1,0:T(8,128)}, bf16[384,1536]{1,0:T(8,128)(2,1)}, f32[384,1536]{1,0:T(8,128)}, bf16[384,1536]{1,0:T(8,128)(2,1)}, f32[9,1536]{1,0:T(8,12...) custom-call(s32[2]{0:T(128)} %pad_add_fusion.idx, bf16[768,768]{1,0:T(8,128)(2,1)} %fusion.perm_ref, ...), custom_call_target="tpu_custom_call" | custom-call | flops 14495514624 | bytes 25165824 | tf_op jit(solution)/shard_map/ffn/pallas_call | solution.py:386
  211.7 18.1 %middle.1 = (bf16[1024,768]{1,0:T(8,128)(2,1)}, f32[1024,768]{1,0:T(8,128)}, bf16[1024,768]{1,0:T(8,128)(2,1)}, f32[4,768]{1,0:T(4,128)}, f32[384,768]{1,0:T(8,128)}, /*index=5*/bf16[384,768]{1,0:T(8,128)(2,1)}) custom-call(s32[2]{0:T(128)} %pad_add_fusion.idx, bf16[768,768]{1,0:T(8,128)(2,1)} %fusion.perm_ref, f32[1024,768]{1,0:T(8,128)} %get-tuple-element.49.res_ref, ...), custom_call_target="tpu_custom_call" | custom-call | flops 4000000000 | bytes 32000000 | tf_op jit(solution)/shard_map/middle/pallas_call | solution.py:485
  229.8 22.4 %attend_back.1.gqkv_ref = bf16[2,1024,1152]{2,1,0:T(8,128)(2,1)} custom-call(bf16[2,1024,1152]{2,1,0:T(8,128)(2,1)} %get-tuple-element.59.qkv_ref, bf16[1024,768]{1,0:T(8,128)(2,1)} %get-tuple-element.60.gmix_ref, s32[4,256,1]{2,1,0:T(8,128)} %broadcast_in_dim_reshape.4.valid_ref), custom_call_target="tpu_custom_call" | custom-call | flops 12000000000 | bytes 12000000 | tf_op jit(solution)/shard_map/attend_back/pallas_call | solution.py:554
  252.2 11.4 %qkv_grad.1 = (f32[2,384,1152]{2,1,0:T(8,128)}, bf16[2,384,1152]{2,1,0:T(8,128)(2,1)}) custom-call(s32[2]{0:T(128)} %pad_add_fusion.idx, bf16[768,768]{1,0:T(8,128)(2,1)} %fusion.perm_ref, bf16[1024,768]{1,0:T(8,128)(2,1)} %get-tuple-element.46.conv_ref, bf16[2,1024,1152]{2,1,0:T(8,128)(2,1)} %attend_back.1.gqkv_ref), custom_call_target="tpu_custom_call" | custom-call | flops 4000000000 | bytes 14000000 | tf_op jit(solution)/shard_map/qkv_grad/pallas_call | solution.py:589
  263.6 24.3 %conv_norm_back.1 = (bf16[1024,768]{1,0:T(8,128)(2,1)}, f32[2,768]{1,0:T(2,128)}, f32[9,768]{1,0:T(8,128)}) custom-call(bf16[2,1024,1152]{2,1,0:T(8,128)(2,1)} %attend_back.1.gqkv_ref, bf16[3,768,384]{2,1,0:T(8,128)(2,1)} %bitcast.215, bf16[3,768,384]{2,1,0:T(8,128)(2,1)} %collective-permute-done.wb_ref, bf16[1024,768]{1,0:T(8,128)(2,1)} %get-tuple-element.47.tok_ref, ...), custom_call_target="tpu_custom_call" | custom-call | flops 4000000000 | bytes 16000000 | tf_op jit(solution)/shard_map/conv_norm_back/pallas_call | solution.py:712
  289.4 72.7 %all-gather = bf16[32,1,4608]{2,1,0:T(2,128)(2,1)S(1)} all-gather(bf16[1,1,4608]{2,1,0:T(2,128)(2,1)S(1)} %reshape.184), channel_id=1, replica_groups=mesh['dp'=16,'mp'=2] {'dp','mp'}, dimensions={0}, use_global_device_ids=true | all-gather | bytes 304128 | tf_op jit(solution)/shard_map/all_gather | solution.py:881
  362.2 5.3 fusion.38
  367.6 1.4 slice_bitcast_fusion.1
  368.9 3.0 fusion.6
  371.9 3.0 fusion.5
  375.4 1.3 fusion.16
  376.7 37.9 %psum.14 = f32[9,768]{1,0:T(8,128)} all-reduce(f32[9,768]{1,0:T(8,128)S(1)} %copy-done.15), channel_id=1, replica_groups=mesh['dp'=16,'mp'=2] {'dp','mp'}, use_global_device_ids=true, to_apply=%region_0.2 | all-reduce | flops 6912 | bytes 55296 | tf_op jit(solution)/shard_map/psum | solution.py:875
  414.6 1.5 constant_dynamic-slice_fusion
  418.1 1.8 convert_add_fusion.3
  419.9 2.3 collective-permute-start.17
  422.2 1.7 convert_add_fusion.1
  424.1 5.8 collective-permute-done.17
  429.9 1.7 collective-permute-start.6
  432.1 3.0 collective-permute-start.18
  435.3 6.2 collective-permute-done.18
  441.8 4.3 collective-permute-done.19
  446.1 1.6 collective-permute-start.20
  447.7 52.9 %collective-permute-done.20 = bf16[48,384]{1,0:T(8,128)(2,1)S(1)} collective-permute-done((bf16[48,384]{1,0:T(8,128)(2,1)S(1)}, bf16[48,384]{1,0:T(8,128)(2,1)S(1)}, u32[]{:S(2)}, u32[]{:S(2)}) %collective-permute-start.20) | collective-permute-done | bytes 36896 | tf_op jit(solution)/shard_map/ppermute | solution.py:742
  500.6 1.5 collective-permute-start.22
  503.6 13.3 %collective-permute-done.22 = bf16[192,1536]{1,0:T(8,128)(2,1)S(1)} collective-permute-done((bf16[192,1536]{1,0:T(8,128)(2,1)S(1)}, bf16[192,1536]{1,0:T(8,128)(2,1)S(1)}, u32[]{:S(2)}, u32[]{:S(2)}) %collective-permute-start.22) | collective-permute-done | bytes 589856 | tf_op jit(solution)/shard_map/ppermute | solution.py:742
  516.9 1.5 collective-permute-start.8
  518.7 10.8 %collective-permute-done.31 = bf16[192,1536]{1,0:T(8,128)(2,1)S(1)} collective-permute-done((bf16[192,1536]{1,0:T(8,128)(2,1)S(1)}, bf16[192,1536]{1,0:T(8,128)(2,1)S(1)}, u32[]{:S(2)}, u32[]{:S(2)}) %collective-permute-start.31) | collective-permute-done | bytes 589856 | tf_op jit(solution)/shard_map/ppermute | solution.py:742
  529.5 1.5 collective-permute-start.12
  531.7 1.6 convert_add_fusion
  533.5 5.5 collective-permute-done.8
  539.0 1.5 collective-permute-start.35
  540.6 7.9 %collective-permute-done.12 = bf16[192,1152]{1,0:T(8,128)(2,1)S(1)} collective-permute-done((bf16[192,1152]{1,0:T(8,128)(2,1)S(1)}, bf16[192,1152]{1,0:T(8,128)(2,1)S(1)}, u32[]{:S(2)}, u32[]{:S(2)}) %collective-permute-start.12) | collective-permute-done | bytes 442400 | tf_op jit(solution)/shard_map/ppermute | solution.py:742
  548.5 3.0 collective-permute-start.23
  551.6 9.5 %collective-permute-done.23 = bf16[96,1536]{1,0:T(8,128)(2,1)S(1)} collective-permute-done((bf16[96,1536]{1,0:T(8,128)(2,1)S(1)}, bf16[96,1536]{1,0:T(8,128)(2,1)S(1)}, u32[]{:S(2)}, u32[]{:S(2)}) %collective-permute-start.23) | collective-permute-done | bytes 294944 | tf_op jit(solution)/shard_map/ppermute | solution.py:742
  561.2 13.6 %collective-permute-done.32 = bf16[96,1536]{1,0:T(8,128)(2,1)S(1)} collective-permute-done((bf16[96,1536]{1,0:T(8,128)(2,1)S(1)}, bf16[96,1536]{1,0:T(8,128)(2,1)S(1)}, u32[]{:S(2)}, u32[]{:S(2)}) %collective-permute-start.32) | collective-permute-done | bytes 294944 | tf_op jit(solution)/shard_map/ppermute | solution.py:742
  574.9 11.8 %collective-permute-done.9 = bf16[96,1152]{1,0:T(8,128)(2,1)S(1)} collective-permute-done((bf16[96,1152]{1,0:T(8,128)(2,1)S(1)}, bf16[96,1152]{1,0:T(8,128)(2,1)S(1)}, u32[]{:S(2)}, u32[]{:S(2)}) %collective-permute-start.9) | collective-permute-done | bytes 221216 | tf_op jit(solution)/shard_map/ppermute | solution.py:742
  586.8 12.6 %collective-permute-done.13 = bf16[96,1152]{1,0:T(8,128)(2,1)S(1)} collective-permute-done((bf16[96,1152]{1,0:T(8,128)(2,1)S(1)}, bf16[96,1152]{1,0:T(8,128)(2,1)S(1)}, u32[]{:S(2)}, u32[]{:S(2)}) %collective-permute-start.13) | collective-permute-done | bytes 221216 | tf_op jit(solution)/shard_map/ppermute | solution.py:742
  599.4 2.1 collective-permute-start.33
  601.8 2.3 reverse_select_fusion
  604.4 2.3 reverse_select_fusion.1
  606.7 4.0 collective-permute-done.14
  611.2 3.1 collective-permute-start.27
  614.6 1.8 collective-permute-done.10
  617.5 16.7 %collective-permute-done.27 = bf16[96,1536]{1,0:T(8,128)(2,1)S(1)} collective-permute-done((bf16[96,1536]{1,0:T(8,128)(2,1)S(1)}, bf16[96,1536]{1,0:T(8,128)(2,1)S(1)}, u32[]{:S(2)}, u32[]{:S(2)}) %collective-permute-start.27) | collective-permute-done | bytes 294944 | tf_op jit(solution)/shard_map/ppermute | solution.py:742
  634.4 5.0 collective-permute-done.36
  639.6 3.0 collective-permute-done.28
  642.6 1.8 collective-permute-start.29
  644.4 1.2 collective-permute-done.37
  645.7 1.8 collective-permute-start.38
  647.4 1.5 collective-permute-done.29
  649.7 1.8 collective-permute-done.38
  (153 shorter events, 16.6 us)
Async XLA Ops:
  7.2 17.5 %copy-start = (bf16[1000,768]{1,0:T(8,128)(2,1)S(1)}, bf16[1000,768]{1,0:T(8,128)(2,1)}, u32[]{:S(2)}) copy-start(bf16[1000,768]{1,0:T(8,128)(2,1)} %param.22) | copy-start | bytes 4608004
  7.2 407.4 %all-reduce.2.cloned.1.call-start = ((), (), s32[]{:S(2)}) async-start(), calls=%async_computation | async-start | bytes 393216 | tf_op jit(solution)/shard_map/psum | solution.py:866
  7.2 56.4 %collective-permute-start = (bf16[3,768,384]{2,1,0:T(8,128)(2,1)}, bf16[3,768,384]{2,1,0:T(8,128)(2,1)}, u32[]{:S(2)}, u32[]{:S(2)}) collective-permute-start(bf16[3,768,384]{2,1,0:T(8,128)(2,1)} %bitcast.213), channel_id=1, source_target_pairs={{0,1},{1,0},{2,3},{3,2},{4,5},{5,4},{6,7},{7,6},{8,9},{9,8},{10,11... | collective-permute-start | bytes 5308424 | tf_op jit(solution)/shard_map/ppermute | solution.py:742
  10.2 131.8 %collective-permute-start.4 = (bf16[9,1536]{1,0:T(8,128)(2,1)}, bf16[9,1536]{1,0:T(8,128)(2,1)S(1)}, u32[]{:S(2)}, u32[]{:S(2)}) collective-permute-start(bf16[9,1536]{1,0:T(8,128)(2,1)} %kern_ref.4), channel_id=1, source_target_pairs={{0,1},{1,0},{2,3},{3,2},{4,5},{5,4},{6,7},{7,6},{8,9},{9,8},{10,11... | collective-permute-start | bytes 82952 | tf_op jit(solution)/shard_map/ppermute | solution.py:742
  10.3 53.3 %collective-permute-start.1 = (bf16[768,384]{1,0:T(8,128)(2,1)}, bf16[768,384]{1,0:T(8,128)(2,1)S(1)}, u32[]{:S(2)}, u32[]{:S(2)}) collective-permute-start(bf16[768,384]{1,0:T(8,128)(2,1)} %oa_ref.3), channel_id=1, source_target_pairs={{0,1},{1,0},{2,3},{3,2},{4,5},{5,4},{6,7},{7,6},{8,9},{9,8},{10,11... | collective-permute-start | bytes 1769480 | tf_op jit(solution)/shard_map/ppermute | solution.py:742
  12.3 129.8 %collective-permute-start.2 = (bf16[768,1536]{1,0:T(8,128)(2,1)}, bf16[768,1536]{1,0:T(8,128)(2,1)}, u32[]{:S(2)}, u32[]{:S(2)}) collective-permute-start(bf16[768,1536]{1,0:T(8,128)(2,1)} %up_ref.1), channel_id=1, source_target_pairs={{0,1},{1,0},{2,3},{3,2},{4,5},{5,4},{6,7},{7,6},{8,9},{9,8},{10,11... | collective-permute-start | bytes 7077896 | tf_op jit(solution)/shard_map/ppermute | solution.py:742
  12.4 151.6 %collective-permute-start.3 = (bf16[768,1536]{1,0:T(8,128)(2,1)}, bf16[768,1536]{1,0:T(8,128)(2,1)}, u32[]{:S(2)}, u32[]{:S(2)}) collective-permute-start(bf16[768,1536]{1,0:T(8,128)(2,1)} %down_ref.1), channel_id=1, source_target_pairs={{0,1},{1,0},{2,3},{3,2},{4,5},{5,4},{6,7},{7,6},{8,9},{9,8},{10,11... | collective-permute-start | bytes 7077896 | tf_op jit(solution)/shard_map/ppermute | solution.py:742
  14.3 10.3 %copy-start.17 = (s32[32]{0:T(128)S(1)}, s32[32]{0:T(128)}, u32[]{:S(2)}) copy-start(s32[32]{0:T(128)} %param.20) | copy-start | bytes 388
  14.3 10.3 %copy-start.18 = (s32[32]{0:T(128)S(1)}, s32[32]{0:T(128)}, u32[]{:S(2)}) copy-start(s32[32]{0:T(128)} %param.19) | copy-start | bytes 388
  27.7 5.0 copy-start.20
  35.4 11.6 %copy-start.19 = (s32[768]{0:T(1024)S(1)}, s32[768]{0:T(1024)}, u32[]{:S(2)}) copy-start(s32[768]{0:T(1024)} %constant.271.clone) | copy-start | bytes 9220
  63.6 0.8 copy-start.12
  141.4 274.9 %collective-permute-start.21 = (bf16[384,1536]{1,0:T(8,128)(2,1)}, bf16[384,1536]{1,0:T(8,128)(2,1)}, u32[]{:S(2)}, u32[]{:S(2)}) collective-permute-start(bf16[384,1536]{1,0:T(8,128)(2,1)} %get-tuple-element.73), channel_id=1, source_target_pairs={{0,2},{2,0},{4,6},{6,4},{8,10},{10,8},{12,14},{14,12},{16,18},{18,... | collective-permute-start | bytes 3538952 | tf_op jit(solution)/shard_map/ppermute | solution.py:742
  141.5 278.3 %collective-permute-start.30 = (bf16[384,1536]{1,0:T(8,128)(2,1)}, bf16[384,1536]{1,0:T(8,128)(2,1)}, u32[]{:S(2)}, u32[]{:S(2)}) collective-permute-start(bf16[384,1536]{1,0:T(8,128)(2,1)} %get-tuple-element.77), channel_id=1, source_target_pairs={{0,2},{2,0},{4,6},{6,4},{8,10},{10,8},{12,14},{14,12},{16,18},{18,... | collective-permute-start | bytes 3538952 | tf_op jit(solution)/shard_map/ppermute | solution.py:742
  142.0 22.0 %copy-start.21 = (bf16[9,1536]{1,0:T(8,128)(2,1)}, bf16[9,1536]{1,0:T(8,128)(2,1)S(1)}, u32[]{:S(2)}) copy-start(bf16[9,1536]{1,0:T(8,128)(2,1)S(1)} %collective-permute-done.4.kern_ref) | copy-start | bytes 82948
  211.6 291.2 %collective-permute-start.25 = (bf16[384,1536]{1,0:T(8,128)(2,1)}, bf16[384,1536]{1,0:T(8,128)(2,1)S(1)}, u32[]{:S(2)}, u32[]{:S(2)}) collective-permute-start(bf16[384,1536]{1,0:T(8,128)(2,1)} %get-tuple-element.75), channel_id=1, source_target_pairs={{0,2},{2,0},{4,6},{6,4},{8,10},{10,8},{12,14},{14,12},{16,18},{18,... | collective-permute-start | bytes 3538952 | tf_op jit(solution)/shard_map/ppermute | solution.py:742
  263.6 25.1 %copy-start.16 = (f32[4,768]{1,0:T(4,128)S(1)}, f32[4,768]{1,0:T(4,128)}, u32[]{:S(2)}) copy-start(f32[4,768]{1,0:T(4,128)} %get-tuple-element.64) | copy-start | bytes 36868
  263.6 25.1 %copy-start.13 = (f32[9,1536]{1,0:T(8,128)S(1)}, f32[9,1536]{1,0:T(8,128)}, u32[]{:S(2)}) copy-start(f32[9,1536]{1,0:T(8,128)} %get-tuple-element.70) | copy-start | bytes 165892
  263.6 25.1 %copy-start.14 = (f32[9,1536]{1,0:T(8,128)S(1)}, f32[9,1536]{1,0:T(8,128)}, u32[]{:S(2)}) copy-start(f32[9,1536]{1,0:T(8,128)} %get-tuple-element.71) | copy-start | bytes 165892
  362.2 5.4 copy-start.7
  367.5 48.7 %collective-permute-start.16 = (bf16[384,768]{1,0:T(8,128)(2,1)}, bf16[384,768]{1,0:T(8,128)(2,1)S(1)}, u32[]{:S(2)}, u32[]{:S(2)}) collective-permute-start(bf16[384,768]{1,0:T(8,128)(2,1)} %get-tuple-element.69), channel_id=1, source_target_pairs={{0,2},{2,0},{4,6},{6,4},{8,10},{10,8},{12,14},{14,12},{16,18},{18,... | collective-permute-start | bytes 1769480 | tf_op jit(solution)/shard_map/ppermute | solution.py:742
  371.9 4.8 copy-start.15
  371.9 44.2 %copy-start.10 = (f32[384,768]{1,0:T(8,128)S(1)}, f32[384,768]{1,0:T(8,128)}, u32[]{:S(2)}) copy-start(f32[384,768]{1,0:T(8,128)} %get-tuple-element.68) | copy-start | bytes 3538948
  374.9 156.3 %collective-permute-start.34 = (bf16[384,1536]{1,0:T(8,128)(2,1)}, bf16[384,1536]{1,0:T(8,128)(2,1)}, u32[]{:S(2)}, u32[]{:S(2)}) collective-permute-start(bf16[384,1536]{1,0:T(8,128)(2,1)} %get-tuple-element.79), channel_id=1, source_target_pairs={{0,2},{2,0},{4,6},{6,4},{8,10},{10,8},{12,14},{14,12},{16,18},{18,... | collective-permute-start | bytes 3538952 | tf_op jit(solution)/shard_map/ppermute | solution.py:742
  416.1 15.6 %collective-permute-start.7 = (bf16[384,1152]{1,0:T(8,128)(2,1)}, bf16[384,1152]{1,0:T(8,128)(2,1)S(1)}, u32[]{:S(2)}, u32[]{:S(2)}) collective-permute-start(bf16[384,1152]{1,0:T(8,128)(2,1)} %get-tuple-element.104), channel_id=1, source_target_pairs={{0,2},{2,0},{4,6},{6,4},{8,10},{10,8},{12,14},{14,12},{16,18},{18,... | collective-permute-start | bytes 2654216 | tf_op jit(solution)/shard_map/ppermute | solution.py:742
  416.1 1.2 copy-start.11
  416.1 1.9 copy-start.6
  417.3 14.8 %collective-permute-start.11 = (bf16[384,1152]{1,0:T(8,128)(2,1)S(1)}, bf16[384,1152]{1,0:T(8,128)(2,1)S(1)}, u32[]{:S(2)}, u32[]{:S(2)}) collective-permute-start(bf16[384,1152]{1,0:T(8,128)(2,1)S(1)} %copy-done.11), channel_id=1, source_target_pairs={{0,2},{2,0},{4,6},{6,4},{8,10},{10,8},{12,14},{14,12},{16,18},{18,... | collective-permute-start | bytes 2654216 | tf_op jit(solution)/shard_map/ppermute | solution.py:742
  418.1 4.1 copy-start.5
  419.9 10.0 %collective-permute-start.17 = (bf16[192,768]{1,0:T(8,128)(2,1)S(1)}, bf16[192,768]{1,0:T(8,128)(2,1)S(1)}, u32[]{:S(2)}, u32[]{:S(2)}) collective-permute-start(bf16[192,768]{1,0:T(8,128)(2,1)S(1)} %fusion.9), channel_id=1, source_target_pairs={{0,4},{2,6},{4,0},{6,2},{8,12},{10,14},{12,8},{14,10},{16,20},{18,... | collective-permute-start | bytes 884744 | tf_op jit(solution)/shard_map/ppermute | solution.py:742
  422.2 7.7 %copy-start.9 = (bf16[1024,768]{1,0:T(8,128)(2,1)S(1)}, bf16[1024,768]{1,0:T(8,128)(2,1)}, u32[]{:S(2)}) copy-start(bf16[1024,768]{1,0:T(8,128)(2,1)} %get-tuple-element.62) | copy-start | bytes 4718596
  422.2 9.5 %copy-start.8 = (bf16[1024,768]{1,0:T(8,128)(2,1)S(1)}, bf16[1024,768]{1,0:T(8,128)(2,1)}, u32[]{:S(2)}) copy-start(bf16[1024,768]{1,0:T(8,128)(2,1)} %get-tuple-element.58) | copy-start | bytes 4718596
  424.0 11.1 %copy-start.2 = (f32[2,384,1152]{2,1,0:T(8,128)S(1)}, f32[2,384,1152]{2,1,0:T(8,128)}, u32[]{:S(2)}) copy-start(f32[2,384,1152]{2,1,0:T(8,128)} %get-tuple-element.66) | copy-start | bytes 10616836
  429.9 169.6 %collective-permute-start.6 = (bf16[1024,768]{1,0:T(8,128)(2,1)S(1)}, bf16[1024,768]{1,0:T(8,128)(2,1)S(1)}, u32[]{:S(2)}, u32[]{:S(2)}) collective-permute-start(bf16[1024,768]{1,0:T(8,128)(2,1)S(1)} %copy-done.9), channel_id=1, source_target_pairs={{0,1},{1,0},{2,3},{3,2},{4,5},{5,4},{6,7},{7,6},{8,9},{9,8},{10,11... | collective-permute-start | bytes 4718600 | tf_op jit(solution)/shard_map/ppermute | solution.py:742
  431.7 172.4 %collective-permute-start.5 = (bf16[1024,768]{1,0:T(8,128)(2,1)S(1)}, bf16[1024,768]{1,0:T(8,128)(2,1)S(1)}, u32[]{:S(2)}, u32[]{:S(2)}) collective-permute-start(bf16[1024,768]{1,0:T(8,128)(2,1)S(1)} %copy-done.8), channel_id=1, source_target_pairs={{0,1},{1,0},{2,3},{3,2},{4,5},{5,4},{6,7},{7,6},{8,9},{9,8},{10,11... | collective-permute-start | bytes 4718600 | tf_op jit(solution)/shard_map/ppermute | solution.py:742
  432.1 9.5 %collective-permute-start.18 = (bf16[96,768]{1,0:T(8,128)(2,1)S(1)}, bf16[96,768]{1,0:T(8,128)(2,1)S(1)}, u32[]{:S(2)}, u32[]{:S(2)}) collective-permute-start(bf16[96,768]{1,0:T(8,128)(2,1)S(1)} %fusion.28), channel_id=1, source_target_pairs={{0,16},{2,18},{4,20},{6,22},{8,24},{10,26},{12,28},{14,30},{16,0},... | collective-permute-start | bytes 442376 | tf_op jit(solution)/shard_map/ppermute | solution.py:742
  435.3 67.9 %copy-start.4 = (f32[384,1536]{1,0:T(8,128)S(1)}, f32[384,1536]{1,0:T(8,128)}, u32[]{:S(2)}) copy-start(f32[384,1536]{1,0:T(8,128)} %get-tuple-element.74) | copy-start | bytes 7077892
  441.6 4.4 collective-permute-start.19
  446.1 54.5 %collective-permute-start.20 = (bf16[48,384]{1,0:T(8,128)(2,1)S(1)}, bf16[48,384]{1,0:T(8,128)(2,1)S(1)}, u32[]{:S(2)}, u32[]{:S(2)}) collective-permute-start(bf16[48,384]{1,0:T(8,128)(2,1)S(1)} %slice.45), channel_id=1, source_target_pairs={{0,1},{1,0},{2,3},{3,2},{4,5},{5,4},{6,7},{7,6},{8,9},{9,8},{10,11... | collective-permute-start | bytes 110600 | tf_op jit(solution)/shard_map/ppermute | solution.py:742
  500.6 16.3 %collective-permute-start.22 = (bf16[192,1536]{1,0:T(8,128)(2,1)S(1)}, bf16[192,1536]{1,0:T(8,128)(2,1)S(1)}, u32[]{:S(2)}, u32[]{:S(2)}) collective-permute-start(bf16[192,1536]{1,0:T(8,128)(2,1)S(1)} %fusion.1), channel_id=1, source_target_pairs={{0,4},{2,6},{4,0},{6,2},{8,12},{10,14},{12,8},{14,10},{16,20},{18,... | collective-permute-start | bytes 1769480 | tf_op jit(solution)/shard_map/ppermute | solution.py:742
  502.8 26.7 %collective-permute-start.31 = (bf16[192,1536]{1,0:T(8,128)(2,1)S(1)}, bf16[192,1536]{1,0:T(8,128)(2,1)S(1)}, u32[]{:S(2)}, u32[]{:S(2)}) collective-permute-start(bf16[192,1536]{1,0:T(8,128)(2,1)S(1)} %fusion.3), channel_id=1, source_target_pairs={{0,4},{2,6},{4,0},{6,2},{8,12},{10,14},{12,8},{14,10},{16,20},{18,... | collective-permute-start | bytes 1769480 | tf_op jit(solution)/shard_map/ppermute | solution.py:742
  516.9 22.1 %collective-permute-start.8 = (bf16[192,1152]{1,0:T(8,128)(2,1)S(1)}, bf16[192,1152]{1,0:T(8,128)(2,1)S(1)}, u32[]{:S(2)}, u32[]{:S(2)}) collective-permute-start(bf16[192,1152]{1,0:T(8,128)(2,1)S(1)} %fusion.7), channel_id=1, source_target_pairs={{0,4},{2,6},{4,0},{6,2},{8,12},{10,14},{12,8},{14,10},{16,20},{18,... | collective-permute-start | bytes 1327112 | tf_op jit(solution)/shard_map/ppermute | solution.py:742
  518.7 13.1 %copy-start.3 = (f32[384,1536]{1,0:T(8,128)S(1)}, f32[384,1536]{1,0:T(8,128)}, u32[]{:S(2)}) copy-start(f32[384,1536]{1,0:T(8,128)} %get-tuple-element.78) | copy-start | bytes 7077892
  529.5 19.0 %collective-permute-start.12 = (bf16[192,1152]{1,0:T(8,128)(2,1)S(1)}, bf16[192,1152]{1,0:T(8,128)(2,1)S(1)}, u32[]{:S(2)}, u32[]{:S(2)}) collective-permute-start(bf16[192,1152]{1,0:T(8,128)(2,1)S(1)} %fusion.8), channel_id=1, source_target_pairs={{0,4},{2,6},{4,0},{6,2},{8,12},{10,14},{12,8},{14,10},{16,20},{18,... | collective-permute-start | bytes 1327112 | tf_op jit(solution)/shard_map/ppermute | solution.py:742
  531.2 79.8 %collective-permute-start.26 = (bf16[192,1536]{1,0:T(8,128)(2,1)S(1)}, bf16[192,1536]{1,0:T(8,128)(2,1)S(1)}, u32[]{:S(2)}, u32[]{:S(2)}) collective-permute-start(bf16[192,1536]{1,0:T(8,128)(2,1)S(1)} %fusion.2), channel_id=1, source_target_pairs={{0,4},{2,6},{4,0},{6,2},{8,12},{10,14},{12,8},{14,10},{16,20},{18,... | collective-permute-start | bytes 1769480 | tf_op jit(solution)/shard_map/ppermute | solution.py:742
  539.0 72.3 %collective-permute-start.35 = (bf16[192,1536]{1,0:T(8,128)(2,1)S(1)}, bf16[192,1536]{1,0:T(8,128)(2,1)S(1)}, u32[]{:S(2)}, u32[]{:S(2)}) collective-permute-start(bf16[192,1536]{1,0:T(8,128)(2,1)S(1)} %fusion.4), channel_id=1, source_target_pairs={{0,4},{2,6},{4,0},{6,2},{8,12},{10,14},{12,8},{14,10},{16,20},{18,... | collective-permute-start | bytes 1769480 | tf_op jit(solution)/shard_map/ppermute | solution.py:742
  548.5 12.6 %collective-permute-start.23 = (bf16[96,1536]{1,0:T(8,128)(2,1)S(1)}, bf16[96,1536]{1,0:T(8,128)(2,1)S(1)}, u32[]{:S(2)}, u32[]{:S(2)}) collective-permute-start(bf16[96,1536]{1,0:T(8,128)(2,1)S(1)} %fusion.10), channel_id=1, source_target_pairs={{0,16},{2,18},{4,20},{6,22},{8,24},{10,26},{12,28},{14,30},{16,0},... | collective-permute-start | bytes 884744 | tf_op jit(solution)/shard_map/ppermute | solution.py:742
  561.1 13.8 %collective-permute-start.32 = (bf16[96,1536]{1,0:T(8,128)(2,1)S(1)}, bf16[96,1536]{1,0:T(8,128)(2,1)S(1)}, u32[]{:S(2)}, u32[]{:S(2)}) collective-permute-start(bf16[96,1536]{1,0:T(8,128)(2,1)S(1)} %fusion.12), channel_id=1, source_target_pairs={{0,16},{2,18},{4,20},{6,22},{8,24},{10,26},{12,28},{14,30},{16,0},... | collective-permute-start | bytes 884744 | tf_op jit(solution)/shard_map/ppermute | solution.py:742
  574.8 11.9 %collective-permute-start.9 = (bf16[96,1152]{1,0:T(8,128)(2,1)S(1)}, bf16[96,1152]{1,0:T(8,128)(2,1)S(1)}, u32[]{:S(2)}, u32[]{:S(2)}) collective-permute-start(bf16[96,1152]{1,0:T(8,128)(2,1)S(1)} %fusion.24), channel_id=1, source_target_pairs={{0,16},{2,18},{4,20},{6,22},{8,24},{10,26},{12,28},{14,30},{16,0},... | collective-permute-start | bytes 663560 | tf_op jit(solution)/shard_map/ppermute | solution.py:742
  586.7 12.6 %collective-permute-start.13 = (bf16[96,1152]{1,0:T(8,128)(2,1)S(1)}, bf16[96,1152]{1,0:T(8,128)(2,1)S(1)}, u32[]{:S(2)}, u32[]{:S(2)}) collective-permute-start(bf16[96,1152]{1,0:T(8,128)(2,1)S(1)} %fusion.25), channel_id=1, source_target_pairs={{0,16},{2,18},{4,20},{6,22},{8,24},{10,26},{12,28},{14,30},{16,0},... | collective-permute-start | bytes 663560 | tf_op jit(solution)/shard_map/ppermute | solution.py:742
  599.4 48.1 %collective-permute-start.24 = (bf16[48,1536]{1,0:T(8,128)(2,1)S(1)}, bf16[48,1536]{1,0:T(8,128)(2,1)S(1)}, u32[]{:S(2)}, u32[]{:S(2)}) collective-permute-start(bf16[48,1536]{1,0:T(8,128)(2,1)S(1)} %fusion.29), channel_id=1, source_target_pairs={{0,8},{2,10},{4,12},{6,14},{8,0},{10,2},{12,4},{14,6},{16,24},{18,... | collective-permute-start | bytes 442376 | tf_op jit(solution)/shard_map/ppermute | solution.py:742
  599.4 50.2 %collective-permute-start.33 = (bf16[48,1536]{1,0:T(8,128)(2,1)S(1)}, bf16[48,1536]{1,0:T(8,128)(2,1)S(1)}, u32[]{:S(2)}, u32[]{:S(2)}) collective-permute-start(bf16[48,1536]{1,0:T(8,128)(2,1)S(1)} %fusion.31), channel_id=1, source_target_pairs={{0,8},{2,10},{4,12},{6,14},{8,0},{10,2},{12,4},{14,6},{16,24},{18,... | collective-permute-start | bytes 442376 | tf_op jit(solution)/shard_map/ppermute | solution.py:742
  604.1 6.6 collective-permute-start.14
  610.7 5.7 collective-permute-start.10
  611.0 5.8 collective-permute-start.15
  611.2 23.0 %collective-permute-start.27 = (bf16[96,1536]{1,0:T(8,128)(2,1)S(1)}, bf16[96,1536]{1,0:T(8,128)(2,1)S(1)}, u32[]{:S(2)}, u32[]{:S(2)}) collective-permute-start(bf16[96,1536]{1,0:T(8,128)(2,1)S(1)} %fusion.11), channel_id=1, source_target_pairs={{0,16},{2,18},{4,20},{6,22},{8,24},{10,26},{12,28},{14,30},{16,0},... | collective-permute-start | bytes 884744 | tf_op jit(solution)/shard_map/ppermute | solution.py:742
  616.4 23.0 %collective-permute-start.36 = (bf16[96,1536]{1,0:T(8,128)(2,1)S(1)}, bf16[96,1536]{1,0:T(8,128)(2,1)S(1)}, u32[]{:S(2)}, u32[]{:S(2)}) collective-permute-start(bf16[96,1536]{1,0:T(8,128)(2,1)S(1)} %fusion.13), channel_id=1, source_target_pairs={{0,16},{2,18},{4,20},{6,22},{8,24},{10,26},{12,28},{14,30},{16,0},... | collective-permute-start | bytes 884744 | tf_op jit(solution)/shard_map/ppermute | solution.py:742
  634.3 8.2 %collective-permute-start.28 = (bf16[48,1536]{1,0:T(8,128)(2,1)S(1)}, bf16[48,1536]{1,0:T(8,128)(2,1)S(1)}, u32[]{:S(2)}, u32[]{:S(2)}) collective-permute-start(bf16[48,1536]{1,0:T(8,128)(2,1)S(1)} %fusion.30), channel_id=1, source_target_pairs={{0,8},{2,10},{4,12},{6,14},{8,0},{10,2},{12,4},{14,6},{16,24},{18,... | collective-permute-start | bytes 442376 | tf_op jit(solution)/shard_map/ppermute | solution.py:742
  639.4 12.8 %copy-start.1 = (bf16[1000,768]{1,0:T(8,128)(2,1)S(1)}, bf16[1000,768]{1,0:T(8,128)(2,1)}, u32[]{:S(2)}) copy-start(bf16[1000,768]{1,0:T(8,128)(2,1)} %param.22) | copy-start | bytes 4608004
  639.5 6.1 collective-permute-start.37
  642.6 6.3 collective-permute-start.29
  645.7 5.8 collective-permute-start.38
Sparse Core Ops, SparseCore 0:
  289.6 124.6 all-reduce.1

commit v2 on v1

v2 whole, which is shorter than its diff:
```python
from functools import partial

import jax
import jax.numpy as jnp
from jax import lax
from jax.experimental import pallas as pl
from jax.experimental.pallas import tpu as pltpu
from jax.sharding import PartitionSpec as P

SIDE = 32
HALF = SIDE // 2
HEAD_DIM = 64
GROUPS = 4
LANES = 128
TILE = 256
EPS = 1e-06
PITCH = HALF + 8
GROUP_ROWS = (HALF + 2) * PITCH + 8
PAD_ROWS = GROUPS * GROUP_ROWS
GELU_A = 0.7978845608028654
GELU_B = 0.044715
F32 = jnp.float32
BF16 = jnp.bfloat16
VMEM_BYTES = 60 * 1024 * 1024
SMALL_COST = pl.CostEstimate(flops=1000, bytes_accessed=1000, transcendentals=0)


def params(count=1):
    return pltpu.CompilerParams(
        dimension_semantics=("arbitrary",) * count, vmem_limit_bytes=VMEM_BYTES
    )


def whole(shape):
    zeros = (0,) * len(shape)
    return pl.BlockSpec(shape, lambda *_: zeros, pipeline_mode=pl.Buffered(1))


def leading(array, count):
    tail = array.shape[1:]
    return pl.BlockSpec((count,) + tail, lambda *_: (0,) * array.ndim, pipeline_mode=pl.Buffered(1))


def entry(array, which):
    tail = (0,) * (array.ndim - 1)
    return pl.BlockSpec(
        (None,) + array.shape[1:], lambda *_: (which,) + tail, pipeline_mode=pl.Buffered(1)
    )


def dot(left, right):
    return jnp.dot(left, right, preferred_element_type=F32)


def dot_nt(left, right):
    return lax.dot_general(left, right, (((1,), (1,)), ((), ())), preferred_element_type=F32)


def pad_row(group, row, shift=0):
    return group * GROUP_ROWS + (row + 1) * PITCH + 8 + shift


AROUND = ((1, -1), (0, 0), (1, 0), (0, 1))


def neighbours(grid_ref, lane_block, row):
    found = []
    for row_par, row_off in AROUND:
        line = []
        for col_par, col_off in AROUND:
            const = pad_row(row_par * 2 + col_par, row_off, col_off)
            line.append(grid_ref[lane_block, pl.ds(row * PITCH + const, HALF), :])
        found.append(line)
    return found


def taps_of(kern_ref, lanes):
    return [
        jnp.broadcast_to(kern_ref[tap : tap + 1, lanes].astype(F32), (HALF, LANES))
        for tap in range(9)
    ]


def conv_at(found, taps, row_par, col_par):
    total = None
    for row_off in range(3):
        for col_off in range(3):
            term = taps[row_off * 3 + col_off] * found[row_par + row_off][col_par + col_off]
            total = term if total is None else total + term
    return total


def conv_back_at(found, taps, sums, source, row_par, col_par):
    total = None
    sums = list(sums)
    for row_off in range(3):
        for col_off in range(3):
            tap = row_off * 3 + col_off
            near = found[row_par + 2 - row_off][col_par + 2 - col_off]
            term = taps[tap] * near
            total = term if total is None else total + term
            part = source * near
            sums[tap] = sums[tap] + (part[:8] + part[8:])
    return total, tuple(sums)


def no_sums():
    return tuple(jnp.zeros((8, LANES), F32) for _ in range(9))


def split_lanes(values_in):
    count = values_in.shape[-1] // LANES
    return [values_in[:, j * LANES : (j + 1) * LANES] for j in range(count)]


def norm_parts(parts):
    width = len(parts) * LANES
    mean = jnp.sum(sum(parts[1:], parts[0]), axis=-1, keepdims=True) * (1.0 / width)
    centre = [part - mean for part in parts]
    squares = [part * part for part in centre]
    var = jnp.sum(sum(squares[1:], squares[0]), axis=-1, keepdims=True) * (1.0 / width)
    rstd = lax.rsqrt(var + EPS)
    return [part * rstd for part in centre], rstd


def norm_rows(values_in):
    mean = jnp.mean(values_in, axis=-1, keepdims=True)
    centre = values_in - mean
    rstd = lax.rsqrt(jnp.mean(centre * centre, axis=-1, keepdims=True) + EPS)
    return centre * rstd, rstd


def modulation_kernel(silu_ref, weight_ref, mod_out):
    left = jnp.broadcast_to(silu_ref[...].astype(F32), (16, silu_ref.shape[-1])).astype(BF16)
    mod_out[pl.ds(pl.program_id(0), 1), :] = dot(left, weight_ref[...])[:1]


def modulation_stage(silu_low, w_mod):
    width = silu_low.shape[-1]
    return pl.pallas_call(
        modulation_kernel,
        out_shape=jax.ShapeDtypeStruct((w_mod.shape[-1] // width, width), F32),
        grid=(w_mod.shape[-1] // width,),
        in_specs=[whole(silu_low.shape), pl.BlockSpec((width, width), lambda i: (0, i))],
        out_specs=whole((w_mod.shape[-1] // width, width)),
        compiler_params=params(),
        name="modulation",
        cost_estimate=SMALL_COST,
    )(silu_low, w_mod)


def group_of(row_par, col_par):
    return row_par * 2 + col_par


def first_kernel(
    idx, tok_ref, cot_ref, mod_ref, kern_ref, conv_out, tok_out, cot_out, tok_tmp, cot_tmp, grid
):
    width = tok_ref.shape[-1]
    count = width // LANES
    grid[...] = jnp.zeros(grid.shape, F32)

    def one_row(row, carry):
        for row_par in range(2):
            start = pl.multiple_of((row * 2 + row_par) * SIDE, SIDE)
            values = tok_ref[0, pl.ds(start, SIDE), :].astype(F32)
            grads = cot_ref[0, pl.ds(start, SIDE), :].astype(F32)
            for j in range(count):
                tok_tmp[row_par, j] = values[:, j * LANES : (j + 1) * LANES]
                cot_tmp[row_par, j] = grads[:, j * LANES : (j + 1) * LANES]
            for col_par in range(2):
                group = group_of(row_par, col_par)
                out_row = pl.multiple_of(group * TILE + row * HALF, HALF)
                parts = [tok_tmp[row_par, j, pl.ds(col_par, HALF, stride=2), :] for j in range(count)]
                for j in range(count):
                    lanes = slice(j * LANES, (j + 1) * LANES)
                    tok_out[pl.ds(out_row, HALF), lanes] = parts[j].astype(BF16)
                    cot_out[pl.ds(out_row, HALF), lanes] = cot_tmp[
                        row_par, j, pl.ds(col_par, HALF, stride=2), :
                    ].astype(BF16)
                normed, _ = norm_parts(parts)
                for j in range(count):
                    lanes = slice(j * LANES, (j + 1) * LANES)
                    value = normed[j] * (1.0 + mod_ref[1:2, lanes]) + mod_ref[0:1, lanes]
                    grid[j, pl.ds(row * PITCH + pad_row(group, 0), HALF), :] = value
        return carry

    lax.fori_loop(0, HALF, one_row, 0)
    for j in range(count):
        lanes = slice(j * LANES, (j + 1) * LANES)
        taps = taps_of(kern_ref, lanes)

        def one_conv(row, carry, j=j, lanes=lanes, taps=taps):
            found = neighbours(grid, j, row)
            for row_par in range(2):
                for col_par in range(2):
                    out_row = pl.multiple_of(group_of(row_par, col_par) * TILE + row * HALF, HALF)
                    value = conv_at(found, taps, row_par, col_par)
                    conv_out[pl.ds(out_row, HALF), lanes] = value.astype(BF16)
            return carry

        lax.fori_loop(0, HALF, one_conv, 0)


def first_stage(idx, tokens, cotangent, mod, kern):
    _, length, width = tokens.shape
    shape = jax.ShapeDtypeStruct((length, width), BF16)
    mine = pl.BlockSpec((1, length, width), lambda i, idx: (idx[0], 0, 0))
    return pl.pallas_call(
        first_kernel,
        out_shape=(shape, shape, shape),
        grid_spec=pltpu.PrefetchScalarGridSpec(
            num_scalar_prefetch=1,
            grid=(1,),
            in_specs=[mine, mine, whole(mod.shape), whole(kern.shape)],
            out_specs=[whole((length, width))] * 3,
            scratch_shapes=[
                pltpu.VMEM((2, width // LANES, SIDE, LANES), F32),
                pltpu.VMEM((2, width // LANES, SIDE, LANES), F32),
                pltpu.VMEM((width // LANES, PAD_ROWS, LANES), F32),
            ],
        ),
        compiler_params=params(),
        name="norm_conv",
        cost_estimate=SMALL_COST,
    )(idx, tokens, cotangent, mod, kern)


def head_mask(values_in, which):
    lane = lax.broadcasted_iota(jnp.int32, values_in.shape, 1)
    keep = lane < HEAD_DIM if which == 0 else lane >= HEAD_DIM
    return jnp.where(keep, values_in, jnp.zeros_like(values_in))


def soft_keys(keys, queries, keep):
    raw = dot_nt(keys, queries)
    scores = jnp.where(keep, raw * (HEAD_DIM**-0.5), -1e30)
    exponent = jnp.exp(scores - jnp.max(scores, axis=0, keepdims=True))
    return exponent * (1.0 / jnp.sum(exponent, axis=0, keepdims=True))


def attend_heads(conved, keep, weight_ref, qkv_out, mixed_out):
    share = weight_ref.shape[-1]
    for which in range(3):
        qkv_out[:, which * share : (which + 1) * share] = dot(conved, weight_ref[which]).astype(BF16)
    for pair in range(share // LANES):
        lanes = [slice(t * share + pair * LANES, t * share + (pair + 1) * LANES) for t in range(3)]
        queries = qkv_out[:, lanes[0]]
        keys = qkv_out[:, lanes[1]]
        values_t = qkv_out[:, lanes[2]].astype(F32).T.astype(BF16)
        halves = []
        for which in range(2):
            probs = soft_keys(head_mask(keys, which), queries, keep).astype(BF16)
            halves.append(dot(values_t[which * HEAD_DIM : (which + 1) * HEAD_DIM], probs))
        mixed_out[:, pair * LANES : (pair + 1) * LANES] = jnp.concatenate(halves, axis=0).T.astype(BF16)


def attend_own_kernel(conv_ref, valid_ref, weight_ref, perm_ref, convt_out, qkv_out, mixed_out):
    conved = conv_ref[...]
    convt_out[...] = dot_nt(perm_ref[...], conved).astype(BF16)
    keep = jnp.broadcast_to(valid_ref[0], (TILE, TILE)) > 0
    attend_heads(conved, keep, weight_ref, qkv_out, mixed_out)


def attend_other_kernel(
    conv_ref, valid_ref, weight_ref, mown_ref, oa_ref, ob_ref, tok_ref, cot_ref, mod_ref,
    qkv_out, mixed_out, attn_out, res_out, norm_out, gdown_out,
):
    keep = jnp.broadcast_to(valid_ref[0], (TILE, TILE)) > 0
    attend_heads(conv_ref[...], keep, weight_ref, qkv_out, mixed_out)
    attn = dot_nt(mown_ref[...], oa_ref[...]) + dot_nt(mixed_out[...], ob_ref[...])
    attn_out[...] = attn
    residual = tok_ref[...].astype(F32) + mod_ref[2:3, :] * attn
    res_out[...] = residual
    normed, _ = norm_rows(residual)
    norm_out[...] = (normed * (1.0 + mod_ref[4:5, :]) + mod_ref[3:4, :]).astype(BF16)
    gdown_out[...] = (mod_ref[5:6, :] * cot_ref[...].astype(F32)).astype(BF16)


def group_rows(cols):
    return pl.BlockSpec((TILE, cols), lambda g: (g, 0))


def attend_own_stage(conved, valid, w_own, perm):
    length, width = conved.shape
    share = w_own.shape[-1]
    return pl.pallas_call(
        attend_own_kernel,
        out_shape=(
            jax.ShapeDtypeStruct((width, length), BF16),
            jax.ShapeDtypeStruct((length, 3 * share), BF16),
            jax.ShapeDtypeStruct((length, share), BF16),
        ),
        grid=(GROUPS,),
        in_specs=[
            group_rows(width),
            pl.BlockSpec((1, TILE, 1), lambda g: (g, 0, 0)),
            whole(w_own.shape),
            whole(perm.shape),
        ],
        out_specs=[
            pl.BlockSpec((width, TILE), lambda g: (0, g)),
            group_rows(3 * share),
            group_rows(share),
        ],
        compiler_params=params(),
        name="attend_own",
        cost_estimate=SMALL_COST,
    )(conved, valid, w_own, perm)


def attend_other_stage(conved, valid, other, mixed_own, o_own, tok, cot, mod):
    length, width = conved.shape
    share = other.shape[-1]
    low = jax.ShapeDtypeStruct((length, width), BF16)
    high = jax.ShapeDtypeStruct((length, width), F32)
    return pl.pallas_call(
        attend_other_kernel,
        out_shape=(
            jax.ShapeDtypeStruct((length, 3 * share), BF16),
            jax.ShapeDtypeStruct((length, share), BF16),
            high,
            high,
            low,
            low,
        ),
        grid=(GROUPS,),
        in_specs=[
            group_rows(width),
            pl.BlockSpec((1, TILE, 1), lambda g: (g, 0, 0)),
            leading(other, 3),
            group_rows(share),
            whole(o_own.shape),
            entry(other, 3),
            group_rows(width),
            group_rows(width),
            whole(mod.shape),
        ],
        out_specs=[group_rows(3 * share), group_rows(share)] + [group_rows(width)] * 4,
        compiler_params=params(),
        name="attend_other",
        cost_estimate=SMALL_COST,
    )(conved, valid, other, mixed_own, o_own, other, tok, cot, mod)


def gelu_pair(value):
    square = value * value
    inner = jnp.tanh(GELU_A * (value + GELU_B * (square * value)))
    cdf = 0.5 * (1.0 + inner)
    slope = cdf + (value * (0.5 * GELU_A)) * (1.0 - inner * inner) * (1.0 + (3.0 * GELU_B) * square)
    return value * cdf, slope


def ffn_kernel(split, *refs):
    idx, perm_ref, norm_ref, gdown_ref, up_ref, down_ref, kern_ref = refs[:7]
    grads_out = refs[7 : 9 if split else 8]
    kern_out, sum_out, gnorm_out = refs[len(grads_out) + 7 : len(grads_out) + 10]
    norm_t, gdown_t, grid_up, grid_gz, gact, active, gupper = refs[len(grads_out) + 10 :]
    width = norm_ref.shape[-1]
    chunk = up_ref.shape[-1]
    first = pl.program_id(0) == 0

    @pl.when(first)
    def _():
        norm_t[...] = dot_nt(perm_ref[...], norm_ref[...]).astype(BF16)
        gdown_t[...] = dot_nt(perm_ref[...], gdown_ref[...]).astype(BF16)
        grid_up[...] = jnp.zeros(grid_up.shape, F32)
        grid_gz[...] = jnp.zeros(grid_gz.shape, F32)

    for block in range(chunk // TILE):
        cols = slice(block * TILE, (block + 1) * TILE)
        upper = dot(norm_ref[...], up_ref[:, cols])
        grads = dot(gdown_ref[...], down_ref[:, cols])
        for side in range(TILE // LANES):
            j = block * (TILE // LANES) + side
            lanes = slice(side * LANES, (side + 1) * LANES)
            gact[j] = grads[:, lanes]
            for group in range(GROUPS):
                for row in range(HALF):
                    at = group * TILE + row * HALF
                    grid_up[j, pl.ds(pad_row(group, row), HALF), :] = upper[at : at + HALF, lanes]

    def one_block(j, carry):
        lanes = pl.ds(pl.multiple_of(j * LANES, LANES), LANES)
        taps = taps_of(kern_ref, lanes)

        def forward(row, carry):
            found = neighbours(grid_up, j, row)
            for row_par in range(2):
                for col_par in range(2):
                    group = group_of(row_par, col_par)
                    out_row = pl.multiple_of(group * TILE + row * HALF, HALF)
                    act, slope = gelu_pair(conv_at(found, taps, row_par, col_par))
                    active[pl.ds(out_row, HALF), lanes] = act.astype(BF16)
                    grid_gz[j, pl.ds(row * PITCH + pad_row(group, 0), HALF), :] = (
                        gact[j, pl.ds(out_row, HALF), :] * slope
                    )
            return carry

        lax.fori_loop(0, HALF, forward, 0)

        def backward(row, sums):
            found = neighbours(grid_gz, j, row)
            for row_par in range(2):
                for col_par in range(2):
                    group = group_of(row_par, col_par)
                    out_row = pl.multiple_of(group * TILE + row * HALF, HALF)
                    source = grid_up[j, pl.ds(row * PITCH + pad_row(group, 0), HALF), :]
                    grad, sums = conv_back_at(found, taps, sums, source, row_par, col_par)
                    gupper[pl.ds(out_row, HALF), lanes] = grad.astype(BF16)
            return sums

        sums = lax.fori_loop(0, HALF, backward, no_sums())
        for tap in range(9):
            kern_out[tap : tap + 1, lanes] = jnp.sum(sums[tap], axis=0, keepdims=True)
        return carry

    lax.fori_loop(0, chunk // LANES, one_block, 0)

    half_rows = width // 2
    mine = pl.multiple_of(idx[1] * half_rows, half_rows)
    theirs = pl.multiple_of((1 - idx[1]) * half_rows, half_rows)
    for block in range(chunk // TILE):
        cols = slice(block * TILE, (block + 1) * TILE)
        for which, (left, right) in enumerate(((norm_t, gupper), (gdown_t, active))):
            out_cols = slice(which * chunk + block * TILE, which * chunk + (block + 1) * TILE)
            if split:
                keep_out, send_out = grads_out
                send_out[:, out_cols] = dot(left[pl.ds(theirs, half_rows), :], right[:, cols]).astype(BF16)
                keep_out[:, out_cols] = dot(left[pl.ds(mine, half_rows), :], right[:, cols])
            else:
                grads_out[0][:, out_cols] = dot(left[...], right[:, cols]).astype(BF16)
    for block in range(width // TILE):
        cols = slice(block * TILE, (block + 1) * TILE)
        part = dot_nt(active[...], down_ref[cols, :])
        gpart = dot_nt(gupper[...], up_ref[cols, :])

        @pl.when(first)
        def _(cols=cols, part=part, gpart=gpart):
            sum_out[:, cols] = part
            gnorm_out[:, cols] = gpart

        @pl.when(jnp.logical_not(first))
        def _(cols=cols, part=part, gpart=gpart):
            sum_out[:, cols] += part
            gnorm_out[:, cols] += gpart


def ffn_stage(idx, perm, normed, gdown, weights, kern, chunk, split):
    length, width = normed.shape
    hidden = kern.shape[-1]
    if isinstance(weights, tuple):
        w_up, w_down = weights
        up_spec = down_spec = pl.BlockSpec((width, chunk), lambda i, idx: (0, i))
    else:
        w_up = w_down = weights
        up_spec = pl.BlockSpec((None, width, chunk), lambda i, idx: (0, 0, i))
        down_spec = pl.BlockSpec((None, width, chunk), lambda i, idx: (1, 0, i))
    small = pl.BlockSpec((9, chunk), lambda i, idx: (0, i))
    count = chunk // LANES
    full = jax.ShapeDtypeStruct((length, width), F32)
    rows = width // 2 if split else width
    grads = [jax.ShapeDtypeStruct((rows, 2 * hidden), BF16)]
    if split:
        grads.insert(0, jax.ShapeDtypeStruct((rows, 2 * hidden), F32))
    grads_spec = pl.BlockSpec((rows, 2 * chunk), lambda i, idx: (0, i))
    return pl.pallas_call(
        partial(ffn_kernel, split),
        out_shape=(*grads, jax.ShapeDtypeStruct((9, hidden), F32), full, full),
        grid_spec=pltpu.PrefetchScalarGridSpec(
            num_scalar_prefetch=1,
            grid=(hidden // chunk,),
            in_specs=[
                whole(perm.shape),
                whole(normed.shape),
                whole(gdown.shape),
                up_spec,
                down_spec,
                small,
            ],
            out_specs=[grads_spec] * len(grads) + [small, whole(full.shape), whole(full.shape)],
            scratch_shapes=[
                pltpu.VMEM((width, length), BF16),
                pltpu.VMEM((width, length), BF16),
                pltpu.VMEM((count, PAD_ROWS, LANES), F32),
                pltpu.VMEM((count, PAD_ROWS, LANES), F32),
                pltpu.VMEM((count, length, LANES), F32),
                pltpu.VMEM((length, chunk), BF16),
                pltpu.VMEM((length, chunk), BF16),
            ],
        ),
        compiler_params=params(),
        name="ffn",
        cost_estimate=SMALL_COST,
    )(idx, perm, normed, gdown, w_up, w_down, kern)


def middle_kernel(
    idx, perm_ref, res_ref, attn_ref, da_ref, db_ref, dc_ref, ga_ref, gb_ref, gc_ref, cot_ref, ma_ref, mb_ref,
    oa_ref, ob_ref, mod_ref, out_ref, gres_out, gmix_out, sums_out, keep_out, send_out, ordered, total,
):
    share = oa_ref.shape[-1]
    width = res_ref.shape[-1]
    group = pl.program_id(0)
    residual = res_ref[...]
    cot = cot_ref[...].astype(F32)
    down = (da_ref[...] + db_ref[...]) + dc_ref[...]
    result = residual + mod_ref[5:6, :] * down
    parity = (group // 2) * SIDE + lax.rem(group, 2)
    for row in range(HALF):
        for j in range(width // LANES):
            ordered[j, pl.ds(parity + row * 2 * SIDE, HALF, stride=2), :] = result[
                row * HALF : (row + 1) * HALF, j * LANES : (j + 1) * LANES
            ]
    grad_n = (ga_ref[...] + gb_ref[...]) + gc_ref[...]
    normed, rstd = norm_rows(residual)
    scaled = grad_n * (1.0 + mod_ref[4:5, :])
    mean_a = jnp.mean(scaled, axis=-1, keepdims=True)
    mean_b = jnp.mean(scaled * normed, axis=-1, keepdims=True)
    gres = cot + rstd * (scaled - mean_a - normed * mean_b)
    gres_out[...] = gres
    sums = jnp.concatenate(
        [
            jnp.sum(gres * attn_ref[...], axis=0, keepdims=True),
            jnp.sum(grad_n, axis=0, keepdims=True),
            jnp.sum(grad_n * normed, axis=0, keepdims=True),
            jnp.sum(cot * down, axis=0, keepdims=True),
        ],
        axis=0,
    )
    gattn = (mod_ref[2:3, :] * gres).astype(BF16)
    gmix_out[:, :share] = dot(gattn, oa_ref[...]).astype(BF16)
    gmix_out[:, share:] = dot(gattn, ob_ref[...]).astype(BF16)
    gattn_t = dot_nt(perm_ref[...], gattn).astype(BF16)
    part = jnp.concatenate([dot(gattn_t, ma_ref[...]), dot(gattn_t, mb_ref[...])], axis=1)

    @pl.when(group == 0)
    def _():
        sums_out[...] = sums
        total[...] = part

    @pl.when(group > 0)
    def _():
        sums_out[...] += sums
        total[...] += part

    @pl.when(group == GROUPS - 1)
    def _():
        half_rows = width // 2
        keep_out[...] = total[pl.ds(pl.multiple_of(idx[1] * half_rows, half_rows), half_rows), :]
        send_out[...] = total[
            pl.ds(pl.multiple_of((1 - idx[1]) * half_rows, half_rows), half_rows), :
        ].astype(BF16)
        for j in range(width // LANES):
            out_ref[:, j * LANES : (j + 1) * LANES] = ordered[j].astype(BF16)


def middle_stage(idx, perm, res, attn, downs, gnorms, cot, mixed, o_own, other, mod):
    half = pl.BlockSpec((TILE, o_own.shape[-1]), lambda g, idx: (g, 0))
    length, width = res.shape
    rows = pl.BlockSpec((TILE, width), lambda g, idx: (g, 0))
    half_rows = width // 2
    low = jax.ShapeDtypeStruct((length, width), BF16)
    return pl.pallas_call(
        middle_kernel,
        out_shape=(
            low,
            jax.ShapeDtypeStruct((length, width), F32),
            low,
            jax.ShapeDtypeStruct((4, width), F32),
            jax.ShapeDtypeStruct((half_rows, width), F32),
            jax.ShapeDtypeStruct((half_rows, width), BF16),
        ),
        grid_spec=pltpu.PrefetchScalarGridSpec(
            num_scalar_prefetch=1,
            grid=(GROUPS,),
            in_specs=[whole(perm.shape)]
            + [rows] * 9
            + [half] * 2
            + [whole(o_own.shape), entry(other, 3), whole(mod.shape)],
            out_specs=[
                whole((length, width)),
                rows,
                rows,
                whole((4, width)),
                whole((half_rows, width)),
                whole((half_rows, width)),
            ],
            scratch_shapes=[
                pltpu.VMEM((width // LANES, length, LANES), F32),
                pltpu.VMEM((width, width), F32),
            ],
        ),
        compiler_params=params(),
        name="middle",
        cost_estimate=SMALL_COST,
    )(idx, perm, res, attn, *downs, *gnorms, cot, *mixed, o_own, other, mod)


def attend_back_kernel(qkv_ref, gmix_ref, valid_ref, gqkv_out):
    share = qkv_ref.shape[-1] // 3
    keep = jnp.broadcast_to(valid_ref[0], (TILE, TILE)) > 0
    lane = lax.broadcasted_iota(jnp.int32, (TILE, LANES), 1)
    for pair in range(share // LANES):
        lanes = [slice(t * share + pair * LANES, t * share + (pair + 1) * LANES) for t in range(3)]
        queries = qkv_ref[:, lanes[0]]
        keys = qkv_ref[:, lanes[1]]
        values = qkv_ref[:, lanes[2]]
        gmix = gmix_ref[:, pair * LANES : (pair + 1) * LANES]
        keys_t = keys.astype(F32).T.astype(BF16)
        gq, gk, gv = [], [], []
        for which in range(2):
            probs = soft_keys(head_mask(keys, which), queries, keep)
            gprobs = dot_nt(head_mask(values, which), gmix)
            gv.append(dot(probs.astype(BF16), gmix))
            weighted = probs * gprobs
            gscores = weighted - probs * jnp.sum(weighted, axis=0, keepdims=True)
            graw = (gscores * (HEAD_DIM**-0.5)).astype(BF16)
            gk.append(dot(graw, queries))
            gq.append(dot(keys_t[which * HEAD_DIM : (which + 1) * HEAD_DIM], graw))
        gqkv_out[:, lanes[0]] = jnp.concatenate(gq, axis=0).T.astype(BF16)
        gqkv_out[:, lanes[1]] = jnp.where(lane < HEAD_DIM, gk[0], gk[1]).astype(BF16)
        gqkv_out[:, lanes[2]] = jnp.where(lane < HEAD_DIM, gv[0], gv[1]).astype(BF16)


def attend_back_stage(qkv, gmix, valid, side):
    length = gmix.shape[0]
    cols = qkv.shape[-1]
    return pl.pallas_call(
        attend_back_kernel,
        out_shape=jax.ShapeDtypeStruct((length, cols), BF16),
        grid=(GROUPS,),
        in_specs=[
            group_rows(cols),
            pl.BlockSpec((TILE, cols // 3), lambda g: (g, side)),
            pl.BlockSpec((1, TILE, 1), lambda g: (g, 0, 0)),
        ],
        out_specs=pl.BlockSpec((TILE, cols), lambda g: (g, 0)),
        compiler_params=params(),
        name="attend_back",
        cost_estimate=SMALL_COST,
    )(qkv, gmix, valid)


def qkv_grad_kernel(idx, conv_ref, gqkv_ref, okeep_ref, osend_ref, keep_out, send_out):
    half_rows = keep_out.shape[0]
    share = okeep_ref.shape[-1]
    mine = pl.multiple_of(idx[1] * half_rows, half_rows)
    theirs = pl.multiple_of((1 - idx[1]) * half_rows, half_rows)
    for which in range(3):
        cols = slice(which * share, (which + 1) * share)
        grads = gqkv_ref[:, cols]
        send_out[:, cols] = dot(conv_ref[pl.ds(theirs, half_rows), :], grads).astype(BF16)
        keep_out[:, cols] = dot(conv_ref[pl.ds(mine, half_rows), :], grads)
    keep_out[:, 3 * share :] = okeep_ref[...]
    send_out[:, 3 * share :] = osend_ref[...]


def qkv_grad_stage(idx, conv_t, gqkv, out_keep, out_send, side):
    width = conv_t.shape[0]
    half_rows = width // 2
    share = gqkv.shape[-1] // 3
    shape = (half_rows, 4 * share)
    part = pl.BlockSpec((half_rows, share), lambda i, idx: (0, side))
    return pl.pallas_call(
        qkv_grad_kernel,
        out_shape=(jax.ShapeDtypeStruct(shape, F32), jax.ShapeDtypeStruct(shape, BF16)),
        grid_spec=pltpu.PrefetchScalarGridSpec(
            num_scalar_prefetch=1,
            grid=(1,),
            in_specs=[whole(conv_t.shape), whole(gqkv.shape), part, part],
            out_specs=[whole(shape), whole(shape)],
        ),
        compiler_params=params(),
        name="qkv_grad",
        cost_estimate=SMALL_COST,
    )(idx, conv_t, gqkv, out_keep, out_send)


def conv_back_kernel(
    ga_ref, gb_ref, wa_ref, wb_ref, tok_ref, mod_ref, kern_ref,
    grads_out, kern_out, sums_out, grid_g, normed_s,
):
    length, width = tok_ref.shape
    count = width // LANES
    share = wa_ref.shape[-1]
    grid_g[...] = jnp.zeros(grid_g.shape, F32)
    for block in range(width // TILE):
        rows = slice(block * TILE, (block + 1) * TILE)
        total = None
        for grads_ref, weight_ref in ((ga_ref, wa_ref), (gb_ref, wb_ref)):
            for which in range(3):
                part = dot_nt(
                    grads_ref[:, which * share : (which + 1) * share], weight_ref[which, rows, :]
                )
                total = part if total is None else total + part
        for side in range(TILE // LANES):
            j = block * (TILE // LANES) + side
            lanes = slice(side * LANES, (side + 1) * LANES)
            for group in range(GROUPS):
                for row in range(HALF):
                    at = group * TILE + row * HALF
                    grid_g[j, pl.ds(pad_row(group, row), HALF), :] = total[at : at + HALF, lanes]

    def one_norm(row, carry):
        at = pl.multiple_of(row * SIDE, SIDE)
        normed, _ = norm_parts(split_lanes(tok_ref[pl.ds(at, SIDE), :].astype(F32)))
        for j in range(count):
            normed_s[j, pl.ds(at, SIDE), :] = normed[j]
        return carry

    lax.fori_loop(0, length // SIDE, one_norm, 0)

    for j in range(count):
        lanes = slice(j * LANES, (j + 1) * LANES)
        taps = taps_of(kern_ref, lanes)

        scale, shift = 1.0 + mod_ref[1:2, lanes], mod_ref[0:1, lanes]

        def backward(row, carry, j=j, lanes=lanes, taps=taps, scale=scale, shift=shift):
            sums, (shift_sum, scale_sum) = carry
            found = neighbours(grid_g, j, row)
            for row_par in range(2):
                for col_par in range(2):
                    at = pl.multiple_of(group_of(row_par, col_par) * TILE + row * HALF, HALF)
                    normed = normed_s[j, pl.ds(at, HALF), :]
                    grad, sums = conv_back_at(found, taps, sums, normed * scale + shift, row_par, col_par)
                    grads_out[pl.ds(at, HALF), lanes] = grad
                    prod = grad * normed
                    shift_sum = shift_sum + (grad[:8] + grad[8:])
                    scale_sum = scale_sum + (prod[:8] + prod[8:])
            return sums, (shift_sum, scale_sum)

        zero = jnp.zeros((8, LANES), F32)
        sums, pair = lax.fori_loop(0, HALF, backward, (no_sums(), (zero, zero)))
        for which in range(2):
            sums_out[which : which + 1, lanes] = jnp.sum(pair[which], axis=0, keepdims=True)
        for tap in range(9):
            kern_out[tap : tap + 1, lanes] = jnp.sum(sums[tap], axis=0, keepdims=True)


def conv_back_stage(g_own, g_other, w_own, other, tok, mod, kern):
    length, width = tok.shape
    count = width // LANES
    operands = (g_own, g_other, w_own, other, tok, mod, kern)
    return pl.pallas_call(
        conv_back_kernel,
        out_shape=(
            jax.ShapeDtypeStruct((length, width), F32),
            jax.ShapeDtypeStruct((9, width), F32),
            jax.ShapeDtypeStruct((2, width), F32),
        ),
        grid=(1,),
        in_specs=[leading(each, 3) if each is other else whole(each.shape) for each in operands],
        out_specs=[whole((length, width)), whole((9, width)), whole((2, width))],
        scratch_shapes=[
            pltpu.VMEM((count, PAD_ROWS, LANES), F32),
            pltpu.VMEM((count, length, LANES), F32),
        ],
        compiler_params=params(),
        name="conv_back",
        cost_estimate=SMALL_COST,
    )(*operands)


def norm_back_kernel(grads_ref, tok_ref, gres_ref, mod_ref, gtok_out, ordered):
    width = tok_ref.shape[-1]
    group = pl.program_id(0)
    grads = grads_ref[...]
    normed, rstd = norm_rows(tok_ref[...].astype(F32))
    scaled = grads * (1.0 + mod_ref[1:2, :])
    mean_a = jnp.mean(scaled, axis=-1, keepdims=True)
    mean_b = jnp.mean(scaled * normed, axis=-1, keepdims=True)
    result = gres_ref[...] + rstd * (scaled - mean_a - normed * mean_b)
    parity = (group // 2) * SIDE + lax.rem(group, 2)
    for row in range(HALF):
        for j in range(width // LANES):
            ordered[j, pl.ds(parity + row * 2 * SIDE, HALF, stride=2), :] = result[
                row * HALF : (row + 1) * HALF, j * LANES : (j + 1) * LANES
            ]

    @pl.when(group == GROUPS - 1)
    def _():
        for j in range(width // LANES):
            gtok_out[:, j * LANES : (j + 1) * LANES] = ordered[j].astype(BF16)


def norm_back_stage(grads, tok, gres, mod):
    length, width = tok.shape
    return pl.pallas_call(
        norm_back_kernel,
        out_shape=jax.ShapeDtypeStruct((length, width), BF16),
        grid=(GROUPS,),
        in_specs=[group_rows(width), group_rows(width), group_rows(width), whole(mod.shape)],
        out_specs=whole((length, width)),
        scratch_shapes=[pltpu.VMEM((width // LANES, length, LANES), F32)],
        compiler_params=params(),
        name="norm_back",
        cost_estimate=SMALL_COST,
    )(grads, tok, gres, mod)


def silu_of(values_in):
    return values_in * jax.nn.sigmoid(values_in)


def swap(values_in, axis, bit):
    size = lax.axis_size(axis)
    return lax.ppermute(values_in, axis, [(i, i ^ bit) for i in range(size)])


def spread(size, position):
    if size < 4:
        return position
    quarter = size // 4
    low, rest = position // (2 * quarter), position % (2 * quarter)
    return (rest % quarter) * 4 + (rest // quarter) * 2 + low


def row_permutation(size, width):
    block = width // size
    order = [spread(size, i // block) * block + i % block for i in range(width)]
    source = jnp.array(order, jnp.int32)
    return (source[:, None] == jnp.arange(width, dtype=jnp.int32)[None, :]).astype(BF16)


def tie(values_in, *first):
    return lax.optimization_barrier((values_in, first))[0]


def halving_bits(size):
    bits = [2] if size > 2 else []
    rest = size // 4
    while rest > 1:
        bits.append(rest * 2)
        rest //= 2
    return bits


def unshuffle(tokens_in):
    blocked = tokens_in.reshape(HALF, 2, HALF, 2)
    return blocked.transpose(1, 3, 0, 2).reshape(GROUPS, TILE)


def local(
    tokens,
    valid,
    steps,
    labels,
    w_mod,
    step_table,
    class_table,
    conv_attn,
    w_qkv,
    w_out,
    conv_ffn,
    w_up,
    w_down,
    cotangent,
):
    dp_size = lax.axis_size("dp")
    width = tokens.shape[-1]
    dp_at = lax.axis_index("dp")
    mp_at = lax.axis_index("mp")
    latent = dp_at * tokens.shape[0] + mp_at
    idx = jnp.stack([mp_at, dp_at % 2]).astype(jnp.int32)
    perm = row_permutation(dp_size, width)

    core = dp_at % 2
    half_rows = width // 2
    hidden = w_up.shape[-1]
    chunk = hidden // 2
    share = w_out.shape[-1]
    rows = width // dp_size
    bits = halving_bits(dp_size)

    def split_rows(total, bit):
        rows = total.shape[-2] // 2
        parts = total.reshape(total.shape[:-2] + (2, rows) + total.shape[-1:])
        axis = parts.ndim - 3
        flag = (dp_at // bit) % 2
        mine = lax.dynamic_index_in_dim(parts, flag, axis, keepdims=False)
        theirs = lax.dynamic_index_in_dim(parts, 1 - flag, axis, keepdims=False)
        return mine, theirs.astype(BF16)

    def ordered_pair(first, second, axis):
        return jnp.concatenate(
            [jnp.where(core == 0, first, second), jnp.where(core == 0, second, first)], axis=axis
        )

    def both(mine, theirs):
        place = lax.broadcasted_iota(jnp.int32, (2,) + mine.shape, 0)
        return jnp.where(place == mp_at, mine[None], theirs[None])

    qkv_own = w_qkv.transpose(1, 0, 2)
    stack = jnp.concatenate([qkv_own, w_out[None]], axis=0)
    part_a = swap(lax.dynamic_slice_in_dim(stack, core * half_rows, half_rows, axis=1), "mp", 1)
    kern_other = swap(conv_ffn, "mp", 1)

    embedding = jnp.take(step_table, steps, axis=0).astype(F32) + jnp.take(
        class_table, labels, axis=0
    ).astype(F32)
    silu_value, silu_pull = jax.vjp(silu_of, embedding)
    silu_low = silu_value.astype(BF16)
    my_silu = lax.dynamic_slice_in_dim(silu_low, latent, 1)
    mod = modulation_stage(my_silu, w_mod)

    my_valid = lax.dynamic_index_in_dim(valid, mp_at, 0, keepdims=False)
    keep = unshuffle(my_valid)[:, :, None]

    conved, tok, cot = first_stage(idx, tokens, cotangent, mod, conv_attn)
    conv_t, qkv_x, mixed_x = attend_own_stage(conved, keep, qkv_own, perm)

    part_a = tie(part_a, mixed_x)
    part_b = swap(part_a, "dp", 1)
    up_part, down_part = tie((w_up, w_down), part_a)
    ffn_part = jnp.stack(
        [
            lax.dynamic_slice_in_dim(up_part, core * chunk, chunk, axis=1),
            lax.dynamic_slice_in_dim(down_part, core * chunk, chunk, axis=1),
        ]
    )
    ffn_a = swap(ffn_part, "mp", 1)
    other = ordered_pair(part_a, part_b, 1)
    qkv_y, mixed_y, attn, res, normed, gdown = attend_other_stage(
        tie(conved, ffn_part), keep, other, mixed_x, w_out, tok, cot, mod
    )

    plain = jnp.eye(width, dtype=BF16)
    grads_x, kern_x, down_x, gnorm_x = ffn_stage(
        idx, plain, normed, gdown, (w_up, w_down), conv_ffn, chunk, False
    )
    sum_x = lax.psum_scatter(grads_x, "dp", scatter_dimension=0, tiled=True)
    ffn_a = tie(ffn_a, down_x)
    ffn_b = swap(ffn_a, "dp", 1)
    kern_part = lax.dynamic_slice_in_dim(kern_other, core * chunk, chunk, axis=1)
    keep_y, send_y, kern_y, down_y, gnorm_y = ffn_stage(
        idx, perm, normed, gdown, ffn_a, kern_part, chunk, True
    )
    got_y = swap(send_y, "dp", 1)
    kern_part = lax.dynamic_slice_in_dim(kern_other, (1 - core) * chunk, chunk, axis=1)
    keep_z, send_z, kern_z, down_z, gnorm_z = ffn_stage(
        idx, perm, tie(normed, down_y), gdown, ffn_b, kern_part, chunk, True
    )
    got_z = swap(send_z, "dp", 1)
    output, gres, gmix, sums_mid, out_keep, out_send = middle_stage(
        idx, perm, res, attn, (down_x, down_y, down_z), (gnorm_x, gnorm_y, tie(gnorm_z, got_y)),
        cot, (mixed_x, mixed_y), w_out, other, mod,
    )
    got_y, got_z = tie((got_y, got_z), gmix)
    total_f = jnp.stack([keep_y + got_z.astype(F32), keep_z + got_y.astype(F32)])
    mine_f, theirs = split_rows(total_f, bits[0])
    got_f = swap(theirs, "dp", bits[0])
    gmix = tie(gmix, theirs)
    output_other = swap(tie(output, theirs), "mp", 1)

    g_other = attend_back_stage(qkv_y, gmix, keep, 1)
    c_keep, c_send = qkv_grad_stage(idx, conv_t, g_other, out_keep, out_send, 1)
    c_got = swap(c_send, "dp", 1)
    g_own = attend_back_stage(qkv_x, tie(gmix, c_send), keep, 0)
    c_got, got_f = tie((c_got, got_f), g_own)
    total_c = (c_keep + c_got.astype(F32)).astype(BF16)
    from_x = swap(total_c, "mp", 1)
    total_f = mine_f + got_f.astype(F32)
    mine_f, theirs = split_rows(total_f, bits[1])
    got_f = swap(theirs, "dp", bits[1])
    d_keep, d_send = qkv_grad_stage(
        idx, conv_t, tie(g_own, total_c, theirs), out_keep, out_send, 0
    )
    d_got = swap(d_send, "dp", 1)
    whole_output = both(output, output_other)
    grads, kern_a, sums_last = conv_back_stage(
        tie(g_own, d_send, whole_output), g_other, qkv_own, other, tok, mod, conv_attn
    )

    d_got, from_x, got_f = tie((d_got, from_x, got_f), grads)
    total_d = d_keep + d_got.astype(F32) + from_x.astype(F32)
    mine_d, theirs = split_rows(total_d, bits[0])
    got_d = swap(theirs, "dp", bits[0])
    total_f = mine_f + got_f.astype(F32)
    mine_f, theirs_f = split_rows(total_f, bits[2])
    got_f = swap(theirs_f, "dp", bits[2])

    kern_there = ordered_pair(kern_y, kern_z, 1)
    sent = jnp.concatenate([kern_there.reshape(-1, width), kern_a], axis=0)
    held = jnp.concatenate([kern_x.reshape(-1, width), kern_a], axis=0)
    grad_mod = jnp.concatenate([sums_last, sums_mid], axis=0)
    mine = grad_mod.reshape(1, -1).astype(BF16)
    mod_there, held_there = swap(mine, "mp", 1), swap(sent, "mp", 1)
    gtok = norm_back_stage(tie(grads, theirs, theirs_f, mine, sent), tok, gres, mod)

    gtok_other = swap(tie(gtok, mod_there, held_there), "mp", 1)
    got_f, got_d, mod_there, held_there = tie((got_f, got_d, mod_there, held_there), gtok)
    total_f = mine_f + got_f.astype(F32)
    for bit in bits[3:]:
        mine_f, theirs = split_rows(total_f, bit)
        total_f = mine_f + swap(theirs, "dp", bit).astype(F32)
    from_f = swap(total_f.astype(BF16), "mp", 1)
    total_d = mine_d + got_d.astype(F32)
    for bit in bits[1:]:
        mine_d, theirs = split_rows(total_d, bit)
        total_d = mine_d + swap(theirs, "dp", bit).astype(F32)
    grad_qkv = total_d[:, : 3 * share].reshape(rows, 3, share)
    grad_out = total_d[:, 3 * share :]
    from_f = from_f.reshape(2, rows, 2 * chunk)
    from_f = jnp.where(core == 0, from_f, from_f[::-1]).astype(F32)
    both_ffn = sum_x.reshape(rows, 2, 2, chunk).transpose(2, 1, 0, 3).astype(F32) + from_f.reshape(
        2, rows, 2, chunk
    ).transpose(2, 0, 1, 3)
    grad_up = both_ffn[0].transpose(1, 0, 2).reshape(rows, hidden)
    grad_down = both_ffn[1].transpose(1, 0, 2).reshape(rows, hidden)

    gathered = jnp.concatenate([mine, mod_there], axis=0)
    held = held + held_there
    step = 1
    while step < dp_size:
        if 4 * step <= dp_size:
            others = [swap(gathered, "dp", step * by) for by in (1, 2, 3)]
            gathered = jnp.concatenate([gathered, *others], axis=0)
            step *= 4
        else:
            gathered = jnp.concatenate([gathered, swap(gathered, "dp", step)], axis=0)
            step *= 2
    step = 1
    while step < dp_size:
        held = held + swap(held, "dp", step)
        step *= 2
    kern_f = held[:-9].reshape(9, hidden)
    kern_a = held[-9:]
    latents = steps.shape[0]
    order = jnp.arange(latents, dtype=jnp.int32) ^ latent.astype(jnp.int32)
    sort = (order[None, :] == jnp.arange(latents, dtype=jnp.int32)[:, None]).astype(BF16)
    grad_mod_low = jnp.dot(sort, gathered, preferred_element_type=F32).astype(BF16)

    my_cols = lax.dynamic_slice_in_dim(silu_low, dp_at * rows, rows, axis=1)
    grad_w_mod = jnp.einsum("lk,lc->kc", my_cols, grad_mod_low, preferred_element_type=F32)
    grad_silu = jnp.einsum("lc,kc->lk", grad_mod_low, w_mod, preferred_element_type=F32)
    (grad_embedding,) = silu_pull(grad_silu)

    def table_grad(indices, count):
        onehot = (jnp.arange(count, dtype=jnp.int32)[:, None] == indices[None, :]).astype(F32)
        return jnp.dot(onehot, grad_embedding, precision=lax.Precision.HIGHEST)

    return (
        whole_output,
        both(gtok, gtok_other),
        grad_w_mod,
        table_grad(steps, step_table.shape[0]),
        table_grad(labels, class_table.shape[0]),
        kern_a,
        grad_qkv,
        grad_out,
        kern_f,
        grad_up,
        grad_down,
    )


def solution(mesh):
    in_specs = (
        P("dp", None, None),
        P("dp", None),
        P(),
        P(),
        P(),
        P(),
        P(),
        P(),
        P(None, None, "mp"),
        P(None, "mp"),
        P(None, "mp"),
        P(None, "mp"),
        P(None, "mp"),
        P("dp", None, None),
    )
    out_specs = (
        P("dp", None, None),
        P("dp", None, None),
        P("dp", None),
        P(),
        P(),
        P(),
        P("dp", None, "mp"),
        P("dp", "mp"),
        P(None, "mp"),
        P("dp", "mp"),
        P("dp", "mp"),
    )
    return jax.shard_map(local, mesh=mesh, in_specs=in_specs, out_specs=out_specs, check_vma=False)
```

time: 666 us -> 390 us (0.59)
  waiting for transfers between devices: 226 us -> 23.6 us
  blocking collectives: 111 us -> 0 us
  Pallas kernels: 213 us -> 239 us
  other arithmetic: 17.7 us -> 38.1 us
  starting transfers between devices: 37.7 us -> 29.1 us
    ppermute x39 -> x31, waiting for transfers between devices: 226 us -> 23.5 us  [swap(): return lax.ppermute(values_in, axis, [(i, i ^ bit) for i in range(size)])]
    all_gather x1 -> x0, blocking collectives: 72.7 us -> none  [local(): lax.all_gather(grad_mod.reshape(1, -1).astype(BF16), ('dp', 'mp'), axis=0...]
    psum x1 -> x0, blocking collectives: 37.9 us -> none  [local(): kern_a = lax.psum(kern_a, ('dp', 'mp'))]
    pallas_call x6 -> x12, Pallas kernels: 183 us -> 207 us  [the longest x3 99.4 us: ffn_stage(): pl.pallas_call(partial(ffn_kernel, split), out_shape=(*grads, jax.ShapeDt...]
    ppermute x39 -> x31, starting transfers between devices: 37.7 us -> 29 us  [swap(): return lax.ppermute(values_in, axis, [(i, i ^ bit) for i in range(size)])]
    convert_element_type x3 -> x4, other arithmetic: 0.08 us -> 7.42 us  [the longest x1 2.83 us: local(): total_c = (c_keep + c_got.astype(F32)).astype(BF16)]
  transfers between devices with their start and end apart: 40 -> 32, of which waited for: 22 -> 7; matrix products, arithmetic and copies ran while one was open for 8% -> 16% of each run, Pallas kernels for 32% -> 62%
where the time goes in v2:
time: 390 us; the launch traced here: 382 us
  Pallas kernels  239 us (61%)
  other arithmetic  38.1 us (10%)
  starting transfers between devices  29.1 us (7%)
  local copies, waits for them, and re-layouts  24 us (6%)
  waiting for transfers between devices  23.6 us (6%)
  between operations  15.2 us (4%)
  matrix products  13.5 us (3%)
    pallas_call x3, Pallas kernels, ffn_stage(): pl.pallas_call(partial(ffn_kernel, split), out_shape=(*grads, jax.ShapeDt...  99.4 us
    ppermute x31, starting transfers between devices, swap(): return lax.ppermute(values_in, axis, [(i, i ^ bit) for i in range(size)])  29 us
    pallas_call x2, Pallas kernels, attend_back_stage(): pl.pallas_call(attend_back_kernel, out_shape=jax.ShapeDtypeStruct((length...  25.3 us
    ppermute x31, waiting for transfers between devices, swap(): return lax.ppermute(values_in, axis, [(i, i ^ bit) for i in range(size)])  23.5 us
    pallas_call x1, Pallas kernels, conv_back_stage(): pl.pallas_call(conv_back_kernel, out_shape=(jax.ShapeDtypeStruct((length,...  21.8 us
    pallas_call x1, Pallas kernels, middle_stage(): pl.pallas_call(middle_kernel, out_shape=(low, jax.ShapeDtypeStruct((lengt...  20 us
    pallas_call x1, Pallas kernels, attend_other_stage(): pl.pallas_call(attend_other_kernel, out_shape=(jax.ShapeDtypeStruct((leng...  18.9 us
    pallas_call x2, Pallas kernels, qkv_grad_stage(): pl.pallas_call(qkv_grad_kernel, out_shape=(jax.ShapeDtypeStruct(shape, F3...  14.9 us
  transfers between devices with their start and end apart: 32, of which 7 were waited for; matrix products, arithmetic and copies ran while one was open for 16% of the time, Pallas kernels for 62%

profile of v2, /device:TPU:0, one launch (start us, length us, event | category | flops | bytes accessed | tf_op | source)
XLA Modules:
  0.0 382.2 jit_solution(6457871758357267169)
XLA Ops:
  7.3 2.5 fusion.7
  9.7 2.9 collective-permute-start
  13.4 2.2 gather_fusion.1
  16.4 5.8 %modulation.1.mod_ref = f32[6,768]{1,0:T(8,128)} custom-call(bf16[1,768]{1,0:T(2,128)(2,1)} %constant_dynamic-slice_fusion.4.silu_ref, bf16[768,4608]{1,0:T(8,128)(2,1)} %weight_ref.1), custom_call_target="tpu_custom_call" | custom-call | flops 1000 | bytes 1000 | tf_op jit(solution)/shard_map/modulation/pallas_call | solution.py:140
  22.9 11.6 %norm_conv.1 = (bf16[1024,768]{1,0:T(8,128)(2,1)}, bf16[1024,768]{1,0:T(8,128)(2,1)}, bf16[1024,768]{1,0:T(8,128)(2,1)}) custom-call(s32[2]{0:T(128)} %pad_add_fusion.idx.refs_0_, bf16[2,1024,768]{2,1,0:T(8,128)(2,1)} %tok_ref.1, bf16[2,1024,768]{2,1,0:T(8,128)(2,1)} %cot_ref.1, f32[6,768]{1,0:T(8,128)} %modulation.1.mod_ref, bf16[9,768]{1,0:T(8,128)(2,1)} %kern_ref.3), custom_call_target="tpu_custom_call" | custom-call | flops 1000 | bytes 1000 | tf_op jit(solution)/shard_map/norm_conv/pallas_call | solution.py:209
  35.0 1.1 broadcast_in_dim_reshape.4.valid_ref
  36.1 1.3 fusion.5.perm_ref.refs_1_
  37.4 14.3 %attend_own.1 = (bf16[768,1024]{1,0:T(8,128)(2,1)}, bf16[1024,1152]{1,0:T(8,128)(2,1)}, bf16[1024,384]{1,0:T(8,128)(2,1)}) custom-call(bf16[1024,768]{1,0:T(8,128)(2,1)} %get-tuple-element.81.conv_ref, s32[4,256,1]{2,1,0:T(8,128)} %broadcast_in_dim_reshape.4.valid_ref, bf16[3,768,384]{2,1,0:T(8,128)(2,1)} %bitcast.80, bf16[768,768]{1,0:T(8,128)(2,1)} %fusion.5.perm_ref.refs_1_), custom_call_target="tpu_custom_call" | custom-call | flops 1000 | bytes 1000 | tf_op jit(solution)/shard_map/attend_own/pallas_call | solution.py:287
  51.7 1.3 dynamic-slice_bitcast_fusion.1
  53.1 1.4 dynamic-slice_bitcast_fusion
  54.4 1.7 pad_maximum_fusion
  56.2 1.1 fusion.6.refs_1_
  57.3 1.9 collective-permute-done.1
  59.1 1.6 broadcast_select_fusion.3
  60.7 1.6 pad_maximum_fusion.1.weight_ref.ob_ref.wb_ref
  62.4 18.9 %attend_other.1 = (bf16[1024,1152]{1,0:T(8,128)(2,1)}, bf16[1024,384]{1,0:T(8,128)(2,1)}, f32[1024,768]{1,0:T(8,128)}, f32[1024,768]{1,0:T(8,128)}, bf16[1024,76...) custom-call(bf16[1024,768]{1,0:T(8,128)(2,1)} %get-tuple-element.81.conv_ref, s32[4,256,1]{2,1,0:T(8,128)} %broadcast_in_dim_reshape.4.valid_ref, ...), custom_call_target="tpu_custom_call" | custom-call | flops 1000 | bytes 1000 | tf_op jit(solution)/shard_map/attend_other/pallas_call | solution.py:317
  81.3 46.9 %ffn.3 = (bf16[768,3072]{1,0:T(8,128)(2,1)}, f32[9,1536]{1,0:T(8,128)}, f32[1024,768]{1,0:T(8,128)}, f32[1024,768]{1,0:T(8,128)}) custom-call(s32[2]{0:T(128)} %pad_add_fusion.idx.refs_0_, bf16[768,768]{1,0:T(8,128)(2,1)} %fusion.6.refs_1_, bf16[1024,768]{1,0:T(8,128)(2,1)} %get-tuple-element.91.refs_2_, bf16[1024,768]{1,0:T(8,128)(2,1)} %get-tuple-element.87.refs_3_, ...), custom_call_target="tpu_custom_call" | custom-call | flops 1000 | bytes 1000 | tf_op jit(solution)/shard_map/ffn/pallas_call | solution.py:467
  128.4 2.0 collective-permute-start.3
  130.5 2.3 collective-permute-done.3
  133.4 26.5 %ffn.4 = (f32[384,1536]{1,0:T(8,128)}, bf16[384,1536]{1,0:T(8,128)(2,1)}, f32[9,768]{1,0:T(8,128)}, f32[1024,768]{1,0:T(8,128)}, f32[1024,768]{1,0:T(8,128)}) custom-call(s32[2]{0:T(128)} %pad_add_fusion.idx.refs_0_, bf16[768,768]{1,0:T(8,128)(2,1)} %fusion.5.perm_ref.refs_1_, bf16[1024,768]{1,0:T(8,128)(2,1)} %get-tuple-element.91.refs_2_, ...), custom_call_target="tpu_custom_call" | custom-call | flops 1000 | bytes 1000 | tf_op jit(solution)/shard_map/ffn/pallas_call | solution.py:467
  159.8 26.0 %ffn.5 = (f32[384,1536]{1,0:T(8,128)}, bf16[384,1536]{1,0:T(8,128)(2,1)}, f32[9,768]{1,0:T(8,128)}, f32[1024,768]{1,0:T(8,128)}, f32[1024,768]{1,0:T(8,128)}) custom-call(s32[2]{0:T(128)} %pad_add_fusion.idx.refs_0_, bf16[768,768]{1,0:T(8,128)(2,1)} %fusion.5.perm_ref.refs_1_, bf16[1024,768]{1,0:T(8,128)(2,1)} %get-tuple-element.91.refs_2_, ...), custom_call_target="tpu_custom_call" | custom-call | flops 1000 | bytes 1000 | tf_op jit(solution)/shard_map/ffn/pallas_call | solution.py:467
  186.4 20.0 %middle.1 = (bf16[1024,768]{1,0:T(8,128)(2,1)}, f32[1024,768]{1,0:T(8,128)}, bf16[1024,768]{1,0:T(8,128)(2,1)}, f32[4,768]{1,0:T(4,128)}, f32[384,768]{1,0:T(8,128)}, /*index=5*/bf16[384,768]{1,0:T(8,128)(2,1)}) custom-call(s32[2]{0:T(128)} %pad_add_fusion.idx.refs_0_, bf16[768,768]{1,0:T(8,128)(2,1)} %fusion.5.perm_ref.refs_1_, ...), custom_call_target="tpu_custom_call" | custom-call | flops 1000 | bytes 1000 | tf_op jit(solution)/shard_map/middle/pallas_call | solution.py:564
  206.5 1.8 convert_add_fusion.2
  209.7 1.2 fusion.8
  210.9 1.8 collective-permute-start.9
  212.7 12.5 %attend_back.2.gqkv_ref.gb_ref = bf16[1024,1152]{1,0:T(8,128)(2,1)} custom-call(bf16[1024,1152]{1,0:T(8,128)(2,1)} %get-tuple-element.110.qkv_ref, bf16[1024,768]{1,0:T(8,128)(2,1)} %get-tuple-element.114.gmix_ref, s32[4,256,1]{2,1,0:T(8,128)} %broadcast_in_dim_reshape.4.valid_ref), custom_call_target="tpu_custom_call" | custom-call | flops 1000 | bytes 1000 | tf_op jit(solution)/shard_map/attend_back/pallas_call | solution.py:629
  225.2 7.4 %qkv_grad.2 = (f32[384,1536]{1,0:T(8,128)}, bf16[384,1536]{1,0:T(8,128)(2,1)}) custom-call(s32[2]{0:T(128)} %pad_add_fusion.idx.refs_0_, bf16[768,1024]{1,0:T(8,128)(2,1)} %get-tuple-element.109.conv_ref, bf16[1024,1152]{1,0:T(8,128)(2,1)} %attend_back.2.gqkv_ref.gb_ref, f32[384,768]{1,0:T(8,128)} %get-tuple-element.111.okeep_ref, ...), custom_call_target="tpu_custom_call" | custom-call | flops 1000 | bytes 1000 | tf_op jit(solution)/shard_map/qkv_grad/pallas_call | solution.py:665
  232.6 1.5 collective-permute-start.7
  234.1 12.8 %attend_back.3.gqkv_ref.ga_ref = bf16[1024,1152]{1,0:T(8,128)(2,1)} custom-call(bf16[1024,1152]{1,0:T(8,128)(2,1)} %get-tuple-element.107.qkv_ref, bf16[1024,768]{1,0:T(8,128)(2,1)} %get-tuple-element.114.gmix_ref, s32[4,256,1]{2,1,0:T(8,128)} %broadcast_in_dim_reshape.4.valid_ref), custom_call_target="tpu_custom_call" | custom-call | flops 1000 | bytes 1000 | tf_op jit(solution)/shard_map/attend_back/pallas_call | solution.py:629
  247.0 4.8 %collective-permute-done.9 = bf16[2,192,1536]{2,1,0:T(8,128)(2,1)S(1)} collective-permute-done((bf16[2,192,1536]{2,1,0:T(8,128)(2,1)}, bf16[2,192,1536]{2,1,0:T(8,128)(2,1)S(1)}, u32[]{:S(2)}, u32[]{:S(2)}) %collective-permute-start.9) | collective-permute-done | bytes 1179680 | tf_op jit(solution)/shard_map/ppermute | solution.py:809
  251.8 1.0 copy-done.16
  252.8 2.8 add_convert_fusion
  255.6 1.7 collective-permute-start.11
  257.3 1.6 fusion.2
  259.0 1.4 copy-done.7
  261.3 7.5 %qkv_grad.3 = (f32[384,1536]{1,0:T(8,128)}, bf16[384,1536]{1,0:T(8,128)(2,1)}) custom-call(s32[2]{0:T(128)} %pad_add_fusion.idx.refs_0_, bf16[768,1024]{1,0:T(8,128)(2,1)} %get-tuple-element.109.conv_ref, bf16[1024,1152]{1,0:T(8,128)(2,1)} %attend_back.3.gqkv_ref.ga_ref, f32[384,768]{1,0:T(8,128)} %get-tuple-element.111.okeep_ref, ...), custom_call_target="tpu_custom_call" | custom-call | flops 1000 | bytes 1000 | tf_op jit(solution)/shard_map/qkv_grad/pallas_call | solution.py:665
  268.9 2.6 collective-permute-start.12
  271.6 3.9 %broadcast_select_fusion.1 = bf16[2,1024,768]{2,1,0:T(8,128)(2,1)} fusion(pred[2]{0:T(512)(128)(4,1)S(1)} %iota_compare_fusion.8, bf16[1024,768]{1,0:T(8,128)(2,1)} %collective-permute-done.7, bf16[1024,768]{1,0:T(8,128)(2,1)} %get-tuple-element.106), kind=kLoop, calls=%fused_computation.8 | loop fusion | flops 1572864 | bytes 6291458 | tf_op jit(solution)/shard_map/jit(_where)/select_n | solution.py:893
  275.5 21.8 %conv_back.1 = (f32[1024,768]{1,0:T(8,128)}, f32[9,768]{1,0:T(8,128)}, f32[2,768]{1,0:T(2,128)}) custom-call(bf16[1024,1152]{1,0:T(8,128)(2,1)} %attend_back.3.gqkv_ref.ga_ref, bf16[1024,1152]{1,0:T(8,128)(2,1)} %attend_back.2.gqkv_ref.gb_ref, bf16[3,768,384]{2,1,0:T(8,128)(2,1)} %bitcast.81, ...), custom_call_target="tpu_custom_call" | custom-call | flops 1000 | bytes 1000 | tf_op jit(solution)/shard_map/conv_back/pallas_call | solution.py:746
  299.7 1.4 collective-permute-start.14
  301.1 1.9 convert_add_fusion
  303.1 1.6 collective-permute-start.17
  304.7 1.2 bitcast_add_fusion.1
  306.0 1.0 copy.47
  307.0 1.5 collective-permute-start.16
  308.6 6.5 %norm_back.1 = bf16[1024,768]{1,0:T(8,128)(2,1)} custom-call(f32[1024,768]{1,0:T(8,128)} %get-tuple-element.131.grads_ref, bf16[1024,768]{1,0:T(8,128)(2,1)} %get-tuple-element.82.tok_ref, f32[1024,768]{1,0:T(8,128)} %get-tuple-element.132.gres_ref, f32[6,768]{1,0:T(8,128)} %modulation.1.mod_ref), custom_call_target="tpu_custom_call" | custom-call | flops 1000 | bytes 1000 | tf_op jit(solution)/shard_map/norm_back/pallas_call | solution.py:790
  315.9 1.5 reshape.120
  318.3 1.6 collective-permute-start.19
  320.2 1.6 bitcast_add_fusion
  323.0 2.3 fusion.11
  325.4 1.9 collective-permute-start.23
  327.4 1.2 collective-permute-start.22
  328.5 1.4 collective-permute-start.21
  330.4 2.1 collective-permute-done.23
  333.5 9.1 %collective-permute-done.22 = bf16[8,4608]{1,0:T(8,128)(2,1)S(1)} collective-permute-done((bf16[8,4608]{1,0:T(8,128)(2,1)S(1)}, bf16[8,4608]{1,0:T(8,128)(2,1)S(1)}, u32[]{:S(2)}, u32[]{:S(2)}) %collective-permute-start.22) | collective-permute-done | bytes 73760 | tf_op jit(solution)/shard_map/ppermute | solution.py:809
  342.7 1.3 collective-permute-start.25
  344.3 5.1 %fusion.30 = f32[32,768]{1,0:T(8,128)S(1)} fusion(bf16[32,4608]{1,0:T(8,128)(2,1)S(1)} %convolution_convert_fusion, bf16[768,4608]{1,0:T(8,128)(2,1)} %weight_ref.1), kind=kOutput, calls=%fused_computation.95 | convolution fusion | flops 226492416 | bytes 7471104 | tf_op jit(solution)/shard_map/lc,kc->lk/dot_general | solution.py:1037
  349.4 3.1 fusion.13
  352.5 3.1 fusion.12
  355.7 2.0 fusion.23
  357.7 2.6 collective-permute-done.26
  360.4 1.0 bitcast_add_fusion.4
  362.3 1.7 rev.3
  371.2 3.6 broadcast_select_fusion
  (153 shorter events, 22.1 us)
Async XLA Ops:
  7.2 5.5 %copy-start = (bf16[1000,768]{1,0:T(8,128)(2,1)S(1)}, bf16[1000,768]{1,0:T(8,128)(2,1)}, u32[]{:S(2)}) copy-start(bf16[1000,768]{1,0:T(8,128)(2,1)} %param.22) | copy-start | bytes 4608004
  7.2 5.5 %copy-start.24 = (s32[32]{0:T(128)S(1)}, s32[32]{0:T(128)}, u32[]{:S(2)}) copy-start(s32[32]{0:T(128)} %param.20) | copy-start | bytes 388
  7.2 5.5 %copy-start.25 = (s32[32]{0:T(128)S(1)}, s32[32]{0:T(128)}, u32[]{:S(2)}) copy-start(s32[32]{0:T(128)} %param.19) | copy-start | bytes 388
  7.2 308.7 %reduce-scatter.2.cloned.1.call-start = ((), (), s32[]{:S(2)}) async-start(), calls=%async_computation.1 | async-start | bytes 5013504 | tf_op jit(solution)/shard_map/reduce_scatter | solution.py:933
  9.7 42.0 %collective-permute-start = (bf16[4,384,384]{2,1,0:T(8,128)(2,1)}, bf16[4,384,384]{2,1,0:T(8,128)(2,1)S(1)}, u32[]{:S(2)}, u32[]{:S(2)}) collective-permute-start(bf16[4,384,384]{2,1,0:T(8,128)(2,1)} %fusion.7), channel_id=1, source_target_pairs={{0,1},{1,0},{2,3},{3,2},{4,5},{5,4},{6,7},{7,6},{8,9},{9,8},{10,11... | collective-permute-start | bytes 3538952 | tf_op jit(solution)/shard_map/ppermute | solution.py:809
  15.8 6.4 %copy-start.19 = (bf16[32,768]{1,0:T(8,128)(2,1)}, bf16[32,768]{1,0:T(8,128)(2,1)S(1)}, u32[]{:S(2)}) copy-start(bf16[32,768]{1,0:T(8,128)(2,1)S(1)} %multiply_convert_fusion) | copy-start | bytes 147460
  22.9 11.6 %copy-start.27 = (s32[2,1024]{1,0:T(2,128)S(1)}, s32[2,1024]{1,0:T(2,128)}, u32[]{:S(2)}) copy-start(s32[2,1024]{1,0:T(2,128)} %param.18) | copy-start | bytes 24580
  22.9 13.2 %copy-start.26 = (s32[768]{0:T(1024)S(1)}, s32[768]{0:T(1024)}, u32[]{:S(2)}) copy-start(s32[768]{0:T(1024)} %constant.147.clone) | copy-start | bytes 9220
  56.1 72.1 %collective-permute-start.2 = (bf16[2,768,768]{2,1,0:T(8,128)(2,1)}, bf16[2,768,768]{2,1,0:T(8,128)(2,1)}, u32[]{:S(2)}, u32[]{:S(2)}) collective-permute-start(bf16[2,768,768]{2,1,0:T(8,128)(2,1)} %pad_maximum_fusion), channel_id=1, source_target_pairs={{0,1},{1,0},{2,3},{3,2},{4,5},{5,4},{6,7},{7,6},{8,9},{9,8},{10,11... | collective-permute-start | bytes 7077896 | tf_op jit(solution)/shard_map/ppermute | solution.py:809
  56.2 3.0 collective-permute-start.1
  81.3 47.2 %copy-start.20 = (bf16[9,1536]{1,0:T(8,128)(2,1)S(1)}, bf16[9,1536]{1,0:T(8,128)(2,1)}, u32[]{:S(2)}) copy-start(bf16[9,1536]{1,0:T(8,128)(2,1)} %refs_6_.1) | copy-start | bytes 82948
  128.2 31.6 %collective-permute-start.4 = (bf16[2,768,768]{2,1,0:T(8,128)(2,1)}, bf16[2,768,768]{2,1,0:T(8,128)(2,1)}, u32[]{:S(2)}, u32[]{:S(2)}) collective-permute-start(bf16[2,768,768]{2,1,0:T(8,128)(2,1)} %collective-permute-done.2.refs_4_.refs_5_), channel_id=1, source_target_pairs={{0,2},{2,0},{4,6},{6,4},{8,10},{10,8},{12,14},{14,12},{16,18},{18,... | collective-permute-start | bytes 7077896 | tf_op jit(solution)/shard_map/ppermute | solution.py:809
  128.4 4.3 %collective-permute-start.3 = (bf16[9,1536]{1,0:T(8,128)(2,1)S(1)}, bf16[9,1536]{1,0:T(8,128)(2,1)S(1)}, u32[]{:S(2)}, u32[]{:S(2)}) collective-permute-start(bf16[9,1536]{1,0:T(8,128)(2,1)S(1)} %copy-done.20), channel_id=1, source_target_pairs={{0,1},{1,0},{2,3},{3,2},{4,5},{5,4},{6,7},{7,6},{8,9},{9,8},{10,11... | collective-permute-start | bytes 82952 | tf_op jit(solution)/shard_map/ppermute | solution.py:809
  159.8 26.6 %collective-permute-start.5 = (bf16[384,1536]{1,0:T(8,128)(2,1)}, bf16[384,1536]{1,0:T(8,128)(2,1)S(1)}, u32[]{:S(2)}, u32[]{:S(2)}) collective-permute-start(bf16[384,1536]{1,0:T(8,128)(2,1)} %get-tuple-element.96), channel_id=1, source_target_pairs={{0,2},{2,0},{4,6},{6,4},{8,10},{10,8},{12,14},{14,12},{16,18},{18,... | collective-permute-start | bytes 3538952 | tf_op jit(solution)/shard_map/ppermute | solution.py:809
  185.8 20.6 %collective-permute-start.6 = (bf16[384,1536]{1,0:T(8,128)(2,1)}, bf16[384,1536]{1,0:T(8,128)(2,1)}, u32[]{:S(2)}, u32[]{:S(2)}) collective-permute-start(bf16[384,1536]{1,0:T(8,128)(2,1)} %get-tuple-element.101), channel_id=1, source_target_pairs={{0,2},{2,0},{4,6},{6,4},{8,10},{10,8},{12,14},{14,12},{16,18},{18,... | collective-permute-start | bytes 3538952 | tf_op jit(solution)/shard_map/ppermute | solution.py:809
  186.4 20.1 %copy-start.12 = (f32[384,1536]{1,0:T(8,128)S(1)}, f32[384,1536]{1,0:T(8,128)}, u32[]{:S(2)}) copy-start(f32[384,1536]{1,0:T(8,128)} %get-tuple-element.100) | copy-start | bytes 7077892
  206.4 2.2 copy-start.13
  208.3 1.4 copy-start.2
  209.0 1.9 copy-start.4
  210.9 40.9 %collective-permute-start.9 = (bf16[2,192,1536]{2,1,0:T(8,128)(2,1)}, bf16[2,192,1536]{2,1,0:T(8,128)(2,1)S(1)}, u32[]{:S(2)}, u32[]{:S(2)}) collective-permute-start(bf16[2,192,1536]{2,1,0:T(8,128)(2,1)} %fusion.8), channel_id=1, source_target_pairs={{0,4},{2,6},{4,0},{6,2},{8,12},{10,14},{12,8},{14,10},{16,20},{18,... | collective-permute-start | bytes 3538952 | tf_op jit(solution)/shard_map/ppermute | solution.py:809
  232.6 19.1 %collective-permute-start.8 = (bf16[384,1536]{1,0:T(8,128)(2,1)}, bf16[384,1536]{1,0:T(8,128)(2,1)}, u32[]{:S(2)}, u32[]{:S(2)}) collective-permute-start(bf16[384,1536]{1,0:T(8,128)(2,1)} %get-tuple-element.113), channel_id=1, source_target_pairs={{0,2},{2,0},{4,6},{6,4},{8,10},{10,8},{12,14},{14,12},{16,18},{18,... | collective-permute-start | bytes 3538952 | tf_op jit(solution)/shard_map/ppermute | solution.py:809
  232.6 38.9 %collective-permute-start.7 = (bf16[1024,768]{1,0:T(8,128)(2,1)}, bf16[1024,768]{1,0:T(8,128)(2,1)}, u32[]{:S(2)}, u32[]{:S(2)}) collective-permute-start(bf16[1024,768]{1,0:T(8,128)(2,1)} %get-tuple-element.106), channel_id=1, source_target_pairs={{0,1},{1,0},{2,3},{3,2},{4,5},{5,4},{6,7},{7,6},{8,9},{9,8},{10,11... | collective-permute-start | bytes 4718600 | tf_op jit(solution)/shard_map/ppermute | solution.py:809
  234.1 18.6 %copy-start.11 = (f32[384,1536]{1,0:T(8,128)S(1)}, f32[384,1536]{1,0:T(8,128)}, u32[]{:S(2)}) copy-start(f32[384,1536]{1,0:T(8,128)} %get-tuple-element.115) | copy-start | bytes 7077892
  251.8 1.0 copy-start.16
  252.8 4.6 %copy-start.3 = (f32[384,1536]{1,0:T(8,128)S(1)}, f32[384,1536]{1,0:T(8,128)}, u32[]{:S(2)}) copy-start(f32[384,1536]{1,0:T(8,128)} %copy-done.2) | copy-start | bytes 7077892
  252.8 4.6 %copy-start.5 = (f32[384,1536]{1,0:T(8,128)S(1)}, f32[384,1536]{1,0:T(8,128)}, u32[]{:S(2)}) copy-start(f32[384,1536]{1,0:T(8,128)} %copy-done.4) | copy-start | bytes 7077892
  255.6 45.5 %collective-permute-start.11 = (bf16[384,1536]{1,0:T(8,128)(2,1)}, bf16[384,1536]{1,0:T(8,128)(2,1)S(1)}, u32[]{:S(2)}, u32[]{:S(2)}) collective-permute-start(bf16[384,1536]{1,0:T(8,128)(2,1)} %add_convert_fusion), channel_id=1, source_target_pairs={{0,1},{1,0},{2,3},{3,2},{4,5},{5,4},{6,7},{7,6},{8,9},{9,8},{10,11... | collective-permute-start | bytes 3538952 | tf_op jit(solution)/shard_map/ppermute | solution.py:809
  259.0 1.5 copy-start.7
  261.3 7.5 %copy-start.23 = (f32[4,768]{1,0:T(4,128)S(1)}, f32[4,768]{1,0:T(4,128)}, u32[]{:S(2)}) copy-start(f32[4,768]{1,0:T(4,128)} %get-tuple-element.127) | copy-start | bytes 36868
  261.3 7.6 %copy-start.21 = (f32[9,768]{1,0:T(8,128)S(1)}, f32[9,768]{1,0:T(8,128)}, u32[]{:S(2)}) copy-start(f32[9,768]{1,0:T(8,128)} %get-tuple-element.128) | copy-start | bytes 82948
  261.3 7.6 %copy-start.22 = (f32[9,768]{1,0:T(8,128)S(1)}, f32[9,768]{1,0:T(8,128)}, u32[]{:S(2)}) copy-start(f32[9,768]{1,0:T(8,128)} %get-tuple-element.129) | copy-start | bytes 82948
  268.8 32.2 %collective-permute-start.10 = (bf16[384,1536]{1,0:T(8,128)(2,1)}, bf16[384,1536]{1,0:T(8,128)(2,1)}, u32[]{:S(2)}, u32[]{:S(2)}) collective-permute-start(bf16[384,1536]{1,0:T(8,128)(2,1)} %get-tuple-element.119), channel_id=1, source_target_pairs={{0,2},{2,0},{4,6},{6,4},{8,10},{10,8},{12,14},{14,12},{16,18},{18,... | collective-permute-start | bytes 3538952 | tf_op jit(solution)/shard_map/ppermute | solution.py:809
  268.9 32.1 %collective-permute-start.12 = (bf16[2,96,1536]{2,1,0:T(8,128)(2,1)}, bf16[2,96,1536]{2,1,0:T(8,128)(2,1)}, u32[]{:S(2)}, u32[]{:S(2)}) collective-permute-start(bf16[2,96,1536]{2,1,0:T(8,128)(2,1)} %fusion.9), channel_id=1, source_target_pairs={{0,16},{2,18},{4,20},{6,22},{8,24},{10,26},{12,28},{14,30},{16,0},... | collective-permute-start | bytes 1769480 | tf_op jit(solution)/shard_map/ppermute | solution.py:809
  275.5 25.6 %copy-start.10 = (f32[384,1536]{1,0:T(8,128)S(1)}, f32[384,1536]{1,0:T(8,128)}, u32[]{:S(2)}) copy-start(f32[384,1536]{1,0:T(8,128)} %get-tuple-element.122) | copy-start | bytes 7077892
  298.1 16.9 %collective-permute-start.13 = (bf16[1,4608]{1,0:T(2,128)(2,1)S(1)}, bf16[1,4608]{1,0:T(2,128)(2,1)S(1)}, u32[]{:S(2)}, u32[]{:S(2)}) collective-permute-start(bf16[1,4608]{1,0:T(2,128)(2,1)S(1)} %bitcast.97), channel_id=1, source_target_pairs={{0,1},{1,0},{2,3},{3,2},{4,5},{5,4},{6,7},{7,6},{8,9},{9,8},{10,11... | collective-permute-start | bytes 27656 | tf_op jit(solution)/shard_map/ppermute | solution.py:809
  299.7 15.4 %collective-permute-start.14 = (f32[27,768]{1,0:T(8,128)S(1)}, f32[27,768]{1,0:T(8,128)}, u32[]{:S(2)}, u32[]{:S(2)}) collective-permute-start(f32[27,768]{1,0:T(8,128)S(1)} %pad_maximum_fusion.3), channel_id=1, source_target_pairs={{0,1},{1,0},{2,3},{3,2},{4,5},{5,4},{6,7},{7,6},{8,9},{9,8},{10,11... | collective-permute-start | bytes 248840 | tf_op jit(solution)/shard_map/ppermute | solution.py:809
  301.1 3.7 copy-start.8
  303.0 2.9 copy-start.6
  303.1 5.4 %copy-start.18 = (f32[9,1536]{1,0:T(8,128)S(1)}, f32[9,1536]{1,0:T(8,128)}, u32[]{:S(2)}) copy-start(f32[9,1536]{1,0:T(8,128)} %get-tuple-element.135) | copy-start | bytes 165892
  303.1 15.0 %collective-permute-start.17 = (bf16[192,1536]{1,0:T(8,128)(2,1)S(1)}, bf16[192,1536]{1,0:T(8,128)(2,1)}, u32[]{:S(2)}, u32[]{:S(2)}) collective-permute-start(bf16[192,1536]{1,0:T(8,128)(2,1)S(1)} %fusion.10), channel_id=1, source_target_pairs={{0,4},{2,6},{4,0},{6,2},{8,12},{10,14},{12,8},{14,10},{16,20},{18,... | collective-permute-start | bytes 1769480 | tf_op jit(solution)/shard_map/ppermute | solution.py:809
  307.0 10.4 %collective-permute-start.16 = (bf16[2,48,1536]{2,0,1:T(2,128)(2,1)}, bf16[2,48,1536]{2,0,1:T(2,128)(2,1)}, u32[]{:S(2)}, u32[]{:S(2)}) collective-permute-start(bf16[2,48,1536]{2,0,1:T(2,128)(2,1)} %bitcast.73), channel_id=1, source_target_pairs={{0,8},{2,10},{4,12},{6,14},{8,0},{10,2},{12,4},{14,6},{16,24},{18,... | collective-permute-start | bytes 884744 | tf_op jit(solution)/shard_map/ppermute | solution.py:809
  315.0 6.7 %copy-start.17 = (f32[9,768]{1,0:T(8,128)S(1)}, f32[9,768]{1,0:T(8,128)}, u32[]{:S(2)}) copy-start(f32[9,768]{1,0:T(8,128)} %get-tuple-element.130) | copy-start | bytes 82948
  315.1 56.2 %collective-permute-start.15 = (bf16[1024,768]{1,0:T(8,128)(2,1)}, bf16[1024,768]{1,0:T(8,128)(2,1)}, u32[]{:S(2)}, u32[]{:S(2)}) collective-permute-start(bf16[1024,768]{1,0:T(8,128)(2,1)} %norm_back.1), channel_id=1, source_target_pairs={{0,1},{1,0},{2,3},{3,2},{4,5},{5,4},{6,7},{7,6},{8,9},{9,8},{10,11... | collective-permute-start | bytes 4718600 | tf_op jit(solution)/shard_map/ppermute | solution.py:809
  318.2 7.0 %collective-permute-start.20 = (bf16[2,4608]{1,0:T(2,128)(2,1)S(1)}, bf16[2,4608]{1,0:T(2,128)(2,1)S(1)}, u32[]{:S(2)}, u32[]{:S(2)}) collective-permute-start(bf16[2,4608]{1,0:T(2,128)(2,1)S(1)} %pad_maximum_fusion.5), channel_id=1, source_target_pairs={{0,6},{2,4},{4,2},{6,0},{8,14},{10,12},{12,10},{14,8},{16,22},{18,... | collective-permute-start | bytes 55304 | tf_op jit(solution)/shard_map/ppermute | solution.py:809
  318.3 7.0 %collective-permute-start.19 = (bf16[2,4608]{1,0:T(2,128)(2,1)S(1)}, bf16[2,4608]{1,0:T(2,128)(2,1)S(1)}, u32[]{:S(2)}, u32[]{:S(2)}) collective-permute-start(bf16[2,4608]{1,0:T(2,128)(2,1)S(1)} %pad_maximum_fusion.5), channel_id=1, source_target_pairs={{0,4},{2,6},{4,0},{6,2},{8,12},{10,14},{12,8},{14,10},{16,20},{18,... | collective-permute-start | bytes 55304 | tf_op jit(solution)/shard_map/ppermute | solution.py:809
  319.9 5.4 %collective-permute-start.18 = (bf16[2,4608]{1,0:T(2,128)(2,1)S(1)}, bf16[2,4608]{1,0:T(2,128)(2,1)S(1)}, u32[]{:S(2)}, u32[]{:S(2)}) collective-permute-start(bf16[2,4608]{1,0:T(2,128)(2,1)S(1)} %pad_maximum_fusion.5), channel_id=1, source_target_pairs={{0,2},{2,0},{4,6},{6,4},{8,10},{10,8},{12,14},{14,12},{16,18},{18,... | collective-permute-start | bytes 55304 | tf_op jit(solution)/shard_map/ppermute | solution.py:809
  322.7 7.2 %collective-permute-start.24 = (f32[27,768]{1,0:T(8,128)S(1)}, f32[27,768]{1,0:T(8,128)S(1)}, u32[]{:S(2)}, u32[]{:S(2)}) collective-permute-start(f32[27,768]{1,0:T(8,128)S(1)} %fusion.19), channel_id=1, source_target_pairs={{0,2},{2,0},{4,6},{6,4},{8,10},{10,8},{12,14},{14,12},{16,18},{18,... | collective-permute-start | bytes 248840 | tf_op jit(solution)/shard_map/ppermute | solution.py:809
  325.4 7.1 %collective-permute-start.23 = (bf16[8,4608]{1,0:T(8,128)(2,1)S(1)}, bf16[8,4608]{1,0:T(8,128)(2,1)S(1)}, u32[]{:S(2)}, u32[]{:S(2)}) collective-permute-start(bf16[8,4608]{1,0:T(8,128)(2,1)S(1)} %concatenate.37), channel_id=1, source_target_pairs={{0,24},{2,26},{4,28},{6,30},{8,16},{10,18},{12,20},{14,22},{16,8},... | collective-permute-start | bytes 221192 | tf_op jit(solution)/shard_map/ppermute | solution.py:809
  327.4 15.3 %collective-permute-start.22 = (bf16[8,4608]{1,0:T(8,128)(2,1)S(1)}, bf16[8,4608]{1,0:T(8,128)(2,1)S(1)}, u32[]{:S(2)}, u32[]{:S(2)}) collective-permute-start(bf16[8,4608]{1,0:T(8,128)(2,1)S(1)} %concatenate.37), channel_id=1, source_target_pairs={{0,16},{2,18},{4,20},{6,22},{8,24},{10,26},{12,28},{14,30},{16,0},... | collective-permute-start | bytes 221192 | tf_op jit(solution)/shard_map/ppermute | solution.py:809
  328.5 15.4 %collective-permute-start.21 = (bf16[8,4608]{1,0:T(8,128)(2,1)S(1)}, bf16[8,4608]{1,0:T(8,128)(2,1)S(1)}, u32[]{:S(2)}, u32[]{:S(2)}) collective-permute-start(bf16[8,4608]{1,0:T(8,128)(2,1)S(1)} %concatenate.37), channel_id=1, source_target_pairs={{0,8},{2,10},{4,12},{6,14},{8,0},{10,2},{12,4},{14,6},{16,24},{18,... | collective-permute-start | bytes 221192 | tf_op jit(solution)/shard_map/ppermute | solution.py:809
  329.9 30.4 %collective-permute-start.28 = (bf16[96,1536]{1,0:T(8,128)(2,1)S(1)}, bf16[96,1536]{1,0:T(8,128)(2,1)}, u32[]{:S(2)}, u32[]{:S(2)}) collective-permute-start(bf16[96,1536]{1,0:T(8,128)(2,1)S(1)} %fusion.15), channel_id=1, source_target_pairs={{0,16},{2,18},{4,20},{6,22},{8,24},{10,26},{12,28},{14,30},{16,0},... | collective-permute-start | bytes 884744 | tf_op jit(solution)/shard_map/ppermute | solution.py:809
  332.5 29.8 %collective-permute-start.30 = (bf16[2,48,1536]{2,0,1:T(2,128)(2,1)}, bf16[2,48,1536]{2,0,1:T(2,128)(2,1)S(1)}, u32[]{:S(2)}, u32[]{:S(2)}) collective-permute-start(bf16[2,48,1536]{2,0,1:T(2,128)(2,1)} %fusion.11), channel_id=1, source_target_pairs={{0,1},{1,0},{2,3},{3,2},{4,5},{5,4},{6,7},{7,6},{8,9},{9,8},{10,11... | collective-permute-start | bytes 884744 | tf_op jit(solution)/shard_map/ppermute | solution.py:809
  342.7 12.9 %collective-permute-start.25 = (f32[27,768]{1,0:T(8,128)S(1)}, f32[27,768]{1,0:T(8,128)S(1)}, u32[]{:S(2)}, u32[]{:S(2)}) collective-permute-start(f32[27,768]{1,0:T(8,128)S(1)} %add.168), channel_id=1, source_target_pairs={{0,4},{2,6},{4,0},{6,2},{8,12},{10,14},{12,8},{14,10},{16,20},{18,... | collective-permute-start | bytes 248840 | tf_op jit(solution)/shard_map/ppermute | solution.py:809
  355.6 4.7 %collective-permute-start.26 = (f32[27,768]{1,0:T(8,128)S(1)}, f32[27,768]{1,0:T(8,128)S(1)}, u32[]{:S(2)}, u32[]{:S(2)}) collective-permute-start(f32[27,768]{1,0:T(8,128)S(1)} %add.169), channel_id=1, source_target_pairs={{0,8},{2,10},{4,12},{6,14},{8,0},{10,2},{12,4},{14,6},{16,24},{18,... | collective-permute-start | bytes 248840 | tf_op jit(solution)/shard_map/ppermute | solution.py:809
  360.3 7.3 %collective-permute-start.27 = (f32[27,768]{1,0:T(8,128)S(1)}, f32[27,768]{1,0:T(8,128)}, u32[]{:S(2)}, u32[]{:S(2)}) collective-permute-start(f32[27,768]{1,0:T(8,128)S(1)} %add.170), channel_id=1, source_target_pairs={{0,16},{2,18},{4,20},{6,22},{8,24},{10,26},{12,28},{14,30},{16,0},... | collective-permute-start | bytes 248840 | tf_op jit(solution)/shard_map/ppermute | solution.py:809
  361.4 0.8 copy-start.14
  362.3 7.6 %collective-permute-start.29 = (bf16[48,1536]{1,0:T(8,128)(2,1)S(1)}, bf16[48,1536]{1,0:T(8,128)(2,1)S(1)}, u32[]{:S(2)}, u32[]{:S(2)}) collective-permute-start(bf16[48,1536]{1,0:T(8,128)(2,1)S(1)} %fusion.18), channel_id=1, source_target_pairs={{0,8},{2,10},{4,12},{6,14},{8,0},{10,2},{12,4},{14,6},{16,24},{18,... | collective-permute-start | bytes 442376 | tf_op jit(solution)/shard_map/ppermute | solution.py:809
  365.3 4.5 %copy-start.15 = (f32[96,1536]{1,0:T(8,128)S(1)}, f32[96,1536]{1,0:T(8,128)}, u32[]{:S(2)}) copy-start(f32[96,1536]{1,0:T(8,128)} %copy-done.14) | copy-start | bytes 1769476
  365.8 5.4 %copy-start.9 = (bf16[1024,768]{1,0:T(8,128)(2,1)S(1)}, bf16[1024,768]{1,0:T(8,128)(2,1)}, u32[]{:S(2)}) copy-start(bf16[1024,768]{1,0:T(8,128)(2,1)} %norm_back.1) | copy-start | bytes 4718596
  370.5 4.4 %copy-start.1 = (bf16[1000,768]{1,0:T(8,128)(2,1)S(1)}, bf16[1000,768]{1,0:T(8,128)(2,1)}, u32[]{:S(2)}) copy-start(bf16[1000,768]{1,0:T(8,128)(2,1)} %param.22) | copy-start | bytes 4608004
Sparse Core Ops, SparseCore 0:
  186.5 103.7 reduce-scatter.1
